TPU v7x, 32 devices: a whole 2x2x4 slice. The times are simulated.
32 devices in a mesh: grp: 2 (over core), ty: 4 (over y, x), tx: 4 (over z).
Axes of the slice: x: 2, y: 2, z: 4, core: 2. Of those that a mesh axis runs over, the one named last changes fastest.
Arguments:
- coupled_state: float32 [2, 23, 32, 8, 512], P('grp', None, None, 'ty', 'tx'), may hold values from -4 to 4, as said below
- land_mask: int32 [8, 512], P('ty', 'tx'), may hold values 0 or 1
- bottom_level: int32 [8, 512], P('ty', 'tx'), may hold values from 1 to 32
- shortwave: float32 [8, 512], P('ty', 'tx'), may hold values from 0.5 to 1.5
- absorb: float32 [19], replicated, may hold values from 0.01 to 0.1
- reaction: float32 [19, 19], replicated, may hold values from -1.25 to 1.25
Outputs:
- new_state: float32 [2, 23, 32, 8, 512], P('grp', None, None, 'ty', 'tx')
Inputs may be any that keep to these rules, and one draw needn't show every extreme that they name: `coupled_state`: fields 0 and 1 lie in -2 to 2, fields 2 and 3 in -4 to 4, the tracers in 0.1 to 2.
All inputs are finite; a program needn't handle non-finite values. No bound on the sum of `land_mask` on one device may be relied on, other than what follows from the above.
Results may differ from a plain program's by a relative error of at most 0.0003.
Values sent between devices are 32-bit elements; how exact they have to be, the bound alone decides.
No kernel may reach another device: no remote copies, remote signals or barrier semaphores. Data moves between devices by JAX's collectives and lax.ppermute only.
A program may use at most 192 MiB of HBM per device.

v0:
```python
import functools

import jax
import jax.numpy as jnp
from jax import lax
from jax.experimental import pallas as pl
from jax.experimental.pallas import tpu as pltpu
from jax.sharding import PartitionSpec as P

STEPS = 2
HALO = 2 * STEPS
LANES = 128
PAD = 8
DYN = 4

integration_interval = 0.1
tracer_interval = 0.08
coriolis = 0.8
barotropic_gradient_coefficient = 0.1
water_extinction = 0.04
layer_depth = 0.05
growth_peak = 2.0
half_light = 0.5
ratio_floor = 0.01

F32 = jnp.float32
BF16 = jnp.bfloat16
HIGHEST = lax.Precision.HIGHEST
VMEM = pl.BlockSpec(memory_space=pltpu.VMEM)
SMEM = pl.BlockSpec(memory_space=pltpu.SMEM)
ANY = pl.BlockSpec(memory_space=pl.ANY)


def dot(a, b):
    return jnp.dot(a, b, precision=HIGHEST, preferred_element_type=F32)


def iota(shape, dim):
    return lax.broadcasted_iota(jnp.int32, shape, dim)


class Plan:
    def __init__(self, mesh, nf, nz, rows, cols):
        self.n, self.m = mesh.shape["ty"], mesh.shape["tx"]
        self.nf, self.nz, self.rows, self.cols = nf, nz, rows, cols
        assert cols == LANES and LANES % nz == 0 and LANES // nz == DYN
        assert self.n & (self.n - 1) == 0 and self.n > 1
        self.per = LANES // nz
        self.groups = -(-(nf + 1) // self.per)
        self.tg = self.groups - 1
        self.chunk = cols // self.n
        self.width = self.chunk + 2 * HALO
        assert self.width % 8 == 0 and self.chunk % 8 == 0 and self.chunk >= HALO
        self.R = self.n * rows
        self.padded = self.width + 2 * PAD
        self.depth_lane = LANES - nz
        self.sw_lane = LANES - nz // 2

    def ty(self):
        return lax.axis_index("ty")

    def is_ocean(self):
        return lax.axis_index("grp") == 0

    def chunk_of(self, ty):
        odd = lax.rem(lax.axis_index("tx"), 2)
        return jnp.where(odd == 0, ty, self.n - 1 - ty)

    def xor(self, mask):
        ty, out, bit = self.ty(), 0, 1
        while bit < self.n:
            here = lax.rem(lax.div(ty, bit), 2)
            out = out + bit * ((1 - here) if mask & bit else here)
            bit *= 2
        return out


def pack_kernel(p, view, land, bottom, sw, absorb, *rest):
    outs_t, outs_o, t_ref = rest[: p.n], rest[p.n : 2 * p.n], rest[2 * p.n]
    nz, rows, step = p.nz, p.rows, p.per * p.nz
    half = nz // 2
    ocean = p.is_ocean()

    def aux(r, upper):
        depth = jnp.where(land[r : r + 1, :] == 1, bottom[r : r + 1, :], 0).astype(F32)
        return jnp.concatenate(
            [
                upper,
                jnp.broadcast_to(depth, (half, LANES)),
                jnp.broadcast_to(sw[r : r + 1, :], (half, LANES)),
            ],
            axis=0,
        )

    def field(r, g, count):
        return view[pl.ds(g * step * rows + r, count, stride=rows), :]

    def put(r, g, block):
        t_ref[g, r, HALO : HALO + LANES, :] = block.T

    def send(outs, count):
        for mask in range(p.n):
            start = pl.multiple_of(p.chunk_of(p.xor(mask)) * p.chunk, 8)
            for g in range(count):
                for r in range(rows):
                    outs[mask][g, r] = t_ref[g, r, pl.ds(start, p.width), :]

    zero = jnp.zeros((HALO, LANES), F32)
    for g in range(p.groups):
        for r in range(rows):
            t_ref[g, r, :HALO, :] = zero
            t_ref[g, r, HALO + LANES :, :] = zero

    @pl.when(jnp.logical_not(ocean))
    def _():
        for r in range(rows):
            for g in range(p.groups - 1):
                put(r, g, field(r, g, step))
            have = (p.nf - p.tg * p.per) * nz
            block = field(r, p.tg, have)
            if have < LANES - nz:
                block = jnp.concatenate([block, jnp.zeros((LANES - nz - have, LANES), F32)], axis=0)
            put(r, p.tg, aux(r, block))
        send(outs_t, p.groups)

    @pl.when(ocean)
    def _():
        lower = (iota((nz, nz), 0) >= iota((nz, nz), 1)).astype(F32)
        for r in range(rows):
            put(r, 0, field(r, 0, step))
            kd = jnp.full((nz, LANES), water_extinction, F32)
            for t in range(p.nf - DYN):
                kd = kd + absorb[t] * view[pl.ds((DYN + t) * nz * rows + r, nz, stride=rows), :]
            below = sw[r : r + 1, :] * jnp.exp(-layer_depth * dot(lower, kd))
            above = below * jnp.exp(layer_depth * kd)
            forcing = (above - below) / layer_depth
            put(r, 1, aux(r, jnp.concatenate([jnp.zeros((2 * nz, LANES), F32), forcing], axis=0)))
        send(outs_o, 2)


def edge_kernel(p, *refs):
    src_t, src_o, z_t, z_o = refs[: p.n], refs[p.n : 2 * p.n], refs[2 * p.n], refs[2 * p.n + 1]
    left = p.chunk_of(p.ty()) == 0
    ocean = p.is_ocean()

    def copy(src, dst, count, lo):
        for mask in range(p.n):
            base = p.xor(mask) * p.rows
            for g in range(count):
                for r in range(p.rows):
                    dst[g, base + r] = src[mask][g, r, lo : lo + HALO, :]

    for cond, src, dst, count in (
        (ocean, src_o, z_o, 2),
        (jnp.logical_not(ocean), src_t, z_t, p.groups),
    ):

        @pl.when(cond & left)
        def _():
            copy(src, dst, count, HALO)

        @pl.when(cond & jnp.logical_not(left))
        def _():
            copy(src, dst, count, p.chunk)


def assemble(p, src, z, g, dst):
    for mask in range(p.n):
        base = p.xor(mask) * p.rows
        for r in range(p.rows):
            dst[1 + base + r, PAD : PAD + p.width, :] = src[mask][g, r]
    chunk = p.chunk_of(p.ty())

    @pl.when(chunk == 0)
    def _():
        dst[1 : 1 + p.R, PAD : PAD + HALO, :] = z[g]

    @pl.when(chunk == p.n - 1)
    def _():
        dst[1 : 1 + p.R, PAD + p.width - HALO : PAD + p.width, :] = z[g]


def aux_fields(p, aux_ref, wet_ref, sw_ref):
    level = (iota((p.width, LANES), 1) % p.nz).astype(F32)
    for r in range(p.R):
        x = aux_ref[1 + r, PAD : PAD + p.width, :]
        wet_ref[r] = (level < x[:, p.depth_lane : p.depth_lane + 1]).astype(F32)
        sw_ref[r] = jnp.broadcast_to(x[:, p.sw_lane : p.sw_lane + 1], (p.width, LANES))


def lanes_of(p, shape, dim):
    i = iota(shape, dim)
    return i // p.nz, i % p.nz


def copy_matrix(p, slot):
    f0, k0 = lanes_of(p, (LANES, LANES), 0)
    _, k1 = lanes_of(p, (LANES, LANES), 1)
    return ((f0 == slot) & (k0 == k1)).astype(F32)


def cumsum_matrix(p):
    _, k0 = lanes_of(p, (LANES, LANES), 0)
    _, k1 = lanes_of(p, (LANES, LANES), 1)
    return (k0 <= k1).astype(F32)


def sum_matrix(p):
    _, k0 = lanes_of(p, (LANES, LANES), 0)
    _, k1 = lanes_of(p, (LANES, LANES), 1)
    return (k0 == k1).astype(F32)


def optical_depth(p, attenuation):
    _, level = lanes_of(p, attenuation.shape, 1)
    plain = (water_extinction * layer_depth) * (level + 1).astype(F32)
    return layer_depth * dot(attenuation, cumsum_matrix(p)) + plain


def ocean_step(p, d, forcing, wet, out, pp):
    f0, k0 = lanes_of(p, (LANES, LANES), 0)
    _, k1 = lanes_of(p, (LANES, LANES), 1)
    weight = jnp.where(f0 == 2, -0.2, jnp.where(f0 == 3, 0.8, 0.0)) * barotropic_gradient_coefficient
    press = jnp.where(k0 <= k1, weight, 0.0)
    mid = slice(PAD, PAD + p.width)
    for r in range(p.R):
        pp[1 + r, mid, :] = dot(d[1 + r, mid, :], press)
    f, _ = lanes_of(p, (p.width, LANES), 1)
    for r in range(p.R):
        x = d[1 + r, mid, :]
        lap = d[2 + r, mid, :] + d[r, mid, :] + d[1 + r, PAD + 1 : PAD + 1 + p.width, :]
        lap = lap + d[1 + r, PAD - 1 : PAD - 1 + p.width, :] - 4.0 * x
        grad_e = 0.5 * (pp[2 + r, mid, :] - pp[r, mid, :])
        grad_n = 0.5 * (
            pp[1 + r, PAD + 1 : PAD + 1 + p.width, :] - pp[1 + r, PAD - 1 : PAD - 1 + p.width, :]
        )
        of_u = coriolis * pltpu.roll(x, LANES - p.nz, 1) - grad_e
        of_v = -coriolis * pltpu.roll(x, p.nz, 1) - grad_n
        other = jnp.where(f == 2, forcing(r), 0.0)
        extra = jnp.where(f == 0, of_u, jnp.where(f == 1, of_v, other))
        out[r] = wet[r] * (x + integration_interval * (lap + extra))


def clear_pads(p, *refs):
    side = jnp.zeros((PAD, LANES), F32)
    for ref in refs:
        count = ref.shape[0]
        for r in range(count):
            ref[r, :PAD, :] = side
            ref[r, PAD + p.width :, :] = side
        row = jnp.zeros((p.padded, LANES), F32)
        ref[0] = row
        ref[count - 1] = row


def tracer_step(p, d, load_group, wet, sw, absorb, r_hi, r_lo, store, scratch):
    c, feh, fnh, va, ae, le, an, ln, low, rin, rout, adv = scratch
    R, W = p.R, p.width
    mid = slice(PAD, PAD + W)
    up = slice(PAD + 1, PAD + 1 + W)
    down = slice(PAD - 1, PAD - 1 + W)
    clear_pads(p, c, va, ae, le, an, ln, rin, rout)

    flat = jnp.concatenate([d[1 + r, mid, :] for r in range(R)], axis=0)
    ua = dot(flat, copy_matrix(p, 0))
    vv = dot(flat, copy_matrix(p, 1))
    for r in range(R):
        va[1 + r, mid, :] = vv[r * W : (r + 1) * W]
    first = lax.axis_index("tx") * p.cols + p.chunk_of(p.ty()) * p.chunk - HALO
    col = first + iota((W, LANES), 0)
    inside = ((col >= 0) & (col + 1 < p.m * p.cols)).astype(F32)
    half = 0.25 * tracer_interval
    for r in range(R):
        if r + 1 < R:
            feh[r] = half * (ua[r * W : (r + 1) * W] + ua[(r + 1) * W : (r + 2) * W])
        else:
            feh[r] = jnp.zeros((W, LANES), F32)
        fnh[r] = half * (va[1 + r, mid, :] + va[1 + r, up, :]) * inside

    def group(g, _):
        load_group(g, c)
        for r in range(R):
            c0 = c[1 + r, mid, :]
            cn = c[1 + r, up, :]
            ce = c[2 + r, mid, :]
            f = feh[r]
            a = jnp.abs(f) * (ce - c0)
            ae[1 + r, mid, :] = a
            le[1 + r, mid, :] = f * (ce + c0) - a
            f = fnh[r]
            a = jnp.abs(f) * (cn - c0)
            an[1 + r, mid, :] = a
            ln[1 + r, mid, :] = f * (cn + c0) - a
        for r in range(R):
            c0 = c[1 + r, mid, :]
            cn = c[1 + r, up, :]
            cs = c[1 + r, down, :]
            ce = c[2 + r, mid, :]
            cw = c[r, mid, :]
            lw = c0 - (le[1 + r, mid, :] - le[r, mid, :] + ln[1 + r, mid, :] - ln[1 + r, down, :])
            low[r] = lw
            hi = jnp.maximum(jnp.maximum(jnp.maximum(c0, ce), jnp.maximum(cw, cn)), cs)
            lo = jnp.minimum(jnp.minimum(jnp.minimum(c0, ce), jnp.minimum(cw, cn)), cs)
            e, w = ae[1 + r, mid, :], ae[r, mid, :]
            nn, s = an[1 + r, mid, :], an[1 + r, down, :]
            ep, wp, np_, sp = (jnp.maximum(x, 0.0) for x in (e, w, nn, s))
            em, wm, nm, sm = (jnp.minimum(x, 0.0) for x in (e, w, nn, s))
            gain_in = wp - em + sp - nm
            gain_out = ep - wm + np_ - sm
            floor = ratio_floor * tracer_interval
            rin[1 + r, mid, :] = jnp.minimum(gain_in, jnp.maximum(hi - lw, 0.0)) / jnp.maximum(
                gain_in, floor
            )
            rout[1 + r, mid, :] = jnp.minimum(gain_out, jnp.maximum(lw - lo, 0.0)) / jnp.maximum(
                gain_out, floor
            )
        before = jnp.zeros((W, LANES), F32)
        for r in range(R):
            ri, ro = rin[1 + r, mid, :], rout[1 + r, mid, :]
            a = ae[1 + r, mid, :]
            east = a * jnp.where(
                a >= 0.0,
                jnp.minimum(rin[2 + r, mid, :], ro),
                jnp.minimum(ri, rout[2 + r, mid, :]),
            )
            a = an[1 + r, mid, :]
            north = a * jnp.where(
                a >= 0.0,
                jnp.minimum(rin[1 + r, up, :], ro),
                jnp.minimum(ri, rout[1 + r, up, :]),
            )
            ln[1 + r, mid, :] = north
            adv[g, r] = low[r] - (east - before + north - ln[1 + r, down, :])
            before = east
        return 0

    lax.fori_loop(0, p.tg, group, 0)

    whole = [adv[g].reshape(R * W, LANES) for g in range(p.tg)]
    att = whole[0] * absorb[0:1, :]
    for g in range(1, p.tg):
        att = att + whole[g] * absorb[g : g + 1, :]
    light = sw[...].reshape(R * W, LANES) * jnp.exp(-optical_depth(p, att))
    warm = jnp.exp(0.063 * flat) * pltpu.roll(1.0 + 0.2 * jnp.tanh(flat), LANES - p.nz, 1)
    growth = (
        (growth_peak * tracer_interval) * dot(warm, copy_matrix(p, 2)) * light / (light + half_light)
    )
    every = jnp.concatenate(whole, axis=1)
    hi = every.astype(BF16)
    lo = (every - hi.astype(F32)).astype(BF16)

    def mm(a, b):
        return jnp.dot(a, b, preferred_element_type=F32)

    mixed = mm(hi, r_hi[...]) + mm(lo, r_hi[...]) + mm(hi, r_lo[...])
    wets = wet[...].reshape(R * W, LANES)
    for g in range(p.tg):
        new = wets * (whole[g] + growth * mixed[:, g * LANES : (g + 1) * LANES])
        store(g, new.reshape(R, W, LANES))


def ocean_first_kernel(p, *refs):
    src, z, dyn, wet, sw, d, aux, pp = (refs[: p.n],) + refs[p.n :]

    @pl.when(p.is_ocean())
    def _():
        clear_pads(p, d, aux, pp)
        assemble(p, src, z, 0, d)
        assemble(p, src, z, 1, aux)
        aux_fields(p, aux, wet, sw)
        ocean_step(p, d, lambda r: aux[1 + r, PAD : PAD + p.width, :], wet, dyn, pp)


def tracer_first_kernel(p, *refs):
    src, (z, absorb, r_hi, r_lo, c1, wet, sw, d), scratch = refs[: p.n], refs[p.n : p.n + 8], refs[p.n + 8 :]

    @pl.when(jnp.logical_not(p.is_ocean()))
    def _():
        c = scratch[0]
        clear_pads(p, d)
        assemble(p, src, z, p.groups - 1, c)
        aux_fields(p, c, wet, sw)
        assemble(p, src, z, 0, d)

        def load(g, dst):
            assemble(p, src, z, g + 1, dst)

        def store(g, value):
            c1[g] = value

        tracer_step(p, d, load, wet, sw, absorb, r_hi, r_lo, store, scratch)


def load_dyn(p, dyn, d):
    clear_pads(p, d)
    for r in range(p.R):
        d[1 + r, PAD : PAD + p.width, :] = dyn[r]


def put_back(p, outs, group, value):
    for mask in range(p.n):
        outs[mask][group] = value(p.xor(mask) * p.rows)


def tracer_second_kernel(p, *refs):
    dyn, c1, wet, sw, absorb, r_hi, r_lo = refs[:7]
    outs, (d, c2), scratch = refs[7 : 7 + p.n], refs[7 + p.n : 9 + p.n], refs[9 + p.n :]
    core = slice(HALO, HALO + p.chunk)

    @pl.when(jnp.logical_not(p.is_ocean()))
    def _():
        load_dyn(p, dyn, d)

        def load(g, dst):
            for r in range(p.R):
                dst[1 + r, PAD : PAD + p.width, :] = c1[g, r]

        def store(g, value):
            c2[...] = value
            put_back(p, outs, g + 1, lambda row: c2[pl.ds(row, p.rows), core, :])

        tracer_step(p, d, load, wet, sw, absorb, r_hi, r_lo, store, scratch)
        put_back(p, outs, 0, lambda row: dyn[pl.ds(row, p.rows), core, :])


def ocean_second_kernel(p, *refs):
    dyn, c1, wet, sw, absorb = refs[:5]
    same, outs, (d, pp, heat, dyn2) = refs[5 : 5 + p.n], refs[5 + p.n : 5 + 2 * p.n], refs[5 + 2 * p.n :]
    core = slice(HALO, HALO + p.chunk)

    @pl.when(jnp.logical_not(p.is_ocean()))
    def _():
        for mask in range(p.n):
            outs[mask][...] = same[mask][...]

    @pl.when(p.is_ocean())
    def _():
        load_dyn(p, dyn, d)
        clear_pads(p, pp)
        flat = (p.R * p.width, LANES)
        att = c1[0].reshape(flat) * absorb[0:1, :]
        for g in range(1, p.tg):
            att = att + c1[g].reshape(flat) * absorb[g : g + 1, :]
        below = sw[...].reshape(flat) * jnp.exp(-optical_depth(p, att))
        kd = dot(att, sum_matrix(p)) + water_extinction
        above = below * jnp.exp(layer_depth * kd)
        heat[...] = ((above - below) / layer_depth).reshape(heat.shape)
        ocean_step(p, d, lambda r: heat[r], wet, dyn2, pp)
        put_back(p, outs, 0, lambda row: dyn2[pl.ds(row, p.rows), core, :])
        for g in range(p.tg):
            put_back(p, outs, g + 1, lambda row: c1[g, pl.ds(row, p.rows), core, :])


def unpack_kernel(p, *refs):
    src, out, t_ref = refs[: p.n], refs[p.n], refs[p.n + 1]
    step = p.per * p.nz
    for g in range(p.groups):
        count = min(step, (p.nf - g * p.per) * p.nz)
        for r in range(p.rows):
            for mask in range(p.n):
                start = pl.multiple_of(p.chunk_of(p.xor(mask)) * p.chunk, 8)
                t_ref[pl.ds(start, p.chunk), :] = src[mask][g, r]
            out[pl.ds(g * step * p.rows + r, count, stride=p.rows), :] = t_ref[...].T[:count]


def mix_kernel(p, reaction, r_hi, r_lo):
    size = p.tg * LANES
    spread = (iota((size, LANES), 0) // p.nz == iota((size, LANES), 1)).astype(F32)
    rows = lax.dot_general(
        spread, reaction[...], (((1,), (1,)), ((), ())), precision=HIGHEST, preferred_element_type=F32
    )
    full = lax.dot_general(
        rows, spread, (((1,), (1,)), ((), ())), precision=HIGHEST, preferred_element_type=F32
    )
    same = iota((size, size), 0) % p.nz == iota((size, size), 1) % p.nz
    full = jnp.where(same, full, 0.0)
    hi = full.astype(BF16)
    r_hi[...] = hi
    r_lo[...] = (full - hi.astype(F32)).astype(BF16)


def solution(mesh):
    def local(coupled_state, land_mask, bottom_level, shortwave, absorb, reaction):
        view = coupled_state[0]
        p = Plan(mesh, *view.shape)
        n, G, R, W = p.n, p.groups, p.R, p.width

        def sds(*shape, dtype=F32):
            return jax.ShapeDtypeStruct(shape, dtype)

        def call(kernel, name, outs, ins, scratch=(), in_specs=None, aliases=None):
            return pl.pallas_call(
                functools.partial(kernel, p),
                name=name,
                out_shape=outs,
                in_specs=in_specs or [VMEM] * len(ins),
                out_specs=jax.tree.map(lambda _: VMEM, outs),
                scratch_shapes=[pltpu.VMEM(s, F32) for s in scratch],
                input_output_aliases=aliases or {},
                compiler_params=pltpu.CompilerParams(vmem_limit_bytes=56 * 2**20),
            )(*ins)

        def swap(value, mask, grp):
            pairs = [(grp * n + i, grp * n + (i ^ mask)) for i in range(n)]
            return lax.ppermute(value, ("grp", "ty"), pairs)

        def edges(value, grp):
            pairs = []
            size = lax.axis_size("tx")
            for tx in range(size - 1):
                end = n - 1 if tx % 2 == 0 else 0
                a = (grp * n + end) * size + tx
                pairs += [(a, a + 1), (a + 1, a)]
            return lax.ppermute(value, ("grp", "ty", "tx"), pairs)

        flat = view.reshape(p.nf * p.nz * p.rows, p.cols)
        packed = call(
            pack_kernel,
            "pack",
            [sds(G, p.rows, W, LANES)] * n + [sds(2, p.rows, W, LANES)] * n,
            [flat, land_mask, bottom_level, shortwave, absorb],
            [(G, p.rows, LANES + 2 * HALO, LANES)],
            [VMEM] * 4 + [SMEM],
        )
        got_t = [packed[0]] + [swap(packed[k], k, 1) for k in range(1, n)]
        got_o = [packed[n]] + [swap(packed[n + k], k, 0) for k in range(1, n)]

        react = jnp.pad(reaction, ((0, LANES - reaction.shape[0]), (0, LANES - reaction.shape[1])))
        size = p.tg * LANES
        r_hi, r_lo = call(
            mix_kernel, "mix", [sds(size, size, dtype=BF16), sds(size, size, dtype=BF16)], [react]
        )
        weights = jnp.pad(absorb, (0, p.tg * p.per - absorb.shape[0])).reshape(p.tg, p.per)
        weights = jnp.repeat(weights, p.nz, axis=1)

        z_t, z_o = call(
            edge_kernel, "edge", [sds(G, R, HALO, LANES), sds(2, R, HALO, LANES)], got_t + got_o
        )
        z_t, z_o = edges(z_t, 1), edges(z_o, 0)

        padded = (R + 2, p.padded, LANES)
        block = (R, W, LANES)
        scratch = [padded, block, block] + [padded] * 5 + [block] + [padded] * 2 + [(p.tg,) + block]
        dyn1, wet_o, sw_o = call(
            ocean_first_kernel, "ocean_first", [sds(*block)] * 3, got_o + [z_o], [padded] * 3
        )

        def across(value, source):
            other = [
                ((source * n + i) , ((1 - source) * n + i)) for i in range(n)
            ]
            return lax.ppermute(value, ("grp", "ty"), other)

        dyn1_t = across(dyn1, 0)
        c1, wet_t, sw_t = call(
            tracer_first_kernel,
            "tracer_first",
            [sds(p.tg, *block), sds(*block), sds(*block)],
            got_t + [z_t, weights, r_hi, r_lo],
            [padded] + scratch,
        )
        c1_o = across(c1, 1)
        back = [sds(G, p.rows, p.chunk, LANES)] * n
        outs = call(
            tracer_second_kernel,
            "tracer_second",
            back,
            [dyn1_t, c1, wet_t, sw_t, weights, r_hi, r_lo],
            [padded, block] + scratch,
        )
        outs = call(
            ocean_second_kernel,
            "ocean_second",
            back,
            [dyn1, c1_o, wet_o, sw_o, weights] + list(outs),
            [padded, padded, block, block],
            aliases={5 + k: k for k in range(n)},
        )
        home = [outs[0]] + [
            lax.ppermute(outs[k], "ty", [(i, i ^ k) for i in range(n)]) for k in range(1, n)
        ]
        out = call(
            unpack_kernel, "unpack", [sds(p.nf * p.nz * p.rows, p.cols)], home, [(LANES, LANES)]
        )[0]
        return out.reshape((1,) + view.shape)

    in_specs = (
        P("grp", None, None, "ty", "tx"),
        P("ty", "tx"),
        P("ty", "tx"),
        P("ty", "tx"),
        P(),
        P(),
    )
    out_specs = P("grp", None, None, "ty", "tx")
    return jax.shard_map(local, mesh=mesh, in_specs=in_specs, out_specs=out_specs, check_vma=False)
```

profile of v0, /device:TPU:1, one launch (start us, length us, event | category | flops | bytes accessed | tf_op | source)
XLA Modules:
  0.0 69.6 jit_solution(604710071670340937)
XLA Ops:
  0.0 2.5 %pack.1 = (f32[6,2,40,128]{3,2,1,0:T(8,128)}, f32[6,2,40,128]{3,2,1,0:T(8,128)}, f32[6,2,40,128]{3,2,1,0:T(8,128)}, f32[6,2,40,128]{3,2,1,0:T(8,128)}, f32[2,2,4...) custom-call(f32[1472,128]{1,0:T(8,128)} %bitcast.2, ...), custom_call_target="tpu_custom_call" | custom-call | tf_op jit(solution)/shard_map/pack/pallas_call | solution.py:492
  2.5 3.9 %collective-permute-start.3 = (f32[6,2,40,128]{3,2,1,0:T(8,128)}, f32[6,2,40,128]{3,2,1,0:T(8,128)S(1)}, u32[]{:S(2)}, u32[]{:S(2)}) collective-permute-start(f32[6,2,40,128]{3,2,1,0:T(8,128)} %get-tuple-element.36), channel_id=1, source_target_pairs={{16,20},{20,16},{24,28},{28,24},{17,21},{21,17},{25,29},{29,25},{1... | collective-permute-start | bytes 737288 | tf_op jit(solution)/shard_map/ppermute | solution.py:505
  6.5 3.1 %collective-permute-start.4 = (f32[6,2,40,128]{3,2,1,0:T(8,128)}, f32[6,2,40,128]{3,2,1,0:T(8,128)S(1)}, u32[]{:S(2)}, u32[]{:S(2)}) collective-permute-start(f32[6,2,40,128]{3,2,1,0:T(8,128)} %get-tuple-element.37), channel_id=1, source_target_pairs={{16,24},{20,28},{24,16},{28,20},{17,25},{21,29},{25,17},{29,21},{1... | collective-permute-start | bytes 737288 | tf_op jit(solution)/shard_map/ppermute | solution.py:505
  9.6 1.9 %collective-permute-start.5 = (f32[6,2,40,128]{3,2,1,0:T(8,128)}, f32[6,2,40,128]{3,2,1,0:T(8,128)S(1)}, u32[]{:S(2)}, u32[]{:S(2)}) collective-permute-start(f32[6,2,40,128]{3,2,1,0:T(8,128)} %get-tuple-element.38), channel_id=1, source_target_pairs={{16,28},{20,24},{24,20},{28,16},{17,29},{21,25},{25,21},{29,17},{1... | collective-permute-start | bytes 737288 | tf_op jit(solution)/shard_map/ppermute | solution.py:505
  11.6 0.7 collective-permute-start
  12.2 0.7 collective-permute-start.1
  12.9 0.0 collective-permute-done.refs_5_.refs_1_
  12.9 0.7 collective-permute-start.2
  13.6 0.0 collective-permute-done.1.refs_6_.refs_2_
  13.6 0.0 copy-start.5
  13.6 0.0 collective-permute-done.2.refs_7_.refs_3_
  13.6 0.0 collective-permute-done.3.refs_1_
  13.7 0.0 collective-permute-done.4.refs_2_
  13.7 0.0 copy-start.1
  13.7 4.1 %collective-permute-done.5.refs_3_ = f32[6,2,40,128]{3,2,1,0:T(8,128)S(1)} collective-permute-done((f32[6,2,40,128]{3,2,1,0:T(8,128)}, f32[6,2,40,128]{3,2,1,0:T(8,128)S(1)}, u32[]{:S(2)}, u32[]{:S(2)}) %collective-permute-start.5) | collective-permute-done | bytes 245792 | tf_op jit(solution)/shard_map/ppermute | solution.py:505
  17.8 0.7 copy-done.2
  18.5 2.1 %edge.1 = (f32[6,8,4,128]{3,2,1,0:T(4,128)}, f32[2,8,4,128]{3,2,1,0:T(4,128)}) custom-call(f32[6,2,40,128]{3,2,1,0:T(8,128)} %get-tuple-element.35.refs_0_, f32[6,2,40,128]{3,2,1,0:T(8,128)} %copy-done, f32[6,2,40,128]{3,2,1,0:T(8,128)} %copy-done.1, f32[6,2,40,128]{3,2,1,0:T(8,128)} %copy-done.2, f32[2,2,40,128]{3,2,1,0:T(8,128)} %get-tuple-element.31.refs_4_.refs_0_, ...), custom_call_target="tpu_custom_call" | custom-call | tf_op jit(solution)/shard_map/edge/pallas_call | solution.py:492
  20.6 0.8 %collective-permute-start.7 = (f32[6,8,4,128]{3,2,1,0:T(4,128)}, f32[6,8,4,128]{3,2,1,0:T(4,128)S(1)}, u32[]{:S(2)}, u32[]{:S(2)}) collective-permute-start(f32[6,8,4,128]{3,2,1,0:T(4,128)} %get-tuple-element.41), channel_id=1, source_target_pairs={{28,29},{29,28},{17,18},{18,17},{30,31},{31,30}} | collective-permute-start | bytes 294920 | tf_op jit(solution)/shard_map/ppermute | solution.py:514
  21.4 0.6 pad.9.reaction
  22.0 4.4 %mix.1 = (bf16[640,640]{1,0:T(8,128)(2,1)}, bf16[640,640]{1,0:T(8,128)(2,1)}) custom-call(f32[128,128]{1,0:T(8,128)} %pad.9.reaction), custom_call_target="tpu_custom_call" | custom-call | tf_op jit(solution)/shard_map/mix/pallas_call | solution.py:492
  26.4 0.1 reshape.9
  26.5 0.1 broadcast_in_dim.3
  26.5 0.7 reshape.10.refs_5_.refs_4_
  27.2 0.0 collective-permute-done.7.refs_4_
  27.2 0.6 copy-done.11
  27.9 7.1 %tracer_first.1 = (f32[5,8,40,128]{3,2,1,0:T(8,128)}, f32[8,40,128]{2,1,0:T(8,128)}, f32[8,40,128]{2,1,0:T(8,128)}) custom-call(f32[6,2,40,128]{3,2,1,0:T(8,128)} %get-tuple-element.35.refs_0_, f32[6,2,40,128]{3,2,1,0:T(8,128)} %copy-done, f32[6,2,40,128]{3,2,1,0:T(8,128)} %copy-done.1, f32[6,2,40,128]{3,2,1,0:T(8,128)} %copy-done.2, ...), custom_call_target="tpu_custom_call" | custom-call | tf_op jit(solution)/shard_map/tracer_first/pallas_call | solution.py:492
  34.9 1.3 %collective-permute-start.8 = (f32[5,8,40,128]{3,2,1,0:T(8,128)}, f32[5,8,40,128]{3,2,1,0:T(8,128)S(1)}, u32[]{:S(2)}, u32[]{:S(2)}) collective-permute-start(f32[5,8,40,128]{3,2,1,0:T(8,128)} %get-tuple-element.44.refs_1_), channel_id=1, source_target_pairs={{16,0},{20,4},{24,8},{28,12},{17,1},{21,5},{25,9},{29,13},{18,2},{... | collective-permute-start | bytes 2457608 | tf_op jit(solution)/shard_map/ppermute | solution.py:552
  36.3 0.7 collective-permute-start.6
  36.9 0.0 collective-permute-done.6.refs_4_
  36.9 0.0 copy-start.12
  36.9 0.6 copy-done.12
  37.6 1.8 %ocean_first.1 = (f32[8,40,128]{2,1,0:T(8,128)}, f32[8,40,128]{2,1,0:T(8,128)}, f32[8,40,128]{2,1,0:T(8,128)}) custom-call(f32[2,2,40,128]{3,2,1,0:T(8,128)} %get-tuple-element.31.refs_4_.refs_0_, f32[2,2,40,128]{3,2,1,0:T(8,128)} %copy-done.4, f32[2,2,40,128]{3,2,1,0:T(8,128)} %copy-done.5, f32[2,2,40,128]{3,2,1,0:T(8,128)} %copy-done.6, ...), custom_call_target="tpu_custom_call" | custom-call | tf_op jit(solution)/shard_map/ocean_first/pallas_call | solution.py:492
  39.4 1.3 %collective-permute-start.9 = (f32[8,40,128]{2,1,0:T(8,128)}, f32[8,40,128]{2,1,0:T(8,128)S(1)}, u32[]{:S(2)}, u32[]{:S(2)}) collective-permute-start(f32[8,40,128]{2,1,0:T(8,128)} %get-tuple-element.40.refs_0_), channel_id=1, source_target_pairs={{0,16},{4,20},{8,24},{12,28},{1,17},{5,21},{9,25},{13,29},{2,18},{... | collective-permute-start | bytes 491528 | tf_op jit(solution)/shard_map/ppermute | solution.py:552
  40.6 2.2 %collective-permute-done.9.refs_0_ = f32[8,40,128]{2,1,0:T(8,128)S(1)} collective-permute-done((f32[8,40,128]{2,1,0:T(8,128)}, f32[8,40,128]{2,1,0:T(8,128)S(1)}, u32[]{:S(2)}, u32[]{:S(2)}) %collective-permute-start.9) | collective-permute-done | bytes 163872 | tf_op jit(solution)/shard_map/ppermute | solution.py:552
  42.8 0.7 copy-done.10
  43.5 6.7 %tracer_second.1 = (f32[6,2,32,128]{3,2,1,0:T(8,128)}, f32[6,2,32,128]{3,2,1,0:T(8,128)}, f32[6,2,32,128]{3,2,1,0:T(8,128)}, f32[6,2,32,128]{3,2,1,0:T(8,128)}) custom-call(f32[8,40,128]{2,1,0:T(8,128)} %copy-done.10, f32[5,8,40,128]{3,2,1,0:T(8,128)} %get-tuple-element.44.refs_1_, f32[8,40,128]{2,1,0:T(8,128)} %get-tuple-element.47.refs_2_, ...), custom_call_target="tpu_custom_call" | custom-call | tf_op jit(solution)/shard_map/tracer_second/pallas_call | solution.py:492
  50.2 0.0 collective-permute-done.8.refs_1_
  50.2 0.9 %copy-done.3 = f32[5,8,40,128]{3,2,1,0:T(8,128)} copy-done((f32[5,8,40,128]{3,2,1,0:T(8,128)}, f32[5,8,40,128]{3,2,1,0:T(8,128)S(1)}, u32[]{:S(2)}) %copy-start.3) | copy-done | bytes 819224
  51.1 2.4 %ocean_second.1 = (f32[6,2,32,128]{3,2,1,0:T(8,128)}, f32[6,2,32,128]{3,2,1,0:T(8,128)}, f32[6,2,32,128]{3,2,1,0:T(8,128)}, f32[6,2,32,128]{3,2,1,0:T(8,128)}) custom-call(f32[8,40,128]{2,1,0:T(8,128)} %get-tuple-element.40.refs_0_, f32[5,8,40,128]{3,2,1,0:T(8,128)} %copy-done.3, ...), custom_call_target="tpu_custom_call", output_to_operand_aliasing={{0}: (5, {}), {1}: (6, {}), {2}: (7, {}), {3}: (8, {})} | custom-call | tf_op jit(solution)/shard_map/ocean_second/pallas_call | solution.py:492
  53.6 0.2 collective-permute-start.10
  53.7 5.2 %collective-permute-start.11 = (f32[6,2,32,128]{3,2,1,0:T(8,128)}, f32[6,2,32,128]{3,2,1,0:T(8,128)S(1)}, u32[]{:S(2)}, u32[]{:S(2)}) collective-permute-start(f32[6,2,32,128]{3,2,1,0:T(8,128)} %get-tuple-element.55), channel_id=1, source_target_pairs={{0,8},{4,12},{8,0},{12,4},{1,9},{5,13},{9,1},{13,5},{2,10},{6,14},... | collective-permute-start | bytes 589832 | tf_op jit(solution)/shard_map/ppermute | solution.py:580
  59.0 0.0 collective-permute-start.12
  59.0 0.0 collective-permute-done.10.refs_1_
  59.0 7.5 %collective-permute-done.11.refs_2_ = f32[6,2,32,128]{3,2,1,0:T(8,128)S(1)} collective-permute-done((f32[6,2,32,128]{3,2,1,0:T(8,128)}, f32[6,2,32,128]{3,2,1,0:T(8,128)S(1)}, u32[]{:S(2)}, u32[]{:S(2)}) %collective-permute-start.11) | collective-permute-done | bytes 196640 | tf_op jit(solution)/shard_map/ppermute | solution.py:580
  66.4 0.0 collective-permute-done.12.refs_3_
  66.4 0.7 copy-done.8
  67.1 0.1 copy-done.9
  67.2 2.4 %unpack.1 = f32[1472,128]{1,0:T(8,128)} custom-call(f32[6,2,32,128]{3,2,1,0:T(8,128)} %get-tuple-element.53.refs_0_, f32[6,2,32,128]{3,2,1,0:T(8,128)} %copy-done.7, f32[6,2,32,128]{3,2,1,0:T(8,128)} %copy-done.8, f32[6,2,32,128]{3,2,1,0:T(8,128)} %copy-done.9), custom_call_target="tpu_custom_call" | custom-call | tf_op jit(solution)/shard_map/unpack/pallas_call | solution.py:492
  (23 shorter events, 0.0 us)
Async XLA Ops:
  2.5 11.1 %collective-permute-start.3 = (f32[6,2,40,128]{3,2,1,0:T(8,128)}, f32[6,2,40,128]{3,2,1,0:T(8,128)S(1)}, u32[]{:S(2)}, u32[]{:S(2)}) collective-permute-start(f32[6,2,40,128]{3,2,1,0:T(8,128)} %get-tuple-element.36), channel_id=1, source_target_pairs={{16,20},{20,16},{24,28},{28,24},{17,21},{21,17},{25,29},{29,25},{1... | collective-permute-start | bytes 737288 | tf_op jit(solution)/shard_map/ppermute | solution.py:505
  6.5 7.2 %collective-permute-start.4 = (f32[6,2,40,128]{3,2,1,0:T(8,128)}, f32[6,2,40,128]{3,2,1,0:T(8,128)S(1)}, u32[]{:S(2)}, u32[]{:S(2)}) collective-permute-start(f32[6,2,40,128]{3,2,1,0:T(8,128)} %get-tuple-element.37), channel_id=1, source_target_pairs={{16,24},{20,28},{24,16},{28,20},{17,25},{21,29},{25,17},{29,21},{1... | collective-permute-start | bytes 737288 | tf_op jit(solution)/shard_map/ppermute | solution.py:505
  9.6 8.2 %collective-permute-start.5 = (f32[6,2,40,128]{3,2,1,0:T(8,128)}, f32[6,2,40,128]{3,2,1,0:T(8,128)S(1)}, u32[]{:S(2)}, u32[]{:S(2)}) collective-permute-start(f32[6,2,40,128]{3,2,1,0:T(8,128)} %get-tuple-element.38), channel_id=1, source_target_pairs={{16,28},{20,24},{24,20},{28,16},{17,29},{21,25},{25,21},{29,17},{1... | collective-permute-start | bytes 737288 | tf_op jit(solution)/shard_map/ppermute | solution.py:505
  11.6 1.4 %collective-permute-start = (f32[2,2,40,128]{3,2,1,0:T(8,128)}, f32[2,2,40,128]{3,2,1,0:T(8,128)S(1)}, u32[]{:S(2)}, u32[]{:S(2)}) collective-permute-start(f32[2,2,40,128]{3,2,1,0:T(8,128)} %get-tuple-element.32), channel_id=1, source_target_pairs={{0,4},{4,0},{8,12},{12,8},{1,5},{5,1},{9,13},{13,9},{2,6},{6,2},{1... | collective-permute-start | bytes 245768 | tf_op jit(solution)/shard_map/ppermute | solution.py:505
  12.2 1.4 %collective-permute-start.1 = (f32[2,2,40,128]{3,2,1,0:T(8,128)}, f32[2,2,40,128]{3,2,1,0:T(8,128)S(1)}, u32[]{:S(2)}, u32[]{:S(2)}) collective-permute-start(f32[2,2,40,128]{3,2,1,0:T(8,128)} %get-tuple-element.33), channel_id=1, source_target_pairs={{0,8},{4,12},{8,0},{12,4},{1,9},{5,13},{9,1},{13,5},{2,10},{6,14},... | collective-permute-start | bytes 245768 | tf_op jit(solution)/shard_map/ppermute | solution.py:505
  12.9 4.9 %copy-start.4 = (f32[2,2,40,128]{3,2,1,0:T(8,128)}, f32[2,2,40,128]{3,2,1,0:T(8,128)S(1)}, u32[]{:S(2)}) copy-start(f32[2,2,40,128]{3,2,1,0:T(8,128)S(1)} %collective-permute-done.refs_5_.refs_1_) | copy-start | bytes 245764
  12.9 0.7 %collective-permute-start.2 = (f32[2,2,40,128]{3,2,1,0:T(8,128)}, f32[2,2,40,128]{3,2,1,0:T(8,128)S(1)}, u32[]{:S(2)}, u32[]{:S(2)}) collective-permute-start(f32[2,2,40,128]{3,2,1,0:T(8,128)} %get-tuple-element.34), channel_id=1, source_target_pairs={{0,12},{4,8},{8,4},{12,0},{1,13},{5,9},{9,5},{13,1},{2,14},{6,10},... | collective-permute-start | bytes 245768 | tf_op jit(solution)/shard_map/ppermute | solution.py:505
  13.6 4.2 %copy-start.5 = (f32[2,2,40,128]{3,2,1,0:T(8,128)}, f32[2,2,40,128]{3,2,1,0:T(8,128)S(1)}, u32[]{:S(2)}) copy-start(f32[2,2,40,128]{3,2,1,0:T(8,128)S(1)} %collective-permute-done.1.refs_6_.refs_2_) | copy-start | bytes 245764
  13.6 4.2 %copy-start.6 = (f32[2,2,40,128]{3,2,1,0:T(8,128)}, f32[2,2,40,128]{3,2,1,0:T(8,128)S(1)}, u32[]{:S(2)}) copy-start(f32[2,2,40,128]{3,2,1,0:T(8,128)S(1)} %collective-permute-done.2.refs_7_.refs_3_) | copy-start | bytes 245764
  13.6 4.1 %copy-start = (f32[6,2,40,128]{3,2,1,0:T(8,128)}, f32[6,2,40,128]{3,2,1,0:T(8,128)S(1)}, u32[]{:S(2)}) copy-start(f32[6,2,40,128]{3,2,1,0:T(8,128)S(1)} %collective-permute-done.3.refs_1_) | copy-start | bytes 737284
  13.7 4.1 %copy-start.1 = (f32[6,2,40,128]{3,2,1,0:T(8,128)}, f32[6,2,40,128]{3,2,1,0:T(8,128)S(1)}, u32[]{:S(2)}) copy-start(f32[6,2,40,128]{3,2,1,0:T(8,128)S(1)} %collective-permute-done.4.refs_2_) | copy-start | bytes 737284
  17.8 0.7 %copy-start.2 = (f32[6,2,40,128]{3,2,1,0:T(8,128)}, f32[6,2,40,128]{3,2,1,0:T(8,128)S(1)}, u32[]{:S(2)}) copy-start(f32[6,2,40,128]{3,2,1,0:T(8,128)S(1)} %collective-permute-done.5.refs_3_) | copy-start | bytes 737284
  18.5 2.9 %copy-start.13 = (f32[19,19]{1,0:T(8,128)S(1)}, f32[19,19]{1,0:T(8,128)}, u32[]{:S(2)}) copy-start(f32[19,19]{1,0:T(8,128)} %param.11) | copy-start | bytes 4336
  20.6 0.8 %copy-start.14 = (f32[19]{0:T(128)S(1)}, f32[19]{0:T(128)}, u32[]{:S(2)}) copy-start(f32[19]{0:T(128)} %absorb.1) | copy-start | bytes 232
  20.6 6.6 %collective-permute-start.7 = (f32[6,8,4,128]{3,2,1,0:T(4,128)}, f32[6,8,4,128]{3,2,1,0:T(4,128)S(1)}, u32[]{:S(2)}, u32[]{:S(2)}) collective-permute-start(f32[6,8,4,128]{3,2,1,0:T(4,128)} %get-tuple-element.41), channel_id=1, source_target_pairs={{28,29},{29,28},{17,18},{18,17},{30,31},{31,30}} | collective-permute-start | bytes 294920 | tf_op jit(solution)/shard_map/ppermute | solution.py:514
  27.2 0.6 copy-start.11
  27.9 8.4 %copy-start.15 = (f32[2,8,4,128]{3,2,1,0:T(4,128)S(1)}, f32[2,8,4,128]{3,2,1,0:T(4,128)}, u32[]{:S(2)}) copy-start(f32[2,8,4,128]{3,2,1,0:T(4,128)} %get-tuple-element.39) | copy-start | bytes 98308
  34.9 15.3 %collective-permute-start.8 = (f32[5,8,40,128]{3,2,1,0:T(8,128)}, f32[5,8,40,128]{3,2,1,0:T(8,128)S(1)}, u32[]{:S(2)}, u32[]{:S(2)}) collective-permute-start(f32[5,8,40,128]{3,2,1,0:T(8,128)} %get-tuple-element.44.refs_1_), channel_id=1, source_target_pairs={{16,0},{20,4},{24,8},{28,12},{17,1},{21,5},{25,9},{29,13},{18,2},{... | collective-permute-start | bytes 2457608 | tf_op jit(solution)/shard_map/ppermute | solution.py:552
  36.3 0.7 collective-permute-start.6
  36.9 0.6 copy-start.12
  39.4 3.5 %collective-permute-start.9 = (f32[8,40,128]{2,1,0:T(8,128)}, f32[8,40,128]{2,1,0:T(8,128)S(1)}, u32[]{:S(2)}, u32[]{:S(2)}) collective-permute-start(f32[8,40,128]{2,1,0:T(8,128)} %get-tuple-element.40.refs_0_), channel_id=1, source_target_pairs={{0,16},{4,20},{8,24},{12,28},{1,17},{5,21},{9,25},{13,29},{2,18},{... | collective-permute-start | bytes 491528 | tf_op jit(solution)/shard_map/ppermute | solution.py:552
  42.8 0.7 copy-start.10
  50.2 0.9 %copy-start.3 = (f32[5,8,40,128]{3,2,1,0:T(8,128)}, f32[5,8,40,128]{3,2,1,0:T(8,128)S(1)}, u32[]{:S(2)}) copy-start(f32[5,8,40,128]{3,2,1,0:T(8,128)S(1)} %collective-permute-done.8.refs_1_) | copy-start | bytes 2457604
  53.6 5.4 %collective-permute-start.10 = (f32[6,2,32,128]{3,2,1,0:T(8,128)}, f32[6,2,32,128]{3,2,1,0:T(8,128)S(1)}, u32[]{:S(2)}, u32[]{:S(2)}) collective-permute-start(f32[6,2,32,128]{3,2,1,0:T(8,128)} %get-tuple-element.54), channel_id=1, source_target_pairs={{0,4},{4,0},{8,12},{12,8},{1,5},{5,1},{9,13},{13,9},{2,6},{6,2},{1... | collective-permute-start | bytes 589832 | tf_op jit(solution)/shard_map/ppermute | solution.py:580
  53.7 12.7 %collective-permute-start.11 = (f32[6,2,32,128]{3,2,1,0:T(8,128)}, f32[6,2,32,128]{3,2,1,0:T(8,128)S(1)}, u32[]{:S(2)}, u32[]{:S(2)}) collective-permute-start(f32[6,2,32,128]{3,2,1,0:T(8,128)} %get-tuple-element.55), channel_id=1, source_target_pairs={{0,8},{4,12},{8,0},{12,4},{1,9},{5,13},{9,1},{13,5},{2,10},{6,14},... | collective-permute-start | bytes 589832 | tf_op jit(solution)/shard_map/ppermute | solution.py:580
  59.0 7.5 %collective-permute-start.12 = (f32[6,2,32,128]{3,2,1,0:T(8,128)}, f32[6,2,32,128]{3,2,1,0:T(8,128)S(1)}, u32[]{:S(2)}, u32[]{:S(2)}) collective-permute-start(f32[6,2,32,128]{3,2,1,0:T(8,128)} %get-tuple-element.56), channel_id=1, source_target_pairs={{0,12},{4,8},{8,4},{12,0},{1,13},{5,9},{9,5},{13,1},{2,14},{6,10},... | collective-permute-start | bytes 589832 | tf_op jit(solution)/shard_map/ppermute | solution.py:580
  59.0 7.5 %copy-start.7 = (f32[6,2,32,128]{3,2,1,0:T(8,128)}, f32[6,2,32,128]{3,2,1,0:T(8,128)S(1)}, u32[]{:S(2)}) copy-start(f32[6,2,32,128]{3,2,1,0:T(8,128)S(1)} %collective-permute-done.10.refs_1_) | copy-start | bytes 589828
  66.4 0.7 copy-start.8
  66.4 0.8 %copy-start.9 = (f32[6,2,32,128]{3,2,1,0:T(8,128)}, f32[6,2,32,128]{3,2,1,0:T(8,128)S(1)}, u32[]{:S(2)}) copy-start(f32[6,2,32,128]{3,2,1,0:T(8,128)S(1)} %collective-permute-done.12.refs_3_) | copy-start | bytes 589828
where the time goes:
time: 70.1 us; the launch traced here: 69.6 us
  Pallas kernels  29.3 us (42%)
  starting transfers between devices  20.4 us (29%)
  waiting for transfers between devices  13.8 us (20%)
  local copies, waits for them, and re-layouts  5.74 us (8%)
    pallas_call x8, Pallas kernels, call(): pl.pallas_call(functools.partial(kernel, p), name=name, out_shape=outs, i...  29.3 us
    ppermute x6, starting transfers between devices, swap(): return lax.ppermute(value, ('grp', 'ty'), pairs)  11 us
    ppermute x3, waiting for transfers between devices, local(): lax.ppermute(outs[k], 'ty', [(i, i ^ k) for i in range(n)])  7.47 us
    ppermute x3, starting transfers between devices, local(): lax.ppermute(outs[k], 'ty', [(i, i ^ k) for i in range(n)])  5.39 us
    unnamed x32, local copies, waits for them, and re-layouts  4.3 us
    ppermute x6, waiting for transfers between devices, swap(): return lax.ppermute(value, ('grp', 'ty'), pairs)  4.11 us
    ppermute x2, starting transfers between devices, across(): return lax.ppermute(value, ('grp', 'ty'), other)  2.61 us
    ppermute x2, waiting for transfers between devices, across(): return lax.ppermute(value, ('grp', 'ty'), other)  2.2 us
  transfers between devices with their start and end apart: 13, of which 3 were waited for; matrix products, arithmetic and copies ran while one was open for 2% of the time, Pallas kernels for 18%

commit v1 on v0

--- a/solution.py
+++ b/solution.py
@@ -497,7 +497,7 @@
                 out_specs=jax.tree.map(lambda _: VMEM, outs),
                 scratch_shapes=[pltpu.VMEM(s, F32) for s in scratch],
                 input_output_aliases=aliases or {},
-                compiler_params=pltpu.CompilerParams(vmem_limit_bytes=56 * 2**20),
+                compiler_params=pltpu.CompilerParams(vmem_limit_bytes=20 * 2**20),
             )(*ins)
 
         def swap(value, mask, grp):

time: 70.1 us -> 50 us (0.71)
  Pallas kernels: 29.3 us -> 12.7 us
  local copies, waits for them, and re-layouts: 5.74 us -> 3.42 us
    pallas_call x8, Pallas kernels: 29.3 us -> 12.7 us  [call(): pl.pallas_call(functools.partial(kernel, p), name=name, out_shape=outs, i...]
    unnamed x32 -> x12, local copies, waits for them, and re-layouts: 4.3 us -> 3.17 us
  transfers between devices with their start and end apart: 13 -> 13, of which waited for: 3 -> 3; matrix products, arithmetic and copies ran while one was open for 2% -> 0% of each run, Pallas kernels for 18% -> 13%
where the time goes in v1:
time: 50 us; the launch traced here: 49.6 us
  starting transfers between devices  20 us (40%)
  waiting for transfers between devices  13.2 us (26%)
  Pallas kernels  12.7 us (25%)
  local copies, waits for them, and re-layouts  3.42 us (7%)
    pallas_call x8, Pallas kernels, call(): pl.pallas_call(functools.partial(kernel, p), name=name, out_shape=outs, i...  12.7 us
    ppermute x6, starting transfers between devices, swap(): return lax.ppermute(value, ('grp', 'ty'), pairs)  11 us
    ppermute x3, waiting for transfers between devices, local(): lax.ppermute(outs[k], 'ty', [(i, i ^ k) for i in range(n)])  7.27 us
    ppermute x3, starting transfers between devices, local(): lax.ppermute(outs[k], 'ty', [(i, i ^ k) for i in range(n)])  5.08 us
    ppermute x6, waiting for transfers between devices, swap(): return lax.ppermute(value, ('grp', 'ty'), pairs)  3.95 us
    unnamed x12, local copies, waits for them, and re-layouts  3.17 us
    ppermute x2, starting transfers between devices, across(): return lax.ppermute(value, ('grp', 'ty'), other)  2.63 us
    ppermute x2, waiting for transfers between devices, across(): return lax.ppermute(value, ('grp', 'ty'), other)  1.99 us
  transfers between devices with their start and end apart: 13, of which 3 were waited for; matrix products, arithmetic and copies ran while one was open for 0% of the time, Pallas kernels for 13%

profile of v1, /device:TPU:1, one launch (start us, length us, event | category | flops | bytes accessed | tf_op | source)
XLA Modules:
  0.0 49.6 jit_solution(7264394011743126872)
XLA Ops:
  0.0 0.0 copy-start.4
  0.0 0.0 copy-start.1
  0.0 0.7 %copy-done.4 = f32[19]{0:T(128)S(1)} copy-done((f32[19]{0:T(128)S(1)}, f32[19]{0:T(128)}, u32[]{:S(2)}) %copy-start.4) | copy-done | bytes 100
  0.7 0.0 copy-done.1
  0.7 0.0 copy-start
  0.7 1.1 %copy-done = f32[1,23,32,2,128]{4,3,2,1,0:T(2,128)S(1)} copy-done((f32[1,23,32,2,128]{4,3,2,1,0:T(2,128)S(1)}, f32[1,23,32,2,128]{4,3,2,1,0:T(2,128)}, u32[]{:S(2)}) %copy-start) | copy-done | bytes 753688
  1.8 0.0 copy-start.2
  1.8 0.7 %copy-done.2 = s32[2,128]{1,0:T(2,128)S(1)} copy-done((s32[2,128]{1,0:T(2,128)S(1)}, s32[2,128]{1,0:T(2,128)}, u32[]{:S(2)}) %copy-start.2) | copy-done | bytes 1048
  2.5 0.0 copy-start.3
  2.5 0.7 %copy-done.3 = f32[2,128]{1,0:T(2,128)S(1)} copy-done((f32[2,128]{1,0:T(2,128)S(1)}, f32[2,128]{1,0:T(2,128)}, u32[]{:S(2)}) %copy-start.3) | copy-done | bytes 1048
  3.2 0.9 %pack.1 = (f32[6,2,40,128]{3,2,1,0:T(8,128)S(1)}, f32[6,2,40,128]{3,2,1,0:T(8,128)S(1)}, f32[6,2,40,128]{3,2,1,0:T(8,128)S(1)}, f32[6,2,40,128]{3,2,1,0:T(8,128)...) custom-call(f32[1472,128]{1,0:T(8,128)S(1)} %bitcast.2, ...), custom_call_target="tpu_custom_call" | custom-call | tf_op jit(solution)/shard_map/pack/pallas_call | solution.py:492
  4.1 3.9 %collective-permute-start.3 = (f32[6,2,40,128]{3,2,1,0:T(8,128)S(1)}, f32[6,2,40,128]{3,2,1,0:T(8,128)S(1)}, u32[]{:S(2)}, u32[]{:S(2)}) collective-permute-start(f32[6,2,40,128]{3,2,1,0:T(8,128)S(1)} %get-tuple-element.36), channel_id=1, source_target_pairs={{16,20},{20,16},{24,28},{28,24},{17,21},{21,17},{25,29},{29,25},{1... | collective-permute-start | bytes 737288 | tf_op jit(solution)/shard_map/ppermute | solution.py:505
  8.0 3.1 %collective-permute-start.4 = (f32[6,2,40,128]{3,2,1,0:T(8,128)S(1)}, f32[6,2,40,128]{3,2,1,0:T(8,128)S(1)}, u32[]{:S(2)}, u32[]{:S(2)}) collective-permute-start(f32[6,2,40,128]{3,2,1,0:T(8,128)S(1)} %get-tuple-element.37), channel_id=1, source_target_pairs={{16,24},{20,28},{24,16},{28,20},{17,25},{21,29},{25,17},{29,21},{1... | collective-permute-start | bytes 737288 | tf_op jit(solution)/shard_map/ppermute | solution.py:505
  11.2 1.9 %collective-permute-start.5 = (f32[6,2,40,128]{3,2,1,0:T(8,128)S(1)}, f32[6,2,40,128]{3,2,1,0:T(8,128)S(1)}, u32[]{:S(2)}, u32[]{:S(2)}) collective-permute-start(f32[6,2,40,128]{3,2,1,0:T(8,128)S(1)} %get-tuple-element.38), channel_id=1, source_target_pairs={{16,28},{20,24},{24,20},{28,16},{17,29},{21,25},{25,21},{29,17},{1... | collective-permute-start | bytes 737288 | tf_op jit(solution)/shard_map/ppermute | solution.py:505
  13.1 0.7 %collective-permute-start = (f32[2,2,40,128]{3,2,1,0:T(8,128)S(1)}, f32[2,2,40,128]{3,2,1,0:T(8,128)S(1)}, u32[]{:S(2)}, u32[]{:S(2)}) collective-permute-start(f32[2,2,40,128]{3,2,1,0:T(8,128)S(1)} %get-tuple-element.32), channel_id=1, source_target_pairs={{0,4},{4,0},{8,12},{12,8},{1,5},{5,1},{9,13},{13,9},{2,6},{6,2},{1... | collective-permute-start | bytes 245768 | tf_op jit(solution)/shard_map/ppermute | solution.py:505
  13.8 0.7 %collective-permute-start.1 = (f32[2,2,40,128]{3,2,1,0:T(8,128)S(1)}, f32[2,2,40,128]{3,2,1,0:T(8,128)S(1)}, u32[]{:S(2)}, u32[]{:S(2)}) collective-permute-start(f32[2,2,40,128]{3,2,1,0:T(8,128)S(1)} %get-tuple-element.33), channel_id=1, source_target_pairs={{0,8},{4,12},{8,0},{12,4},{1,9},{5,13},{9,1},{13,5},{2,10},{6,14},... | collective-permute-start | bytes 245768 | tf_op jit(solution)/shard_map/ppermute | solution.py:505
  14.4 0.0 collective-permute-done.refs_5_.refs_1_
  14.5 0.7 %collective-permute-start.2 = (f32[2,2,40,128]{3,2,1,0:T(8,128)S(1)}, f32[2,2,40,128]{3,2,1,0:T(8,128)S(1)}, u32[]{:S(2)}, u32[]{:S(2)}) collective-permute-start(f32[2,2,40,128]{3,2,1,0:T(8,128)S(1)} %get-tuple-element.34), channel_id=1, source_target_pairs={{0,12},{4,8},{8,4},{12,0},{1,13},{5,9},{9,5},{13,1},{2,14},{6,10},... | collective-permute-start | bytes 245768 | tf_op jit(solution)/shard_map/ppermute | solution.py:505
  15.1 0.0 collective-permute-done.1.refs_6_.refs_2_
  15.1 0.0 collective-permute-done.2.refs_7_.refs_3_
  15.2 0.0 collective-permute-done.3.refs_1_
  15.2 0.0 collective-permute-done.4.refs_2_
  15.2 3.9 %collective-permute-done.5.refs_3_ = f32[6,2,40,128]{3,2,1,0:T(8,128)S(1)} collective-permute-done((f32[6,2,40,128]{3,2,1,0:T(8,128)S(1)}, f32[6,2,40,128]{3,2,1,0:T(8,128)S(1)}, u32[]{:S(2)}, u32[]{:S(2)}) %collective-permute-start.5) | collective-permute-done | bytes 245792 | tf_op jit(solution)/shard_map/ppermute | solution.py:505
  19.1 0.0 copy-start.5
  19.1 0.7 %collective-permute-start.7 = (f32[6,8,4,128]{3,2,1,0:T(4,128)S(1)}, f32[6,8,4,128]{3,2,1,0:T(4,128)S(1)}, u32[]{:S(2)}, u32[]{:S(2)}) collective-permute-start(f32[6,8,4,128]{3,2,1,0:T(4,128)S(1)} %get-tuple-element.41), channel_id=1, source_target_pairs={{28,29},{29,28},{17,18},{18,17},{30,31},{31,30}} | collective-permute-start | bytes 294920 | tf_op jit(solution)/shard_map/ppermute | solution.py:514
  19.8 0.0 copy-done.5
  19.9 2.3 %mix.1 = (bf16[640,640]{1,0:T(8,128)(2,1)S(1)}, bf16[640,640]{1,0:T(8,128)(2,1)S(1)}) custom-call(f32[128,128]{1,0:T(8,128)S(1)} %pad.9.reaction), custom_call_target="tpu_custom_call" | custom-call | tf_op jit(solution)/shard_map/mix/pallas_call | solution.py:492
  22.2 0.1 reshape.9
  22.3 0.1 broadcast_in_dim.3
  22.3 0.1 reshape.10.refs_5_.refs_4_
  22.4 0.0 collective-permute-done.7.refs_4_
  22.4 4.1 %tracer_first.1 = (f32[5,8,40,128]{3,2,1,0:T(8,128)S(1)}, f32[8,40,128]{2,1,0:T(8,128)S(1)}, f32[8,40,128]{2,1,0:T(8,128)S(1)}) custom-call(f32[6,2,40,128]{3,2,1,0:T(8,128)S(1)} %get-tuple-element.35.refs_0_, f32[6,2,40,128]{3,2,1,0:T(8,128)S(1)} %collective-permute-done.3.refs_1_, f32[6,2,40,128]{3,2,1,0:T(8,128)S(1)} %collective-permute-done.4.refs_2_, ...), custom_call_target="tpu_custom_call" | custom-call | tf_op jit(solution)/shard_map/tracer_first/pallas_call | solution.py:492
  26.6 1.3 %collective-permute-start.8 = (f32[5,8,40,128]{3,2,1,0:T(8,128)S(1)}, f32[5,8,40,128]{3,2,1,0:T(8,128)S(1)}, u32[]{:S(2)}, u32[]{:S(2)}) collective-permute-start(f32[5,8,40,128]{3,2,1,0:T(8,128)S(1)} %get-tuple-element.44.refs_1_), channel_id=1, source_target_pairs={{16,0},{20,4},{24,8},{28,12},{17,1},{21,5},{25,9},{29,13},{18,2},{... | collective-permute-start | bytes 2457608 | tf_op jit(solution)/shard_map/ppermute | solution.py:552
  27.9 0.7 %collective-permute-start.6 = (f32[2,8,4,128]{3,2,1,0:T(4,128)S(1)}, f32[2,8,4,128]{3,2,1,0:T(4,128)S(1)}, u32[]{:S(2)}, u32[]{:S(2)}) collective-permute-start(f32[2,8,4,128]{3,2,1,0:T(4,128)S(1)} %get-tuple-element.39), channel_id=1, source_target_pairs={{12,13},{13,12},{1,2},{2,1},{14,15},{15,14}} | collective-permute-start | bytes 98312 | tf_op jit(solution)/shard_map/ppermute | solution.py:514
  28.6 0.0 collective-permute-done.6.refs_4_
  28.6 1.3 %collective-permute-start.9 = (f32[8,40,128]{2,1,0:T(8,128)S(1)}, f32[8,40,128]{2,1,0:T(8,128)S(1)}, u32[]{:S(2)}, u32[]{:S(2)}) collective-permute-start(f32[8,40,128]{2,1,0:T(8,128)S(1)} %get-tuple-element.40.refs_0_), channel_id=1, source_target_pairs={{0,16},{4,20},{8,24},{12,28},{1,17},{5,21},{9,25},{13,29},{2,18},{... | collective-permute-start | bytes 491528 | tf_op jit(solution)/shard_map/ppermute | solution.py:552
  29.9 2.0 %collective-permute-done.9.refs_0_ = f32[8,40,128]{2,1,0:T(8,128)S(1)} collective-permute-done((f32[8,40,128]{2,1,0:T(8,128)S(1)}, f32[8,40,128]{2,1,0:T(8,128)S(1)}, u32[]{:S(2)}, u32[]{:S(2)}) %collective-permute-start.9) | collective-permute-done | bytes 163872 | tf_op jit(solution)/shard_map/ppermute | solution.py:552
  31.9 4.0 %tracer_second.1 = (f32[6,2,32,128]{3,2,1,0:T(8,128)S(1)}, f32[6,2,32,128]{3,2,1,0:T(8,128)S(1)}, f32[6,2,32,128]{3,2,1,0:T(8,128)S(1)}, f32[6,2,32,128]{3,2,1,0:T(8,128)S(1)}) custom-call(f32[8,40,128]{2,1,0:T(8,128)S(1)} %collective-permute-done.9.refs_0_, f32[5,8,40,128]{3,2,1,0:T(8,128)S(1)} %get-tuple-element.44.refs_1_, ...), custom_call_target="tpu_custom_call" | custom-call | tf_op jit(solution)/shard_map/tracer_second/pallas_call | solution.py:492
  35.9 0.0 collective-permute-done.8.refs_1_
  35.9 0.1 ocean_second.1
  36.0 0.2 collective-permute-start.10
  36.2 4.9 %collective-permute-start.11 = (f32[6,2,32,128]{3,2,1,0:T(8,128)S(1)}, f32[6,2,32,128]{3,2,1,0:T(8,128)S(1)}, u32[]{:S(2)}, u32[]{:S(2)}) collective-permute-start(f32[6,2,32,128]{3,2,1,0:T(8,128)S(1)} %get-tuple-element.55), channel_id=1, source_target_pairs={{0,8},{4,12},{8,0},{12,4},{1,9},{5,13},{9,1},{13,5},{2,10},{6,14},... | collective-permute-start | bytes 589832 | tf_op jit(solution)/shard_map/ppermute | solution.py:580
  41.1 0.0 collective-permute-start.12
  41.1 0.0 collective-permute-done.10.refs_1_
  41.1 7.3 %collective-permute-done.11.refs_2_ = f32[6,2,32,128]{3,2,1,0:T(8,128)S(1)} collective-permute-done((f32[6,2,32,128]{3,2,1,0:T(8,128)S(1)}, f32[6,2,32,128]{3,2,1,0:T(8,128)S(1)}, u32[]{:S(2)}, u32[]{:S(2)}) %collective-permute-start.11) | collective-permute-done | bytes 196640 | tf_op jit(solution)/shard_map/ppermute | solution.py:580
  48.4 0.0 collective-permute-done.12.refs_3_
  48.4 1.2 %unpack.1 = f32[1472,128]{1,0:T(8,128)} custom-call(f32[6,2,32,128]{3,2,1,0:T(8,128)S(1)} %get-tuple-element.53.refs_0_, f32[6,2,32,128]{3,2,1,0:T(8,128)S(1)} %collective-permute-done.10.refs_1_, f32[6,2,32,128]{3,2,1,0:T(8,128)S(1)} %collective-permute-done.11.refs_2_, f32[6,2,32,128]{3,2,1,0:T(8,128)S(1)} %collective-permute-done.12.refs_3_), custom_call_target="tpu_custom_call" | custom-call | tf_op jit(solution)/shard_map/unpack/pallas_call | solution.py:492
  (4 shorter events, 0.1 us)
Async XLA Ops:
  0.0 0.7 %copy-start.4 = (f32[19]{0:T(128)S(1)}, f32[19]{0:T(128)}, u32[]{:S(2)}) copy-start(f32[19]{0:T(128)} %absorb.1) | copy-start | bytes 232
  0.0 0.7 %copy-start.1 = (s32[2,128]{1,0:T(2,128)S(1)}, s32[2,128]{1,0:T(2,128)}, u32[]{:S(2)}) copy-start(s32[2,128]{1,0:T(2,128)} %land.1) | copy-start | bytes 3076
  0.7 1.1 %copy-start = (f32[1,23,32,2,128]{4,3,2,1,0:T(2,128)S(1)}, f32[1,23,32,2,128]{4,3,2,1,0:T(2,128)}, u32[]{:S(2)}) copy-start(f32[1,23,32,2,128]{4,3,2,1,0:T(2,128)} %param.6) | copy-start | bytes 2260996
  1.8 0.7 %copy-start.2 = (s32[2,128]{1,0:T(2,128)S(1)}, s32[2,128]{1,0:T(2,128)}, u32[]{:S(2)}) copy-start(s32[2,128]{1,0:T(2,128)} %bottom.1) | copy-start | bytes 3076
  2.5 0.7 %copy-start.3 = (f32[2,128]{1,0:T(2,128)S(1)}, f32[2,128]{1,0:T(2,128)}, u32[]{:S(2)}) copy-start(f32[2,128]{1,0:T(2,128)} %sw.1) | copy-start | bytes 3076
  4.1 11.1 %collective-permute-start.3 = (f32[6,2,40,128]{3,2,1,0:T(8,128)S(1)}, f32[6,2,40,128]{3,2,1,0:T(8,128)S(1)}, u32[]{:S(2)}, u32[]{:S(2)}) collective-permute-start(f32[6,2,40,128]{3,2,1,0:T(8,128)S(1)} %get-tuple-element.36), channel_id=1, source_target_pairs={{16,20},{20,16},{24,28},{28,24},{17,21},{21,17},{25,29},{29,25},{1... | collective-permute-start | bytes 737288 | tf_op jit(solution)/shard_map/ppermute | solution.py:505
  8.0 7.1 %collective-permute-start.4 = (f32[6,2,40,128]{3,2,1,0:T(8,128)S(1)}, f32[6,2,40,128]{3,2,1,0:T(8,128)S(1)}, u32[]{:S(2)}, u32[]{:S(2)}) collective-permute-start(f32[6,2,40,128]{3,2,1,0:T(8,128)S(1)} %get-tuple-element.37), channel_id=1, source_target_pairs={{16,24},{20,28},{24,16},{28,20},{17,25},{21,29},{25,17},{29,21},{1... | collective-permute-start | bytes 737288 | tf_op jit(solution)/shard_map/ppermute | solution.py:505
  11.2 7.9 %collective-permute-start.5 = (f32[6,2,40,128]{3,2,1,0:T(8,128)S(1)}, f32[6,2,40,128]{3,2,1,0:T(8,128)S(1)}, u32[]{:S(2)}, u32[]{:S(2)}) collective-permute-start(f32[6,2,40,128]{3,2,1,0:T(8,128)S(1)} %get-tuple-element.38), channel_id=1, source_target_pairs={{16,28},{20,24},{24,20},{28,16},{17,29},{21,25},{25,21},{29,17},{1... | collective-permute-start | bytes 737288 | tf_op jit(solution)/shard_map/ppermute | solution.py:505
  13.1 1.4 %collective-permute-start = (f32[2,2,40,128]{3,2,1,0:T(8,128)S(1)}, f32[2,2,40,128]{3,2,1,0:T(8,128)S(1)}, u32[]{:S(2)}, u32[]{:S(2)}) collective-permute-start(f32[2,2,40,128]{3,2,1,0:T(8,128)S(1)} %get-tuple-element.32), channel_id=1, source_target_pairs={{0,4},{4,0},{8,12},{12,8},{1,5},{5,1},{9,13},{13,9},{2,6},{6,2},{1... | collective-permute-start | bytes 245768 | tf_op jit(solution)/shard_map/ppermute | solution.py:505
  13.8 1.4 %collective-permute-start.1 = (f32[2,2,40,128]{3,2,1,0:T(8,128)S(1)}, f32[2,2,40,128]{3,2,1,0:T(8,128)S(1)}, u32[]{:S(2)}, u32[]{:S(2)}) collective-permute-start(f32[2,2,40,128]{3,2,1,0:T(8,128)S(1)} %get-tuple-element.33), channel_id=1, source_target_pairs={{0,8},{4,12},{8,0},{12,4},{1,9},{5,13},{9,1},{13,5},{2,10},{6,14},... | collective-permute-start | bytes 245768 | tf_op jit(solution)/shard_map/ppermute | solution.py:505
  14.5 0.7 %collective-permute-start.2 = (f32[2,2,40,128]{3,2,1,0:T(8,128)S(1)}, f32[2,2,40,128]{3,2,1,0:T(8,128)S(1)}, u32[]{:S(2)}, u32[]{:S(2)}) collective-permute-start(f32[2,2,40,128]{3,2,1,0:T(8,128)S(1)} %get-tuple-element.34), channel_id=1, source_target_pairs={{0,12},{4,8},{8,4},{12,0},{1,13},{5,9},{9,5},{13,1},{2,14},{6,10},... | collective-permute-start | bytes 245768 | tf_op jit(solution)/shard_map/ppermute | solution.py:505
  19.1 0.7 %copy-start.5 = (f32[19,19]{1,0:T(8,128)S(1)}, f32[19,19]{1,0:T(8,128)}, u32[]{:S(2)}) copy-start(f32[19,19]{1,0:T(8,128)} %param.11) | copy-start | bytes 4336
  19.1 3.3 %collective-permute-start.7 = (f32[6,8,4,128]{3,2,1,0:T(4,128)S(1)}, f32[6,8,4,128]{3,2,1,0:T(4,128)S(1)}, u32[]{:S(2)}, u32[]{:S(2)}) collective-permute-start(f32[6,8,4,128]{3,2,1,0:T(4,128)S(1)} %get-tuple-element.41), channel_id=1, source_target_pairs={{28,29},{29,28},{17,18},{18,17},{30,31},{31,30}} | collective-permute-start | bytes 294920 | tf_op jit(solution)/shard_map/ppermute | solution.py:514
  26.6 9.4 %collective-permute-start.8 = (f32[5,8,40,128]{3,2,1,0:T(8,128)S(1)}, f32[5,8,40,128]{3,2,1,0:T(8,128)S(1)}, u32[]{:S(2)}, u32[]{:S(2)}) collective-permute-start(f32[5,8,40,128]{3,2,1,0:T(8,128)S(1)} %get-tuple-element.44.refs_1_), channel_id=1, source_target_pairs={{16,0},{20,4},{24,8},{28,12},{17,1},{21,5},{25,9},{29,13},{18,2},{... | collective-permute-start | bytes 2457608 | tf_op jit(solution)/shard_map/ppermute | solution.py:552
  27.9 0.7 %collective-permute-start.6 = (f32[2,8,4,128]{3,2,1,0:T(4,128)S(1)}, f32[2,8,4,128]{3,2,1,0:T(4,128)S(1)}, u32[]{:S(2)}, u32[]{:S(2)}) collective-permute-start(f32[2,8,4,128]{3,2,1,0:T(4,128)S(1)} %get-tuple-element.39), channel_id=1, source_target_pairs={{12,13},{13,12},{1,2},{2,1},{14,15},{15,14}} | collective-permute-start | bytes 98312 | tf_op jit(solution)/shard_map/ppermute | solution.py:514
  28.6 3.3 %collective-permute-start.9 = (f32[8,40,128]{2,1,0:T(8,128)S(1)}, f32[8,40,128]{2,1,0:T(8,128)S(1)}, u32[]{:S(2)}, u32[]{:S(2)}) collective-permute-start(f32[8,40,128]{2,1,0:T(8,128)S(1)} %get-tuple-element.40.refs_0_), channel_id=1, source_target_pairs={{0,16},{4,20},{8,24},{12,28},{1,17},{5,21},{9,25},{13,29},{2,18},{... | collective-permute-start | bytes 491528 | tf_op jit(solution)/shard_map/ppermute | solution.py:552
  36.0 5.1 %collective-permute-start.10 = (f32[6,2,32,128]{3,2,1,0:T(8,128)S(1)}, f32[6,2,32,128]{3,2,1,0:T(8,128)S(1)}, u32[]{:S(2)}, u32[]{:S(2)}) collective-permute-start(f32[6,2,32,128]{3,2,1,0:T(8,128)S(1)} %get-tuple-element.54), channel_id=1, source_target_pairs={{0,4},{4,0},{8,12},{12,8},{1,5},{5,1},{9,13},{13,9},{2,6},{6,2},{1... | collective-permute-start | bytes 589832 | tf_op jit(solution)/shard_map/ppermute | solution.py:580
  36.2 12.2 %collective-permute-start.11 = (f32[6,2,32,128]{3,2,1,0:T(8,128)S(1)}, f32[6,2,32,128]{3,2,1,0:T(8,128)S(1)}, u32[]{:S(2)}, u32[]{:S(2)}) collective-permute-start(f32[6,2,32,128]{3,2,1,0:T(8,128)S(1)} %get-tuple-element.55), channel_id=1, source_target_pairs={{0,8},{4,12},{8,0},{12,4},{1,9},{5,13},{9,1},{13,5},{2,10},{6,14},... | collective-permute-start | bytes 589832 | tf_op jit(solution)/shard_map/ppermute | solution.py:580
  41.1 7.3 %collective-permute-start.12 = (f32[6,2,32,128]{3,2,1,0:T(8,128)S(1)}, f32[6,2,32,128]{3,2,1,0:T(8,128)S(1)}, u32[]{:S(2)}, u32[]{:S(2)}) collective-permute-start(f32[6,2,32,128]{3,2,1,0:T(8,128)S(1)} %get-tuple-element.56), channel_id=1, source_target_pairs={{0,12},{4,8},{8,4},{12,0},{1,13},{5,9},{9,5},{13,1},{2,14},{6,10},... | collective-permute-start | bytes 589832 | tf_op jit(solution)/shard_map/ppermute | solution.py:580

commit v2 on v1

--- a/solution.py
+++ b/solution.py
@@ -7,11 +7,13 @@
 from jax.experimental.pallas import tpu as pltpu
 from jax.sharding import PartitionSpec as P
 
+
 STEPS = 2
 HALO = 2 * STEPS
 LANES = 128
 PAD = 8
 DYN = 4
+SHARED = 2
 
 integration_interval = 0.1
 tracer_interval = 0.08
@@ -29,6 +31,7 @@
 VMEM = pl.BlockSpec(memory_space=pltpu.VMEM)
 SMEM = pl.BlockSpec(memory_space=pltpu.SMEM)
 ANY = pl.BlockSpec(memory_space=pl.ANY)
+HBM = pl.BlockSpec(memory_space=pltpu.HBM)
 
 
 def dot(a, b):
@@ -75,8 +78,19 @@
         return out
 
 
-def pack_kernel(p, view, land, bottom, sw, absorb, *rest):
-    outs_t, outs_o, t_ref = rest[: p.n], rest[p.n : 2 * p.n], rest[2 * p.n]
+def part(src, mask, g):
+    n = len(src) // 2
+    return src[mask].at[g] if g < SHARED else src[n + mask].at[g - SHARED]
+
+
+def pack_kernel(p, *refs):
+    given, outs, t_ref, here, sems = refs[:5], refs[5 : 5 + 2 * p.n], refs[5 + 2 * p.n], refs[6 + 2 * p.n : 11 + 2 * p.n], refs[11 + 2 * p.n]
+    copies = [pltpu.make_async_copy(a, b, sems.at[i]) for i, (a, b) in enumerate(zip(given, here))]
+    for copy in copies:
+        copy.start()
+    for copy in copies:
+        copy.wait()
+    view, land, bottom, sw, absorb = here
     nz, rows, step = p.nz, p.rows, p.per * p.nz
     half = nz // 2
     ocean = p.is_ocean()
@@ -98,12 +112,12 @@
     def put(r, g, block):
         t_ref[g, r, HALO : HALO + LANES, :] = block.T
 
-    def send(outs, count):
+    def send(count):
         for mask in range(p.n):
             start = pl.multiple_of(p.chunk_of(p.xor(mask)) * p.chunk, 8)
             for g in range(count):
                 for r in range(rows):
-                    outs[mask][g, r] = t_ref[g, r, pl.ds(start, p.width), :]
+                    part(outs, mask, g)[r] = t_ref[g, r, pl.ds(start, p.width), :]
 
     zero = jnp.zeros((HALO, LANES), F32)
     for g in range(p.groups):
@@ -121,7 +135,7 @@
             if have < LANES - nz:
                 block = jnp.concatenate([block, jnp.zeros((LANES - nz - have, LANES), F32)], axis=0)
             put(r, p.tg, aux(r, block))
-        send(outs_t, p.groups)
+        send(p.groups)
 
     @pl.when(ocean)
     def _():
@@ -135,49 +149,45 @@
             above = below * jnp.exp(layer_depth * kd)
             forcing = (above - below) / layer_depth
             put(r, 1, aux(r, jnp.concatenate([jnp.zeros((2 * nz, LANES), F32), forcing], axis=0)))
-        send(outs_o, 2)
+        send(2)
 
 
 def edge_kernel(p, *refs):
-    src_t, src_o, z_t, z_o = refs[: p.n], refs[p.n : 2 * p.n], refs[2 * p.n], refs[2 * p.n + 1]
+    src, z = refs[: 2 * p.n], refs[2 * p.n + 1]
     left = p.chunk_of(p.ty()) == 0
-    ocean = p.is_ocean()
-
-    def copy(src, dst, count, lo):
+
+    def copy(lo):
         for mask in range(p.n):
             base = p.xor(mask) * p.rows
-            for g in range(count):
+            for g in range(p.groups):
                 for r in range(p.rows):
-                    dst[g, base + r] = src[mask][g, r, lo : lo + HALO, :]
-
-    for cond, src, dst, count in (
-        (ocean, src_o, z_o, 2),
-        (jnp.logical_not(ocean), src_t, z_t, p.groups),
-    ):
-
-        @pl.when(cond & left)
-        def _():
-            copy(src, dst, count, HALO)
-
-        @pl.when(cond & jnp.logical_not(left))
-        def _():
-            copy(src, dst, count, p.chunk)
+                    z[g, base + r] = part(src, mask, g)[r, lo : lo + HALO, :]
+
+    @pl.when(left)
+    def _():
+        copy(HALO)
+
+    @pl.when(jnp.logical_not(left))
+    def _():
+        copy(p.chunk)
 
 
 def assemble(p, src, z, g, dst):
     for mask in range(p.n):
         base = p.xor(mask) * p.rows
         for r in range(p.rows):
-            dst[1 + base + r, PAD : PAD + p.width, :] = src[mask][g, r]
-    chunk = p.chunk_of(p.ty())
+            dst[1 + base + r, PAD : PAD + p.width, :] = part(src, mask, g)[r]
+    chunk, tx = p.chunk_of(p.ty()), lax.axis_index("tx")
 
     @pl.when(chunk == 0)
     def _():
-        dst[1 : 1 + p.R, PAD : PAD + HALO, :] = z[g]
+        dst[1 : 1 + p.R, PAD : PAD + HALO, :] = jnp.where(tx > 0, z[g], 0.0)
 
     @pl.when(chunk == p.n - 1)
     def _():
-        dst[1 : 1 + p.R, PAD + p.width - HALO : PAD + p.width, :] = z[g]
+        dst[1 : 1 + p.R, PAD + p.width - HALO : PAD + p.width, :] = jnp.where(
+            tx < p.m - 1, z[g], 0.0
+        )
 
 
 def aux_fields(p, aux_ref, wet_ref, sw_ref):
@@ -277,7 +287,7 @@
             feh[r] = jnp.zeros((W, LANES), F32)
         fnh[r] = half * (va[1 + r, mid, :] + va[1 + r, up, :]) * inside
 
-    def group(g, _):
+    def group(g):
         load_group(g, c)
         for r in range(R):
             c0 = c[1 + r, mid, :]
@@ -334,7 +344,8 @@
             before = east
         return 0
 
-    lax.fori_loop(0, p.tg, group, 0)
+    for g in range(p.tg):
+        group(g)
 
     whole = [adv[g].reshape(R * W, LANES) for g in range(p.tg)]
     att = whole[0] * absorb[0:1, :]
@@ -360,7 +371,7 @@
 
 
 def ocean_first_kernel(p, *refs):
-    src, z, dyn, wet, sw, d, aux, pp = (refs[: p.n],) + refs[p.n :]
+    src, z, dyn, wet, sw, d, aux, pp = (refs[: 2 * p.n],) + refs[2 * p.n :]
 
     @pl.when(p.is_ocean())
     def _():
@@ -372,7 +383,7 @@
 
 
 def tracer_first_kernel(p, *refs):
-    src, (z, absorb, r_hi, r_lo, c1, wet, sw, d), scratch = refs[: p.n], refs[p.n : p.n + 8], refs[p.n + 8 :]
+    src, (z, absorb, r_hi, r_lo, _, c1, wet, sw, d), scratch = refs[: 2 * p.n], refs[2 * p.n : 2 * p.n + 9], refs[2 * p.n + 9 :]
 
     @pl.when(jnp.logical_not(p.is_ocean()))
     def _():
@@ -488,100 +499,107 @@
         def sds(*shape, dtype=F32):
             return jax.ShapeDtypeStruct(shape, dtype)
 
-        def call(kernel, name, outs, ins, scratch=(), in_specs=None, aliases=None):
+        def call(kernel, outs, ins, scratch=(), in_specs=None, aliases=None, cost=1):
             return pl.pallas_call(
                 functools.partial(kernel, p),
-                name=name,
                 out_shape=outs,
                 in_specs=in_specs or [VMEM] * len(ins),
                 out_specs=jax.tree.map(lambda _: VMEM, outs),
-                scratch_shapes=[pltpu.VMEM(s, F32) for s in scratch],
+                scratch_shapes=[pltpu.VMEM(s, F32) if isinstance(s, tuple) else s for s in scratch],
                 input_output_aliases=aliases or {},
+                cost_estimate=pl.CostEstimate(
+                    flops=cost * 10**9, bytes_accessed=cost * 10**6, transcendentals=0
+                ),
                 compiler_params=pltpu.CompilerParams(vmem_limit_bytes=20 * 2**20),
             )(*ins)
 
-        def swap(value, mask, grp):
-            pairs = [(grp * n + i, grp * n + (i ^ mask)) for i in range(n)]
-            return lax.ppermute(value, ("grp", "ty"), pairs)
-
-        def edges(value, grp):
-            pairs = []
-            size = lax.axis_size("tx")
+        def swap(value, mask):
+            return lax.ppermute(value, "ty", [(i, i ^ mask) for i in range(n)])
+
+        def swap_tracers(value, mask):
+            size = p.m
+            pairs = [(t * size + x, t * size + (x ^ 1)) for t in range(n) for x in range(size)]
+            both = n * size
+            pairs += [
+                (both + t * size + x, both + (t ^ mask) * size + x)
+                for t in range(n)
+                for x in range(size)
+            ]
+            return lax.ppermute(value, ("grp", "ty", "tx"), pairs)
+
+        def edges(value):
+            size = p.m
+            to = {i: (i + n * size) % (2 * n * size) for i in range(2 * n * size)}
             for tx in range(size - 1):
-                end = n - 1 if tx % 2 == 0 else 0
-                a = (grp * n + end) * size + tx
-                pairs += [(a, a + 1), (a + 1, a)]
-            return lax.ppermute(value, ("grp", "ty", "tx"), pairs)
+                for grp in range(2):
+                    a = (grp * n + (n - 1 if tx % 2 == 0 else 0)) * size + tx
+                    to[a], to[a + 1] = a + 1, a
+            return lax.ppermute(value, ("grp", "ty", "tx"), list(to.items()))
+
+        def across(value):
+            return lax.ppermute(value, "grp", [(0, 1), (1, 0)])
 
         flat = view.reshape(p.nf * p.nz * p.rows, p.cols)
         packed = call(
             pack_kernel,
-            "pack",
-            [sds(G, p.rows, W, LANES)] * n + [sds(2, p.rows, W, LANES)] * n,
-            [flat, land_mask, bottom_level, shortwave, absorb],
-            [(G, p.rows, LANES + 2 * HALO, LANES)],
-            [VMEM] * 4 + [SMEM],
+            [sds(SHARED, p.rows, W, LANES)] * n + [sds(G - SHARED, p.rows, W, LANES)] * n,
+            [pltpu.with_memory_space_constraint(x, pltpu.HBM) for x in (flat, land_mask, bottom_level, shortwave, absorb)],
+            [
+                (G, p.rows, LANES + 2 * HALO, LANES),
+                pltpu.VMEM(flat.shape, F32),
+                pltpu.VMEM(land_mask.shape, jnp.int32),
+                pltpu.VMEM(bottom_level.shape, jnp.int32),
+                pltpu.VMEM(shortwave.shape, F32),
+                pltpu.SMEM(absorb.shape, F32),
+                pltpu.SemaphoreType.DMA((5,)),
+            ],
+            [HBM] * 5,
         )
-        got_t = [packed[0]] + [swap(packed[k], k, 1) for k in range(1, n)]
-        got_o = [packed[n]] + [swap(packed[n + k], k, 0) for k in range(1, n)]
+        got = [packed[0]] + [swap(packed[k], k) for k in range(1, n)]
+        got += [packed[n]] + [swap_tracers(packed[n + k], k) for k in range(1, n)]
 
         react = jnp.pad(reaction, ((0, LANES - reaction.shape[0]), (0, LANES - reaction.shape[1])))
         size = p.tg * LANES
-        r_hi, r_lo = call(
-            mix_kernel, "mix", [sds(size, size, dtype=BF16), sds(size, size, dtype=BF16)], [react]
-        )
+        r_hi, r_lo = call(mix_kernel, [sds(size, size, dtype=BF16), sds(size, size, dtype=BF16)], [react])
         weights = jnp.pad(absorb, (0, p.tg * p.per - absorb.shape[0])).reshape(p.tg, p.per)
         weights = jnp.repeat(weights, p.nz, axis=1)
 
-        z_t, z_o = call(
-            edge_kernel, "edge", [sds(G, R, HALO, LANES), sds(2, R, HALO, LANES)], got_t + got_o
-        )
-        z_t, z_o = edges(z_t, 1), edges(z_o, 0)
+        z = edges(call(edge_kernel, [sds(G, R, HALO, LANES)], got + [r_hi], in_specs=[VMEM] * (2 * n) + [ANY])[0])
 
         padded = (R + 2, p.padded, LANES)
         block = (R, W, LANES)
         scratch = [padded, block, block] + [padded] * 5 + [block] + [padded] * 2 + [(p.tg,) + block]
-        dyn1, wet_o, sw_o = call(
-            ocean_first_kernel, "ocean_first", [sds(*block)] * 3, got_o + [z_o], [padded] * 3
-        )
-
-        def across(value, source):
-            other = [
-                ((source * n + i) , ((1 - source) * n + i)) for i in range(n)
-            ]
-            return lax.ppermute(value, ("grp", "ty"), other)
-
-        dyn1_t = across(dyn1, 0)
+        dyn1, wet_o, sw_o = call(ocean_first_kernel, [sds(*block)] * 3, got + [z], [padded] * 3)
+
+        dyn1_t = across(dyn1)
         c1, wet_t, sw_t = call(
             tracer_first_kernel,
-            "tracer_first",
             [sds(p.tg, *block), sds(*block), sds(*block)],
-            got_t + [z_t, weights, r_hi, r_lo],
+            got + [z, weights, r_hi, r_lo, dyn1],
             [padded] + scratch,
+            [VMEM] * (2 * n + 4) + [ANY],
+            cost=4,
         )
-        c1_o = across(c1, 1)
+        c1_o = across(c1)
         back = [sds(G, p.rows, p.chunk, LANES)] * n
         outs = call(
             tracer_second_kernel,
-            "tracer_second",
             back,
             [dyn1_t, c1, wet_t, sw_t, weights, r_hi, r_lo],
             [padded, block] + scratch,
+            cost=4,
         )
         outs = call(
             ocean_second_kernel,
-            "ocean_second",
             back,
             [dyn1, c1_o, wet_o, sw_o, weights] + list(outs),
             [padded, padded, block, block],
             aliases={5 + k: k for k in range(n)},
         )
         home = [outs[0]] + [
-            lax.ppermute(outs[k], "ty", [(i, i ^ k) for i in range(n)]) for k in range(1, n)
+            swap(outs[k], k) for k in range(1, n)
         ]
-        out = call(
-            unpack_kernel, "unpack", [sds(p.nf * p.nz * p.rows, p.cols)], home, [(LANES, LANES)]
-        )[0]
+        out = call(unpack_kernel, [sds(p.nf * p.nz * p.rows, p.cols)], home, [(LANES, LANES)])[0]
         return out.reshape((1,) + view.shape)
 
     in_specs = (

time: 50 us -> 38.5 us (0.77)
  starting transfers between devices: 20 us -> 12.5 us
  local copies, waits for them, and re-layouts: 3.42 us -> 0.25 us
  waiting for transfers between devices: 13.2 us -> 11.7 us
  Pallas kernels: 12.7 us -> 13.9 us
    ppermute x13 -> x12, starting transfers between devices: 20 us -> 12.5 us  [the longest x6 6.38 us: swap(): return lax.ppermute(value, 'ty', [(i, i ^ mask) for i in range(n)])]
    unnamed x12 -> x4, local copies, waits for them, and re-layouts: 3.17 us -> 0.01 us
    ppermute x13 -> x12, waiting for transfers between devices: 13.2 us -> 11.7 us  [the longest x6 8.91 us: swap(): return lax.ppermute(value, 'ty', [(i, i ^ mask) for i in range(n)])]
    pallas_call x8, Pallas kernels: 12.7 us -> 13.9 us  [call(): pl.pallas_call(functools.partial(kernel, p), out_shape=outs, in_specs=in_...]
  transfers between devices with their start and end apart: 13 -> 12, of which waited for: 3 -> 6; matrix products, arithmetic and copies ran while one was open for 0% -> 1% of each run, Pallas kernels for 13% -> 18%
where the time goes in v2:
time: 38.5 us; the launch traced here: 38.4 us
  Pallas kernels  13.9 us (36%)
  starting transfers between devices  12.5 us (32%)
  waiting for transfers between devices  11.7 us (30%)
    pallas_call x8, Pallas kernels, call(): pl.pallas_call(functools.partial(kernel, p), out_shape=outs, in_specs=in_...  13.9 us
    ppermute x6, waiting for transfers between devices, swap(): return lax.ppermute(value, 'ty', [(i, i ^ mask) for i in range(n)])  8.91 us
    ppermute x6, starting transfers between devices, swap(): return lax.ppermute(value, 'ty', [(i, i ^ mask) for i in range(n)])  6.38 us
    ppermute x1, starting transfers between devices, edges(): return lax.ppermute(value, ('grp', 'ty', 'tx'), list(to.items()))  2.91 us
    ppermute x3, starting transfers between devices, swap_tracers(): return lax.ppermute(value, ('grp', 'ty', 'tx'), pairs)  2.65 us
    ppermute x2, waiting for transfers between devices, across(): return lax.ppermute(value, 'grp', [(0, 1), (1, 0)])  2.06 us
  transfers between devices with their start and end apart: 12, of which 6 were waited for; matrix products, arithmetic and copies ran while one was open for 1% of the time, Pallas kernels for 18%

profile of v2, /device:TPU:1, one launch (start us, length us, event | category | flops | bytes accessed | tf_op | source)
XLA Modules:
  0.0 38.4 jit_solution(13113701953286862619)
XLA Ops:
  0.0 0.0 copy-start
  0.0 1.5 %shard_map.64 = (f32[2,2,40,128]{3,2,1,0:T(8,128)S(1)}, f32[2,2,40,128]{3,2,1,0:T(8,128)S(1)}, f32[2,2,40,128]{3,2,1,0:T(8,128)S(1)}, f32[2,2,40,128]{3,2,1,0:T(...) custom-call(f32[1472,128]{1,0:T(8,128)} %bitcast.2, ...), custom_call_target="tpu_custom_call" | custom-call | flops 1000000000 | bytes 1000000 | tf_op jit(solution)/shard_map/pallas_call | solution.py:503
  1.5 2.1 %collective-permute-start = (f32[2,2,40,128]{3,2,1,0:T(8,128)S(1)}, f32[2,2,40,128]{3,2,1,0:T(8,128)S(1)}, u32[]{:S(2)}, u32[]{:S(2)}) collective-permute-start(f32[2,2,40,128]{3,2,1,0:T(8,128)S(1)} %get-tuple-element.30), channel_id=1, source_target_pairs={{0,4},{4,0},{8,12},{12,8},{1,5},{5,1},{9,13},{13,9},{2,6},{6,2},{1... | collective-permute-start | bytes 245768 | tf_op jit(solution)/shard_map/ppermute | solution.py:517
  3.6 0.1 collective-permute-start.3
  3.7 1.4 %collective-permute-start.4 = (f32[4,2,40,128]{3,2,1,0:T(8,128)S(1)}, f32[4,2,40,128]{3,2,1,0:T(8,128)S(1)}, u32[]{:S(2)}, u32[]{:S(2)}) collective-permute-start(f32[4,2,40,128]{3,2,1,0:T(8,128)S(1)} %get-tuple-element.35), channel_id=1, source_target_pairs={{0,1},{1,0},{2,3},{3,2},{4,5},{5,4},{6,7},{7,6},{8,9},{9,8},{10,11... | collective-permute-start | bytes 491528 | tf_op jit(solution)/shard_map/ppermute | solution.py:528
  5.1 1.1 %collective-permute-start.5 = (f32[4,2,40,128]{3,2,1,0:T(8,128)S(1)}, f32[4,2,40,128]{3,2,1,0:T(8,128)S(1)}, u32[]{:S(2)}, u32[]{:S(2)}) collective-permute-start(f32[4,2,40,128]{3,2,1,0:T(8,128)S(1)} %get-tuple-element.36), channel_id=1, source_target_pairs={{0,1},{1,0},{2,3},{3,2},{4,5},{5,4},{6,7},{7,6},{8,9},{9,8},{10,11... | collective-permute-start | bytes 491528 | tf_op jit(solution)/shard_map/ppermute | solution.py:528
  6.3 1.2 %collective-permute-start.1 = (f32[2,2,40,128]{3,2,1,0:T(8,128)S(1)}, f32[2,2,40,128]{3,2,1,0:T(8,128)S(1)}, u32[]{:S(2)}, u32[]{:S(2)}) collective-permute-start(f32[2,2,40,128]{3,2,1,0:T(8,128)S(1)} %get-tuple-element.31), channel_id=1, source_target_pairs={{0,8},{4,12},{8,0},{12,4},{1,9},{5,13},{9,1},{13,5},{2,10},{6,14},... | collective-permute-start | bytes 245768 | tf_op jit(solution)/shard_map/ppermute | solution.py:517
  7.5 0.0 copy-done
  7.5 0.0 collective-permute-done.refs_1_
  7.6 0.3 collective-permute-start.2
  7.9 2.3 %shard_map.65 = (bf16[640,640]{1,0:T(8,128)(2,1)S(1)}, bf16[640,640]{1,0:T(8,128)(2,1)S(1)}) custom-call(f32[128,128]{1,0:T(8,128)S(1)} %pad.8.reaction), custom_call_target="tpu_custom_call" | custom-call | flops 1000000000 | bytes 1000000 | tf_op jit(solution)/shard_map/pallas_call | solution.py:503
  10.2 1.2 %collective-permute-done.1.refs_2_ = f32[2,2,40,128]{3,2,1,0:T(8,128)S(1)} collective-permute-done((f32[2,2,40,128]{3,2,1,0:T(8,128)S(1)}, f32[2,2,40,128]{3,2,1,0:T(8,128)S(1)}, u32[]{:S(2)}, u32[]{:S(2)}) %collective-permute-start.1) | collective-permute-done | bytes 81952 | tf_op jit(solution)/shard_map/ppermute | solution.py:517
  11.4 0.9 %collective-permute-done.2.refs_3_ = f32[2,2,40,128]{3,2,1,0:T(8,128)S(1)} collective-permute-done((f32[2,2,40,128]{3,2,1,0:T(8,128)S(1)}, f32[2,2,40,128]{3,2,1,0:T(8,128)S(1)}, u32[]{:S(2)}, u32[]{:S(2)}) %collective-permute-start.2) | collective-permute-done | bytes 81952 | tf_op jit(solution)/shard_map/ppermute | solution.py:517
  12.3 0.0 collective-permute-done.3.refs_5_
  12.3 0.0 collective-permute-done.4.refs_6_
  12.3 0.0 collective-permute-done.5.refs_7_
  12.3 0.0 copy-start.1
  12.4 2.9 %collective-permute-start.6 = (f32[6,8,4,128]{3,2,1,0:T(4,128)S(1)}, f32[6,8,4,128]{3,2,1,0:T(4,128)S(1)}, u32[]{:S(2)}, u32[]{:S(2)}) collective-permute-start(f32[6,8,4,128]{3,2,1,0:T(4,128)S(1)} %shard_map.66), channel_id=1, source_target_pairs={{0,16},{1,2},{2,1},{3,19},{4,20},{5,21},{6,22},{7,23},{8,24},{9,25... | collective-permute-start | bytes 294920 | tf_op jit(solution)/shard_map/ppermute | solution.py:537
  15.3 0.0 copy-done.1
  15.3 0.1 reshape.9
  15.4 0.1 broadcast_in_dim.3
  15.5 0.1 reshape.10.refs_9_.refs_4_
  15.6 0.7 %collective-permute-done.6.refs_8_ = f32[6,8,4,128]{3,2,1,0:T(4,128)S(1)} collective-permute-done((f32[6,8,4,128]{3,2,1,0:T(4,128)S(1)}, f32[6,8,4,128]{3,2,1,0:T(4,128)S(1)}, u32[]{:S(2)}, u32[]{:S(2)}) %collective-permute-start.6) | collective-permute-done | bytes 98336 | tf_op jit(solution)/shard_map/ppermute | solution.py:537
  16.3 4.2 %shard_map.68 = (f32[5,8,40,128]{3,2,1,0:T(8,128)S(1)}, f32[8,40,128]{2,1,0:T(8,128)S(1)}, f32[8,40,128]{2,1,0:T(8,128)S(1)}) custom-call(f32[2,2,40,128]{3,2,1,0:T(8,128)S(1)} %get-tuple-element.29.refs_0_, f32[2,2,40,128]{3,2,1,0:T(8,128)S(1)} %collective-permute-done.refs_1_, f32[2,2,40,128]{3,2,1,0:T(8,128)S(1)} %collective-permute-done.1.refs_2_, ...), custom_call_target="tpu_custom_call" | custom-call | flops 4000000000 | bytes 4000000 | tf_op jit(solution)/shard_map/pallas_call | solution.py:503
  20.5 0.1 collective-permute-start.7
  20.6 0.5 %collective-permute-start.8 = (f32[8,40,128]{2,1,0:T(8,128)S(1)}, f32[8,40,128]{2,1,0:T(8,128)S(1)}, u32[]{:S(2)}, u32[]{:S(2)}) collective-permute-start(f32[8,40,128]{2,1,0:T(8,128)S(1)} %get-tuple-element.38.refs_12_.refs_0_), channel_id=1, source_target_pairs={{0,16},{16,0},{1,17},{17,1},{2,18},{18,2},{3,19},{19,3},{4,20},{20... | collective-permute-start | bytes 491528 | tf_op jit(solution)/shard_map/ppermute | solution.py:540
  21.1 2.1 %collective-permute-done.8.refs_0_ = f32[8,40,128]{2,1,0:T(8,128)S(1)} collective-permute-done((f32[8,40,128]{2,1,0:T(8,128)S(1)}, f32[8,40,128]{2,1,0:T(8,128)S(1)}, u32[]{:S(2)}, u32[]{:S(2)}) %collective-permute-start.8) | collective-permute-done | bytes 163872 | tf_op jit(solution)/shard_map/ppermute | solution.py:540
  23.1 4.5 %shard_map.69 = (f32[6,2,32,128]{3,2,1,0:T(8,128)S(1)}, f32[6,2,32,128]{3,2,1,0:T(8,128)S(1)}, f32[6,2,32,128]{3,2,1,0:T(8,128)S(1)}, f32[6,2,32,128]{3,2,1,0:T(8,128)S(1)}) custom-call(f32[8,40,128]{2,1,0:T(8,128)S(1)} %collective-permute-done.8.refs_0_, f32[5,8,40,128]{3,2,1,0:T(8,128)S(1)} %get-tuple-element.40.refs_1_, ...), custom_call_target="tpu_custom_call" | custom-call | flops 4000000000 | bytes 4000000 | tf_op jit(solution)/shard_map/pallas_call | solution.py:503
  27.6 0.0 collective-permute-done.7.refs_1_
  27.6 0.1 shard_map.70
  27.7 0.5 %collective-permute-start.9 = (f32[6,2,32,128]{3,2,1,0:T(8,128)S(1)}, f32[6,2,32,128]{3,2,1,0:T(8,128)S(1)}, u32[]{:S(2)}, u32[]{:S(2)}) collective-permute-start(f32[6,2,32,128]{3,2,1,0:T(8,128)S(1)} %get-tuple-element.50), channel_id=1, source_target_pairs={{0,4},{4,0},{8,12},{12,8},{1,5},{5,1},{9,13},{13,9},{2,6},{6,2},{1... | collective-permute-start | bytes 589832 | tf_op jit(solution)/shard_map/ppermute | solution.py:517
  28.2 1.8 %collective-permute-start.10 = (f32[6,2,32,128]{3,2,1,0:T(8,128)S(1)}, f32[6,2,32,128]{3,2,1,0:T(8,128)S(1)}, u32[]{:S(2)}, u32[]{:S(2)}) collective-permute-start(f32[6,2,32,128]{3,2,1,0:T(8,128)S(1)} %get-tuple-element.51), channel_id=1, source_target_pairs={{0,8},{4,12},{8,0},{12,4},{1,9},{5,13},{9,1},{13,5},{2,10},{6,14},... | collective-permute-start | bytes 589832 | tf_op jit(solution)/shard_map/ppermute | solution.py:517
  30.0 0.4 %collective-permute-start.11 = (f32[6,2,32,128]{3,2,1,0:T(8,128)S(1)}, f32[6,2,32,128]{3,2,1,0:T(8,128)S(1)}, u32[]{:S(2)}, u32[]{:S(2)}) collective-permute-start(f32[6,2,32,128]{3,2,1,0:T(8,128)S(1)} %get-tuple-element.52), channel_id=1, source_target_pairs={{0,12},{4,8},{8,4},{12,0},{1,13},{5,9},{9,5},{13,1},{2,14},{6,10},... | collective-permute-start | bytes 589832 | tf_op jit(solution)/shard_map/ppermute | solution.py:517
  30.4 3.5 %collective-permute-done.9.refs_1_ = f32[6,2,32,128]{3,2,1,0:T(8,128)S(1)} collective-permute-done((f32[6,2,32,128]{3,2,1,0:T(8,128)S(1)}, f32[6,2,32,128]{3,2,1,0:T(8,128)S(1)}, u32[]{:S(2)}, u32[]{:S(2)}) %collective-permute-start.9) | collective-permute-done | bytes 196640 | tf_op jit(solution)/shard_map/ppermute | solution.py:517
  33.9 3.3 %collective-permute-done.10.refs_2_ = f32[6,2,32,128]{3,2,1,0:T(8,128)S(1)} collective-permute-done((f32[6,2,32,128]{3,2,1,0:T(8,128)S(1)}, f32[6,2,32,128]{3,2,1,0:T(8,128)S(1)}, u32[]{:S(2)}, u32[]{:S(2)}) %collective-permute-start.10) | collective-permute-done | bytes 196640 | tf_op jit(solution)/shard_map/ppermute | solution.py:517
  37.2 0.0 collective-permute-done.11.refs_3_
  37.2 1.2 %shard_map.71 = f32[1472,128]{1,0:T(8,128)} custom-call(f32[6,2,32,128]{3,2,1,0:T(8,128)S(1)} %get-tuple-element.49.refs_0_, f32[6,2,32,128]{3,2,1,0:T(8,128)S(1)} %collective-permute-done.9.refs_1_, f32[6,2,32,128]{3,2,1,0:T(8,128)S(1)} %collective-permute-done.10.refs_2_, f32[6,2,32,128]{3,2,1,0:T(8,128)S(1)} %collective-permute-done.11.refs_3_), custom_call_target="tpu_custom_call" | custom-call | flops 1000000000 | bytes 1000000 | tf_op jit(solution)/shard_map/pallas_call | solution.py:503
  (4 shorter events, 0.1 us)
Async XLA Ops:
  0.0 7.5 %copy-start = (f32[19,19]{1,0:T(8,128)S(1)}, f32[19,19]{1,0:T(8,128)}, u32[]{:S(2)}) copy-start(f32[19,19]{1,0:T(8,128)} %param.11) | copy-start | bytes 4336
  1.5 6.0 %collective-permute-start = (f32[2,2,40,128]{3,2,1,0:T(8,128)S(1)}, f32[2,2,40,128]{3,2,1,0:T(8,128)S(1)}, u32[]{:S(2)}, u32[]{:S(2)}) collective-permute-start(f32[2,2,40,128]{3,2,1,0:T(8,128)S(1)} %get-tuple-element.30), channel_id=1, source_target_pairs={{0,4},{4,0},{8,12},{12,8},{1,5},{5,1},{9,13},{13,9},{2,6},{6,2},{1... | collective-permute-start | bytes 245768 | tf_op jit(solution)/shard_map/ppermute | solution.py:517
  3.6 8.7 %collective-permute-start.3 = (f32[4,2,40,128]{3,2,1,0:T(8,128)S(1)}, f32[4,2,40,128]{3,2,1,0:T(8,128)S(1)}, u32[]{:S(2)}, u32[]{:S(2)}) collective-permute-start(f32[4,2,40,128]{3,2,1,0:T(8,128)S(1)} %get-tuple-element.34), channel_id=1, source_target_pairs={{0,1},{1,0},{2,3},{3,2},{4,5},{5,4},{6,7},{7,6},{8,9},{9,8},{10,11... | collective-permute-start | bytes 491528 | tf_op jit(solution)/shard_map/ppermute | solution.py:528
  3.7 8.6 %collective-permute-start.4 = (f32[4,2,40,128]{3,2,1,0:T(8,128)S(1)}, f32[4,2,40,128]{3,2,1,0:T(8,128)S(1)}, u32[]{:S(2)}, u32[]{:S(2)}) collective-permute-start(f32[4,2,40,128]{3,2,1,0:T(8,128)S(1)} %get-tuple-element.35), channel_id=1, source_target_pairs={{0,1},{1,0},{2,3},{3,2},{4,5},{5,4},{6,7},{7,6},{8,9},{9,8},{10,11... | collective-permute-start | bytes 491528 | tf_op jit(solution)/shard_map/ppermute | solution.py:528
  5.1 7.2 %collective-permute-start.5 = (f32[4,2,40,128]{3,2,1,0:T(8,128)S(1)}, f32[4,2,40,128]{3,2,1,0:T(8,128)S(1)}, u32[]{:S(2)}, u32[]{:S(2)}) collective-permute-start(f32[4,2,40,128]{3,2,1,0:T(8,128)S(1)} %get-tuple-element.36), channel_id=1, source_target_pairs={{0,1},{1,0},{2,3},{3,2},{4,5},{5,4},{6,7},{7,6},{8,9},{9,8},{10,11... | collective-permute-start | bytes 491528 | tf_op jit(solution)/shard_map/ppermute | solution.py:528
  6.3 5.1 %collective-permute-start.1 = (f32[2,2,40,128]{3,2,1,0:T(8,128)S(1)}, f32[2,2,40,128]{3,2,1,0:T(8,128)S(1)}, u32[]{:S(2)}, u32[]{:S(2)}) collective-permute-start(f32[2,2,40,128]{3,2,1,0:T(8,128)S(1)} %get-tuple-element.31), channel_id=1, source_target_pairs={{0,8},{4,12},{8,0},{12,4},{1,9},{5,13},{9,1},{13,5},{2,10},{6,14},... | collective-permute-start | bytes 245768 | tf_op jit(solution)/shard_map/ppermute | solution.py:517
  7.6 4.8 %collective-permute-start.2 = (f32[2,2,40,128]{3,2,1,0:T(8,128)S(1)}, f32[2,2,40,128]{3,2,1,0:T(8,128)S(1)}, u32[]{:S(2)}, u32[]{:S(2)}) collective-permute-start(f32[2,2,40,128]{3,2,1,0:T(8,128)S(1)} %get-tuple-element.32), channel_id=1, source_target_pairs={{0,12},{4,8},{8,4},{12,0},{1,13},{5,9},{9,5},{13,1},{2,14},{6,10},... | collective-permute-start | bytes 245768 | tf_op jit(solution)/shard_map/ppermute | solution.py:517
  12.3 3.0 %copy-start.1 = (f32[19]{0:T(128)S(1)}, f32[19]{0:T(128)}, u32[]{:S(2)}) copy-start(f32[19]{0:T(128)} %refs_4_.1) | copy-start | bytes 232
  12.4 3.9 %collective-permute-start.6 = (f32[6,8,4,128]{3,2,1,0:T(4,128)S(1)}, f32[6,8,4,128]{3,2,1,0:T(4,128)S(1)}, u32[]{:S(2)}, u32[]{:S(2)}) collective-permute-start(f32[6,8,4,128]{3,2,1,0:T(4,128)S(1)} %shard_map.66), channel_id=1, source_target_pairs={{0,16},{1,2},{2,1},{3,19},{4,20},{5,21},{6,22},{7,23},{8,24},{9,25... | collective-permute-start | bytes 294920 | tf_op jit(solution)/shard_map/ppermute | solution.py:537
  20.5 7.1 %collective-permute-start.7 = (f32[5,8,40,128]{3,2,1,0:T(8,128)S(1)}, f32[5,8,40,128]{3,2,1,0:T(8,128)S(1)}, u32[]{:S(2)}, u32[]{:S(2)}) collective-permute-start(f32[5,8,40,128]{3,2,1,0:T(8,128)S(1)} %get-tuple-element.40.refs_1_), channel_id=1, source_target_pairs={{0,16},{16,0},{1,17},{17,1},{2,18},{18,2},{3,19},{19,3},{4,20},{20... | collective-permute-start | bytes 2457608 | tf_op jit(solution)/shard_map/ppermute | solution.py:540
  20.6 2.6 %collective-permute-start.8 = (f32[8,40,128]{2,1,0:T(8,128)S(1)}, f32[8,40,128]{2,1,0:T(8,128)S(1)}, u32[]{:S(2)}, u32[]{:S(2)}) collective-permute-start(f32[8,40,128]{2,1,0:T(8,128)S(1)} %get-tuple-element.38.refs_12_.refs_0_), channel_id=1, source_target_pairs={{0,16},{16,0},{1,17},{17,1},{2,18},{18,2},{3,19},{19,3},{4,20},{20... | collective-permute-start | bytes 491528 | tf_op jit(solution)/shard_map/ppermute | solution.py:540
  27.7 6.2 %collective-permute-start.9 = (f32[6,2,32,128]{3,2,1,0:T(8,128)S(1)}, f32[6,2,32,128]{3,2,1,0:T(8,128)S(1)}, u32[]{:S(2)}, u32[]{:S(2)}) collective-permute-start(f32[6,2,32,128]{3,2,1,0:T(8,128)S(1)} %get-tuple-element.50), channel_id=1, source_target_pairs={{0,4},{4,0},{8,12},{12,8},{1,5},{5,1},{9,13},{13,9},{2,6},{6,2},{1... | collective-permute-start | bytes 589832 | tf_op jit(solution)/shard_map/ppermute | solution.py:517
  28.2 9.0 %collective-permute-start.10 = (f32[6,2,32,128]{3,2,1,0:T(8,128)S(1)}, f32[6,2,32,128]{3,2,1,0:T(8,128)S(1)}, u32[]{:S(2)}, u32[]{:S(2)}) collective-permute-start(f32[6,2,32,128]{3,2,1,0:T(8,128)S(1)} %get-tuple-element.51), channel_id=1, source_target_pairs={{0,8},{4,12},{8,0},{12,4},{1,9},{5,13},{9,1},{13,5},{2,10},{6,14},... | collective-permute-start | bytes 589832 | tf_op jit(solution)/shard_map/ppermute | solution.py:517
  30.0 7.2 %collective-permute-start.11 = (f32[6,2,32,128]{3,2,1,0:T(8,128)S(1)}, f32[6,2,32,128]{3,2,1,0:T(8,128)S(1)}, u32[]{:S(2)}, u32[]{:S(2)}) collective-permute-start(f32[6,2,32,128]{3,2,1,0:T(8,128)S(1)} %get-tuple-element.52), channel_id=1, source_target_pairs={{0,12},{4,8},{8,4},{12,0},{1,13},{5,9},{9,5},{13,1},{2,14},{6,10},... | collective-permute-start | bytes 589832 | tf_op jit(solution)/shard_map/ppermute | solution.py:517

commit v3 on v2

--- a/solution.py
+++ b/solution.py
@@ -203,38 +203,48 @@
     return i // p.nz, i % p.nz
 
 
-def copy_matrix(p, slot):
-    f0, k0 = lanes_of(p, (LANES, LANES), 0)
-    _, k1 = lanes_of(p, (LANES, LANES), 1)
-    return ((f0 == slot) & (k0 == k1)).astype(F32)
-
-
-def cumsum_matrix(p):
+def spread(p, x, slot):
+    f, _ = lanes_of(p, x.shape, 1)
+    return field_sum(p, jnp.where(f == slot, x, 0.0))
+
+
+def field_sum(p, x):
+    shift = p.nz
+    while shift < LANES:
+        x = x + pltpu.roll(x, shift, 1)
+        shift *= 2
+    return x
+
+
+def level_sum(p, x):
     _, k0 = lanes_of(p, (LANES, LANES), 0)
     _, k1 = lanes_of(p, (LANES, LANES), 1)
-    return (k0 <= k1).astype(F32)
-
-
-def sum_matrix(p):
-    _, k0 = lanes_of(p, (LANES, LANES), 0)
-    _, k1 = lanes_of(p, (LANES, LANES), 1)
-    return (k0 == k1).astype(F32)
+    ones = (k0 <= k1).astype(F32).astype(BF16)
+    hi = x.astype(BF16)
+    rest = x - hi.astype(F32)
+    mid = rest.astype(BF16)
+    lo = (rest - mid.astype(F32)).astype(BF16)
+    return jnp.dot(
+        jnp.concatenate([hi, mid, lo], axis=1),
+        jnp.concatenate([ones] * 3, axis=0),
+        preferred_element_type=F32,
+    )
 
 
 def optical_depth(p, attenuation):
     _, level = lanes_of(p, attenuation.shape, 1)
     plain = (water_extinction * layer_depth) * (level + 1).astype(F32)
-    return layer_depth * dot(attenuation, cumsum_matrix(p)) + plain
+    return layer_depth * level_sum(p, attenuation) + plain
 
 
 def ocean_step(p, d, forcing, wet, out, pp):
-    f0, k0 = lanes_of(p, (LANES, LANES), 0)
-    _, k1 = lanes_of(p, (LANES, LANES), 1)
-    weight = jnp.where(f0 == 2, -0.2, jnp.where(f0 == 3, 0.8, 0.0)) * barotropic_gradient_coefficient
-    press = jnp.where(k0 <= k1, weight, 0.0)
     mid = slice(PAD, PAD + p.width)
+    flat = jnp.concatenate([d[1 + r, mid, :] for r in range(p.R)], axis=0)
+    f, _ = lanes_of(p, flat.shape, 1)
+    weight = jnp.where(f == 2, -0.2, jnp.where(f == 3, 0.8, 0.0)) * barotropic_gradient_coefficient
+    press = level_sum(p, weight * flat)
     for r in range(p.R):
-        pp[1 + r, mid, :] = dot(d[1 + r, mid, :], press)
+        pp[1 + r, mid, :] = press[r * p.width : (r + 1) * p.width]
     f, _ = lanes_of(p, (p.width, LANES), 1)
     for r in range(p.R):
         x = d[1 + r, mid, :]
@@ -263,17 +273,20 @@
         ref[count - 1] = row
 
 
-def tracer_step(p, d, load_group, wet, sw, absorb, r_hi, r_lo, store, scratch):
-    c, feh, fnh, va, ae, le, an, ln, low, rin, rout, adv = scratch
+def tracer_step(p, d, load_group, wet, sw, absorb, mix, store, scratch, lo, count):
+    c, feh, fnh, va, ae, le, an, ln, low, rin, rout, fe, adv = scratch
     R, W = p.R, p.width
     mid = slice(PAD, PAD + W)
     up = slice(PAD + 1, PAD + 1 + W)
     down = slice(PAD - 1, PAD - 1 + W)
-    clear_pads(p, c, va, ae, le, an, ln, rin, rout)
+    win = slice(PAD + lo, PAD + lo + count)
+    clear_pads(p, va)
+    for g in range(p.tg):
+        clear_pads(p, *(x.at[g] for x in (c, ae, le, an, ln, rin, rout)))
 
     flat = jnp.concatenate([d[1 + r, mid, :] for r in range(R)], axis=0)
-    ua = dot(flat, copy_matrix(p, 0))
-    vv = dot(flat, copy_matrix(p, 1))
+    ua = spread(p, flat, 0)
+    vv = spread(p, flat, 1)
     for r in range(R):
         va[1 + r, mid, :] = vv[r * W : (r + 1) * W]
     first = lax.axis_index("tx") * p.cols + p.chunk_of(p.ty()) * p.chunk - HALO
@@ -287,87 +300,107 @@
             feh[r] = jnp.zeros((W, LANES), F32)
         fnh[r] = half * (va[1 + r, mid, :] + va[1 + r, up, :]) * inside
 
-    def group(g):
-        load_group(g, c)
-        for r in range(R):
-            c0 = c[1 + r, mid, :]
-            cn = c[1 + r, up, :]
-            ce = c[2 + r, mid, :]
-            f = feh[r]
-            a = jnp.abs(f) * (ce - c0)
-            ae[1 + r, mid, :] = a
-            le[1 + r, mid, :] = f * (ce + c0) - a
-            f = fnh[r]
-            a = jnp.abs(f) * (cn - c0)
-            an[1 + r, mid, :] = a
-            ln[1 + r, mid, :] = f * (cn + c0) - a
-        for r in range(R):
-            c0 = c[1 + r, mid, :]
-            cn = c[1 + r, up, :]
-            cs = c[1 + r, down, :]
-            ce = c[2 + r, mid, :]
-            cw = c[r, mid, :]
-            lw = c0 - (le[1 + r, mid, :] - le[r, mid, :] + ln[1 + r, mid, :] - ln[1 + r, down, :])
-            low[r] = lw
-            hi = jnp.maximum(jnp.maximum(jnp.maximum(c0, ce), jnp.maximum(cw, cn)), cs)
-            lo = jnp.minimum(jnp.minimum(jnp.minimum(c0, ce), jnp.minimum(cw, cn)), cs)
-            e, w = ae[1 + r, mid, :], ae[r, mid, :]
-            nn, s = an[1 + r, mid, :], an[1 + r, down, :]
-            ep, wp, np_, sp = (jnp.maximum(x, 0.0) for x in (e, w, nn, s))
-            em, wm, nm, sm = (jnp.minimum(x, 0.0) for x in (e, w, nn, s))
-            gain_in = wp - em + sp - nm
-            gain_out = ep - wm + np_ - sm
-            floor = ratio_floor * tracer_interval
-            rin[1 + r, mid, :] = jnp.minimum(gain_in, jnp.maximum(hi - lw, 0.0)) / jnp.maximum(
-                gain_in, floor
-            )
-            rout[1 + r, mid, :] = jnp.minimum(gain_out, jnp.maximum(lw - lo, 0.0)) / jnp.maximum(
-                gain_out, floor
-            )
-        before = jnp.zeros((W, LANES), F32)
-        for r in range(R):
-            ri, ro = rin[1 + r, mid, :], rout[1 + r, mid, :]
-            a = ae[1 + r, mid, :]
-            east = a * jnp.where(
-                a >= 0.0,
-                jnp.minimum(rin[2 + r, mid, :], ro),
-                jnp.minimum(ri, rout[2 + r, mid, :]),
-            )
-            a = an[1 + r, mid, :]
-            north = a * jnp.where(
-                a >= 0.0,
-                jnp.minimum(rin[1 + r, up, :], ro),
-                jnp.minimum(ri, rout[1 + r, up, :]),
-            )
-            ln[1 + r, mid, :] = north
-            adv[g, r] = low[r] - (east - before + north - ln[1 + r, down, :])
-            before = east
-        return 0
-
+    def faces(g, r):
+        c0 = c[g, 1 + r, mid, :]
+        cn = c[g, 1 + r, up, :]
+        ce = c[g, 2 + r, mid, :]
+        f = feh[r]
+        a = jnp.abs(f) * (ce - c0)
+        ae[g, 1 + r, mid, :] = a
+        le[g, 1 + r, mid, :] = f * (ce + c0) - a
+        f = fnh[r]
+        a = jnp.abs(f) * (cn - c0)
+        an[g, 1 + r, mid, :] = a
+        ln[g, 1 + r, mid, :] = f * (cn + c0) - a
+
+    def ratios(g, r):
+        c0 = c[g, 1 + r, mid, :]
+        cn = c[g, 1 + r, up, :]
+        cs = c[g, 1 + r, down, :]
+        ce = c[g, 2 + r, mid, :]
+        cw = c[g, r, mid, :]
+        lw = c0 - (
+            le[g, 1 + r, mid, :] - le[g, r, mid, :] + ln[g, 1 + r, mid, :] - ln[g, 1 + r, down, :]
+        )
+        low[g, r] = lw
+        high = jnp.maximum(jnp.maximum(jnp.maximum(c0, ce), jnp.maximum(cw, cn)), cs)
+        least = jnp.minimum(jnp.minimum(jnp.minimum(c0, ce), jnp.minimum(cw, cn)), cs)
+        e, w = ae[g, 1 + r, mid, :], ae[g, r, mid, :]
+        nn, s = an[g, 1 + r, mid, :], an[g, 1 + r, down, :]
+        ep, wp, np_, sp = (jnp.maximum(x, 0.0) for x in (e, w, nn, s))
+        positive = (ep + wp) + (np_ + sp)
+        gain_in = positive - (e + nn)
+        gain_out = positive - (w + s)
+        floor = ratio_floor * tracer_interval
+        rin[g, 1 + r, mid, :] = jnp.minimum(gain_in, jnp.maximum(high - lw, 0.0)) / jnp.maximum(
+            gain_in, floor
+        )
+        rout[g, 1 + r, mid, :] = jnp.minimum(gain_out, jnp.maximum(lw - least, 0.0)) / jnp.maximum(
+            gain_out, floor
+        )
+
+    def limited(g, r):
+        a = an[g, 1 + r, mid, :]
+        north = a * jnp.where(
+            a >= 0.0,
+            jnp.minimum(rin[g, 1 + r, up, :], rout[g, 1 + r, mid, :]),
+            jnp.minimum(rin[g, 1 + r, mid, :], rout[g, 1 + r, up, :]),
+        )
+        ln[g, 1 + r, mid, :] = north
+        a = ae[g, 1 + r, win, :]
+        east = a * jnp.where(
+            a >= 0.0,
+            jnp.minimum(rin[g, 2 + r, win, :], rout[g, 1 + r, win, :]),
+            jnp.minimum(rin[g, 1 + r, win, :], rout[g, 2 + r, win, :]),
+        )
+        fe[g, r] = east
+        south = ln[g, 1 + r, PAD + lo - 1 : PAD + lo - 1 + count, :]
+        div = east + (ln[g, 1 + r, win, :] - south)
+        if r:
+            div = div - fe[g, r - 1]
+        adv[g, r] = low[g, r, lo : lo + count, :] - div
+
+    def column(r0, r1):
+        shape = ((r1 - r0) * count, LANES)
+        whole = [adv[g, r0:r1].reshape(shape) for g in range(p.tg)]
+        att = whole[0] * absorb[0:1, :]
+        for g in range(1, p.tg):
+            att = att + whole[g] * absorb[g : g + 1, :]
+        light = sw[r0:r1, lo : lo + count, :].reshape(shape) * jnp.exp(-optical_depth(p, att))
+        x = jnp.concatenate([d[1 + r, win, :] for r in range(r0, r1)], axis=0)
+        warm = jnp.exp(0.063 * x) * pltpu.roll(1.0 + 0.2 * jnp.tanh(x), LANES - p.nz, 1)
+        growth = (
+            (growth_peak * tracer_interval) * spread(p, warm, 2) * light / (light + half_light)
+        )
+        every = jnp.concatenate(whole, axis=1)
+        hi = every.astype(BF16)
+        rest = (every - hi.astype(F32)).astype(BF16)
+        mixed = jnp.dot(
+            jnp.concatenate([hi, rest, hi], axis=1), mix[...], preferred_element_type=F32
+        )
+        wets = wet[r0:r1, lo : lo + count, :].reshape(shape)
+        for g in range(p.tg):
+            new = wets * (whole[g] + growth * mixed[:, g * LANES : (g + 1) * LANES])
+            store(g, r0, r1, new.reshape(r1 - r0, count, LANES))
+
+    h = (5 * R) // 8
     for g in range(p.tg):
-        group(g)
-
-    whole = [adv[g].reshape(R * W, LANES) for g in range(p.tg)]
-    att = whole[0] * absorb[0:1, :]
-    for g in range(1, p.tg):
-        att = att + whole[g] * absorb[g : g + 1, :]
-    light = sw[...].reshape(R * W, LANES) * jnp.exp(-optical_depth(p, att))
-    warm = jnp.exp(0.063 * flat) * pltpu.roll(1.0 + 0.2 * jnp.tanh(flat), LANES - p.nz, 1)
-    growth = (
-        (growth_peak * tracer_interval) * dot(warm, copy_matrix(p, 2)) * light / (light + half_light)
-    )
-    every = jnp.concatenate(whole, axis=1)
-    hi = every.astype(BF16)
-    lo = (every - hi.astype(F32)).astype(BF16)
-
-    def mm(a, b):
-        return jnp.dot(a, b, preferred_element_type=F32)
-
-    mixed = mm(hi, r_hi[...]) + mm(lo, r_hi[...]) + mm(hi, r_lo[...])
-    wets = wet[...].reshape(R * W, LANES)
+        load_group(g, c.at[g])
+        for r in range(h + 1):
+            faces(g, r)
+        for r in range(h + 1):
+            ratios(g, r)
+        for r in range(h):
+            limited(g, r)
+    column(0, h)
     for g in range(p.tg):
-        new = wets * (whole[g] + growth * mixed[:, g * LANES : (g + 1) * LANES])
-        store(g, new.reshape(R, W, LANES))
+        for r in range(h + 1, R):
+            faces(g, r)
+        for r in range(h + 1, R):
+            ratios(g, r)
+        for r in range(h, R):
+            limited(g, r)
+    column(h, R)
 
 
 def ocean_first_kernel(p, *refs):
@@ -383,23 +416,27 @@
 
 
 def tracer_first_kernel(p, *refs):
-    src, (z, absorb, r_hi, r_lo, _, c1, wet, sw, d), scratch = refs[: 2 * p.n], refs[2 * p.n : 2 * p.n + 9], refs[2 * p.n + 9 :]
+    src, (z, absorb, mix, _, c1, core, wet, sw, d, spare), scratch = (
+        refs[: 2 * p.n],
+        refs[2 * p.n : 2 * p.n + 10],
+        refs[2 * p.n + 10 :],
+    )
 
     @pl.when(jnp.logical_not(p.is_ocean()))
     def _():
-        c = scratch[0]
         clear_pads(p, d)
-        assemble(p, src, z, p.groups - 1, c)
-        aux_fields(p, c, wet, sw)
+        assemble(p, src, z, p.groups - 1, spare)
+        aux_fields(p, spare, wet, sw)
         assemble(p, src, z, 0, d)
 
         def load(g, dst):
             assemble(p, src, z, g + 1, dst)
 
-        def store(g, value):
-            c1[g] = value
-
-        tracer_step(p, d, load, wet, sw, absorb, r_hi, r_lo, store, scratch)
+        def store(g, r0, r1, value):
+            c1[g, r0:r1] = value
+            core[g, r0:r1] = c1[g, r0:r1, HALO : HALO + p.chunk, :]
+
+        tracer_step(p, d, load, wet, sw, absorb, mix, store, scratch, 0, p.width)
 
 
 def load_dyn(p, dyn, d):
@@ -414,8 +451,8 @@
 
 
 def tracer_second_kernel(p, *refs):
-    dyn, c1, wet, sw, absorb, r_hi, r_lo = refs[:7]
-    outs, (d, c2), scratch = refs[7 : 7 + p.n], refs[7 + p.n : 9 + p.n], refs[9 + p.n :]
+    dyn, c1, wet, sw, absorb, mix = refs[:6]
+    outs, (d, c2), scratch = refs[6 : 6 + p.n], refs[6 + p.n : 8 + p.n], refs[8 + p.n :]
     core = slice(HALO, HALO + p.chunk)
 
     @pl.when(jnp.logical_not(p.is_ocean()))
@@ -426,11 +463,12 @@
             for r in range(p.R):
                 dst[1 + r, PAD : PAD + p.width, :] = c1[g, r]
 
-        def store(g, value):
-            c2[...] = value
-            put_back(p, outs, g + 1, lambda row: c2[pl.ds(row, p.rows), core, :])
-
-        tracer_step(p, d, load, wet, sw, absorb, r_hi, r_lo, store, scratch)
+        def store(g, r0, r1, value):
+            c2[g, r0:r1] = value
+
+        tracer_step(p, d, load, wet, sw, absorb, mix, store, scratch, HALO, p.chunk)
+        for g in range(p.tg):
+            put_back(p, outs, g + 1, lambda row: c2[g, pl.ds(row, p.rows)])
         put_back(p, outs, 0, lambda row: dyn[pl.ds(row, p.rows), core, :])
 
 
@@ -448,18 +486,19 @@
     def _():
         load_dyn(p, dyn, d)
         clear_pads(p, pp)
-        flat = (p.R * p.width, LANES)
+        flat = (p.R * p.chunk, LANES)
         att = c1[0].reshape(flat) * absorb[0:1, :]
         for g in range(1, p.tg):
             att = att + c1[g].reshape(flat) * absorb[g : g + 1, :]
-        below = sw[...].reshape(flat) * jnp.exp(-optical_depth(p, att))
-        kd = dot(att, sum_matrix(p)) + water_extinction
+        below = sw[:, core, :].reshape(flat) * jnp.exp(-optical_depth(p, att))
+        kd = field_sum(p, att) + water_extinction
         above = below * jnp.exp(layer_depth * kd)
-        heat[...] = ((above - below) / layer_depth).reshape(heat.shape)
+        heat[...] = jnp.zeros(heat.shape, F32)
+        heat[:, core, :] = ((above - below) / layer_depth).reshape(p.R, p.chunk, LANES)
         ocean_step(p, d, lambda r: heat[r], wet, dyn2, pp)
         put_back(p, outs, 0, lambda row: dyn2[pl.ds(row, p.rows), core, :])
         for g in range(p.tg):
-            put_back(p, outs, g + 1, lambda row: c1[g, pl.ds(row, p.rows), core, :])
+            put_back(p, outs, g + 1, lambda row: c1[g, pl.ds(row, p.rows)])
 
 
 def unpack_kernel(p, *refs):
@@ -474,20 +513,44 @@
             out[pl.ds(g * step * p.rows + r, count, stride=p.rows), :] = t_ref[...].T[:count]
 
 
-def mix_kernel(p, reaction, r_hi, r_lo):
+def mix_kernel(p, reaction_hbm, absorb_hbm, mix, weights, small, reaction, absorb, sems):
     size = p.tg * LANES
-    spread = (iota((size, LANES), 0) // p.nz == iota((size, LANES), 1)).astype(F32)
-    rows = lax.dot_general(
-        spread, reaction[...], (((1,), (1,)), ((), ())), precision=HIGHEST, preferred_element_type=F32
-    )
-    full = lax.dot_general(
-        rows, spread, (((1,), (1,)), ((), ())), precision=HIGHEST, preferred_element_type=F32
-    )
-    same = iota((size, size), 0) % p.nz == iota((size, size), 1) % p.nz
-    full = jnp.where(same, full, 0.0)
-    hi = full.astype(BF16)
-    r_hi[...] = hi
-    r_lo[...] = (full - hi.astype(F32)).astype(BF16)
+    copies = [
+        pltpu.make_async_copy(reaction_hbm, reaction, sems.at[0]),
+        pltpu.make_async_copy(absorb_hbm, absorb, sems.at[1]),
+    ]
+    for copy in copies:
+        copy.start()
+    for copy in copies:
+        copy.wait()
+    small[...] = jnp.zeros((LANES, LANES), F32)
+    small[: p.nf - DYN, : p.nf - DYN] = reaction[...]
+    hi = small[...].astype(BF16)
+    lo = (small[...] - hi.astype(F32)).astype(BF16)
+    expand = (iota((size, LANES), 0) // p.nz == iota((size, LANES), 1)).astype(F32).astype(BF16)
+    same = (iota((LANES, LANES), 0) % p.nz == iota((LANES, LANES), 1) % p.nz).astype(F32)
+
+    def wide(value):
+        dims = (((1,), (1,)), ((), ()))
+        rows = lax.dot_general(expand, value, dims, preferred_element_type=F32).astype(BF16)
+        return lax.dot_general(rows, expand, dims, preferred_element_type=F32)
+
+    for value, starts in ((hi, (0, size)), (lo, (2 * size,))):
+        full = wide(value)
+        for i in range(p.tg):
+            for j in range(p.tg):
+                at = slice(j * LANES, (j + 1) * LANES)
+                block = (full[i * LANES : (i + 1) * LANES, at] * same).astype(BF16)
+                for start in starts:
+                    mix[start + i * LANES : start + (i + 1) * LANES, at] = block
+    f, _ = lanes_of(p, (1, LANES), 1)
+    for g in range(p.tg):
+        row = jnp.zeros((1, LANES), F32)
+        for k in range(p.per):
+            t = g * p.per + k
+            if t < p.nf - DYN:
+                row = jnp.where(f == k, absorb[t], row)
+        weights[g : g + 1, :] = row
 
 
 def solution(mesh):
@@ -508,9 +571,11 @@
                 scratch_shapes=[pltpu.VMEM(s, F32) if isinstance(s, tuple) else s for s in scratch],
                 input_output_aliases=aliases or {},
                 cost_estimate=pl.CostEstimate(
-                    flops=cost * 10**9, bytes_accessed=cost * 10**6, transcendentals=0
+                    flops=cost * 10**8, bytes_accessed=cost * 10**5, transcendentals=0
                 ),
-                compiler_params=pltpu.CompilerParams(vmem_limit_bytes=20 * 2**20),
+                compiler_params=pltpu.CompilerParams(
+                    vmem_limit_bytes=(20 if cost > 1 else 10) * 2**20,
+                ),
             )(*ins)
 
         def swap(value, mask):
@@ -558,35 +623,48 @@
         got = [packed[0]] + [swap(packed[k], k) for k in range(1, n)]
         got += [packed[n]] + [swap_tracers(packed[n + k], k) for k in range(1, n)]
 
-        react = jnp.pad(reaction, ((0, LANES - reaction.shape[0]), (0, LANES - reaction.shape[1])))
         size = p.tg * LANES
-        r_hi, r_lo = call(mix_kernel, [sds(size, size, dtype=BF16), sds(size, size, dtype=BF16)], [react])
-        weights = jnp.pad(absorb, (0, p.tg * p.per - absorb.shape[0])).reshape(p.tg, p.per)
-        weights = jnp.repeat(weights, p.nz, axis=1)
-
-        z = edges(call(edge_kernel, [sds(G, R, HALO, LANES)], got + [r_hi], in_specs=[VMEM] * (2 * n) + [ANY])[0])
+        mix, weights = call(
+            mix_kernel,
+            [sds(3 * size, size, dtype=BF16), sds(p.tg, LANES)],
+            [pltpu.with_memory_space_constraint(x, pltpu.HBM) for x in (reaction, absorb)],
+            [
+                (LANES, LANES),
+                pltpu.VMEM(reaction.shape, F32),
+                pltpu.SMEM(absorb.shape, F32),
+                pltpu.SemaphoreType.DMA((2,)),
+            ],
+            [HBM] * 2,
+        )
+
+        z = edges(call(edge_kernel, [sds(G, R, HALO, LANES)], got + [mix], in_specs=[VMEM] * (2 * n) + [ANY])[0])
 
         padded = (R + 2, p.padded, LANES)
         block = (R, W, LANES)
-        scratch = [padded, block, block] + [padded] * 5 + [block] + [padded] * 2 + [(p.tg,) + block]
+
+        def work(count):
+            every, cut = (p.tg,) + padded, (p.tg, R, count, LANES)
+            scratch = [every, block, block, padded] + [every] * 4
+            return scratch + [(p.tg,) + block] + [every] * 2 + [cut] * 2
+
         dyn1, wet_o, sw_o = call(ocean_first_kernel, [sds(*block)] * 3, got + [z], [padded] * 3)
 
         dyn1_t = across(dyn1)
-        c1, wet_t, sw_t = call(
+        c1, c1_core, wet_t, sw_t = call(
             tracer_first_kernel,
-            [sds(p.tg, *block), sds(*block), sds(*block)],
-            got + [z, weights, r_hi, r_lo, dyn1],
-            [padded] + scratch,
-            [VMEM] * (2 * n + 4) + [ANY],
+            [sds(p.tg, *block), sds(p.tg, R, p.chunk, LANES), sds(*block), sds(*block)],
+            got + [z, weights, mix, dyn1],
+            [padded, padded] + work(W),
+            [VMEM] * (2 * n + 3) + [ANY],
             cost=4,
         )
-        c1_o = across(c1)
+        c1_o = across(c1_core)
         back = [sds(G, p.rows, p.chunk, LANES)] * n
         outs = call(
             tracer_second_kernel,
             back,
-            [dyn1_t, c1, wet_t, sw_t, weights, r_hi, r_lo],
-            [padded, block] + scratch,
+            [dyn1_t, c1, wet_t, sw_t, weights, mix],
+            [padded, (p.tg, R, p.chunk, LANES)] + work(p.chunk),
             cost=4,
         )
         outs = call(
@@ -596,9 +674,7 @@
             [padded, padded, block, block],
             aliases={5 + k: k for k in range(n)},
         )
-        home = [outs[0]] + [
-            swap(outs[k], k) for k in range(1, n)
-        ]
+        home = [outs[0]] + [swap(outs[k], k) for k in range(1, n)]
         out = call(unpack_kernel, [sds(p.nf * p.nz * p.rows, p.cols)], home, [(LANES, LANES)])[0]
         return out.reshape((1,) + view.shape)
 

time: 38.5 us -> 37.4 us (0.971)
  Pallas kernels: 13.9 us -> 11.9 us
  waiting for transfers between devices: 11.7 us -> 12.8 us
    pallas_call x8, Pallas kernels: 13.9 us -> 11.9 us  [call(): pl.pallas_call(functools.partial(kernel, p), out_shape=outs, in_specs=in_...]
    ppermute x6, waiting for transfers between devices: 8.91 us -> 9.98 us  [swap(): return lax.ppermute(value, 'ty', [(i, i ^ mask) for i in range(n)])]
  transfers between devices with their start and end apart: 12 -> 12, of which waited for: 6 -> 6; matrix products, arithmetic and copies ran while one was open for 1% -> 0% of each run, Pallas kernels for 18% -> 14%
where the time goes in v3:
time: 37.4 us; the launch traced here: 37.2 us
  waiting for transfers between devices  12.8 us (34%)
  starting transfers between devices  12.4 us (33%)
  Pallas kernels  11.9 us (32%)
    pallas_call x8, Pallas kernels, call(): pl.pallas_call(functools.partial(kernel, p), out_shape=outs, in_specs=in_...  11.9 us
    ppermute x6, waiting for transfers between devices, swap(): return lax.ppermute(value, 'ty', [(i, i ^ mask) for i in range(n)])  9.98 us
    ppermute x6, starting transfers between devices, swap(): return lax.ppermute(value, 'ty', [(i, i ^ mask) for i in range(n)])  6.4 us
    ppermute x1, starting transfers between devices, edges(): return lax.ppermute(value, ('grp', 'ty', 'tx'), list(to.items()))  2.83 us
    ppermute x3, starting transfers between devices, swap_tracers(): return lax.ppermute(value, ('grp', 'ty', 'tx'), pairs)  2.65 us
    ppermute x2, waiting for transfers between devices, across(): return lax.ppermute(value, 'grp', [(0, 1), (1, 0)])  1.82 us
    ppermute x1, waiting for transfers between devices, edges(): return lax.ppermute(value, ('grp', 'ty', 'tx'), list(to.items()))  0.94 us
  transfers between devices with their start and end apart: 12, of which 6 were waited for; matrix products, arithmetic and copies ran while one was open for 0% of the time, Pallas kernels for 14%

profile of v3, /device:TPU:1, one launch (start us, length us, event | category | flops | bytes accessed | tf_op | source)
XLA Modules:
  0.0 37.2 jit_solution(8923995128486373312)
XLA Ops:
  0.0 1.5 %shard_map.64 = (f32[2,2,40,128]{3,2,1,0:T(8,128)S(1)}, f32[2,2,40,128]{3,2,1,0:T(8,128)S(1)}, f32[2,2,40,128]{3,2,1,0:T(8,128)S(1)}, f32[2,2,40,128]{3,2,1,0:T(...) custom-call(f32[1472,128]{1,0:T(8,128)} %bitcast.2, ...), custom_call_target="tpu_custom_call" | custom-call | flops 100000000 | bytes 100000 | tf_op jit(solution)/shard_map/pallas_call | solution.py:566
  1.5 2.1 %collective-permute-start = (f32[2,2,40,128]{3,2,1,0:T(8,128)S(1)}, f32[2,2,40,128]{3,2,1,0:T(8,128)S(1)}, u32[]{:S(2)}, u32[]{:S(2)}) collective-permute-start(f32[2,2,40,128]{3,2,1,0:T(8,128)S(1)} %get-tuple-element.31), channel_id=1, source_target_pairs={{0,4},{4,0},{8,12},{12,8},{1,5},{5,1},{9,13},{13,9},{2,6},{6,2},{1... | collective-permute-start | bytes 245768 | tf_op jit(solution)/shard_map/ppermute | solution.py:582
  3.6 0.1 collective-permute-start.3
  3.7 1.4 %collective-permute-start.4 = (f32[4,2,40,128]{3,2,1,0:T(8,128)S(1)}, f32[4,2,40,128]{3,2,1,0:T(8,128)S(1)}, u32[]{:S(2)}, u32[]{:S(2)}) collective-permute-start(f32[4,2,40,128]{3,2,1,0:T(8,128)S(1)} %get-tuple-element.36), channel_id=1, source_target_pairs={{0,1},{1,0},{2,3},{3,2},{4,5},{5,4},{6,7},{7,6},{8,9},{9,8},{10,11... | collective-permute-start | bytes 491528 | tf_op jit(solution)/shard_map/ppermute | solution.py:593
  5.1 1.1 %collective-permute-start.5 = (f32[4,2,40,128]{3,2,1,0:T(8,128)S(1)}, f32[4,2,40,128]{3,2,1,0:T(8,128)S(1)}, u32[]{:S(2)}, u32[]{:S(2)}) collective-permute-start(f32[4,2,40,128]{3,2,1,0:T(8,128)S(1)} %get-tuple-element.37), channel_id=1, source_target_pairs={{0,1},{1,0},{2,3},{3,2},{4,5},{5,4},{6,7},{7,6},{8,9},{9,8},{10,11... | collective-permute-start | bytes 491528 | tf_op jit(solution)/shard_map/ppermute | solution.py:593
  6.3 1.2 %collective-permute-start.1 = (f32[2,2,40,128]{3,2,1,0:T(8,128)S(1)}, f32[2,2,40,128]{3,2,1,0:T(8,128)S(1)}, u32[]{:S(2)}, u32[]{:S(2)}) collective-permute-start(f32[2,2,40,128]{3,2,1,0:T(8,128)S(1)} %get-tuple-element.32), channel_id=1, source_target_pairs={{0,8},{4,12},{8,0},{12,4},{1,9},{5,13},{9,1},{13,5},{2,10},{6,14},... | collective-permute-start | bytes 245768 | tf_op jit(solution)/shard_map/ppermute | solution.py:582
  7.5 0.0 collective-permute-done.refs_1_
  7.5 0.4 collective-permute-start.2
  7.9 1.7 %shard_map.65 = (bf16[1920,640]{1,0:T(8,128)(2,1)S(1)}, f32[5,128]{1,0:T(8,128)S(1)}) custom-call(f32[19,19]{1,0:T(8,128)} %reaction_hbm.1, f32[19]{0:T(128)} %absorb_hbm.1), custom_call_target="tpu_custom_call" | custom-call | flops 100000000 | bytes 100000 | tf_op jit(solution)/shard_map/pallas_call | solution.py:566
  9.6 1.8 %collective-permute-done.1.refs_2_ = f32[2,2,40,128]{3,2,1,0:T(8,128)S(1)} collective-permute-done((f32[2,2,40,128]{3,2,1,0:T(8,128)S(1)}, f32[2,2,40,128]{3,2,1,0:T(8,128)S(1)}, u32[]{:S(2)}, u32[]{:S(2)}) %collective-permute-start.1) | collective-permute-done | bytes 81952 | tf_op jit(solution)/shard_map/ppermute | solution.py:582
  11.4 0.9 %collective-permute-done.2.refs_3_ = f32[2,2,40,128]{3,2,1,0:T(8,128)S(1)} collective-permute-done((f32[2,2,40,128]{3,2,1,0:T(8,128)S(1)}, f32[2,2,40,128]{3,2,1,0:T(8,128)S(1)}, u32[]{:S(2)}, u32[]{:S(2)}) %collective-permute-start.2) | collective-permute-done | bytes 81952 | tf_op jit(solution)/shard_map/ppermute | solution.py:582
  12.3 0.0 collective-permute-done.3.refs_5_
  12.3 0.0 collective-permute-done.4.refs_6_
  12.3 0.0 collective-permute-done.5.refs_7_
  12.4 2.8 %collective-permute-start.6 = (f32[6,8,4,128]{3,2,1,0:T(4,128)S(1)}, f32[6,8,4,128]{3,2,1,0:T(4,128)S(1)}, u32[]{:S(2)}, u32[]{:S(2)}) collective-permute-start(f32[6,8,4,128]{3,2,1,0:T(4,128)S(1)} %shard_map.66), channel_id=1, source_target_pairs={{0,16},{1,2},{2,1},{3,19},{4,20},{5,21},{6,22},{7,23},{8,24},{9,25... | collective-permute-start | bytes 294920 | tf_op jit(solution)/shard_map/ppermute | solution.py:602
  15.2 0.9 %collective-permute-done.6.refs_8_ = f32[6,8,4,128]{3,2,1,0:T(4,128)S(1)} collective-permute-done((f32[6,8,4,128]{3,2,1,0:T(4,128)S(1)}, f32[6,8,4,128]{3,2,1,0:T(4,128)S(1)}, u32[]{:S(2)}, u32[]{:S(2)}) %collective-permute-start.6) | collective-permute-done | bytes 98336 | tf_op jit(solution)/shard_map/ppermute | solution.py:602
  16.1 4.0 %shard_map.68 = (f32[5,8,40,128]{3,2,1,0:T(8,128)S(1)}, f32[5,8,32,128]{3,2,1,0:T(8,128)S(1)}, f32[8,40,128]{2,1,0:T(8,128)S(1)}, f32[8,40,128]{2,1,0:T(8,128)S(1)}) custom-call(f32[2,2,40,128]{3,2,1,0:T(8,128)S(1)} %get-tuple-element.30.refs_0_, f32[2,2,40,128]{3,2,1,0:T(8,128)S(1)} %collective-permute-done.refs_1_, ...), custom_call_target="tpu_custom_call" | custom-call | flops 400000000 | bytes 400000 | tf_op jit(solution)/shard_map/pallas_call | solution.py:566
  20.2 0.1 collective-permute-start.7
  20.2 0.5 %collective-permute-start.8 = (f32[8,40,128]{2,1,0:T(8,128)S(1)}, f32[8,40,128]{2,1,0:T(8,128)S(1)}, u32[]{:S(2)}, u32[]{:S(2)}) collective-permute-start(f32[8,40,128]{2,1,0:T(8,128)S(1)} %get-tuple-element.39.refs_11_.refs_0_), channel_id=1, source_target_pairs={{0,16},{16,0},{1,17},{17,1},{2,18},{18,2},{3,19},{19,3},{4,20},{20... | collective-permute-start | bytes 491528 | tf_op jit(solution)/shard_map/ppermute | solution.py:605
  20.7 1.8 %collective-permute-done.8.refs_0_ = f32[8,40,128]{2,1,0:T(8,128)S(1)} collective-permute-done((f32[8,40,128]{2,1,0:T(8,128)S(1)}, f32[8,40,128]{2,1,0:T(8,128)S(1)}, u32[]{:S(2)}, u32[]{:S(2)}) %collective-permute-start.8) | collective-permute-done | bytes 163872 | tf_op jit(solution)/shard_map/ppermute | solution.py:605
  22.6 3.4 %shard_map.69 = (f32[6,2,32,128]{3,2,1,0:T(8,128)S(1)}, f32[6,2,32,128]{3,2,1,0:T(8,128)S(1)}, f32[6,2,32,128]{3,2,1,0:T(8,128)S(1)}, f32[6,2,32,128]{3,2,1,0:T(8,128)S(1)}) custom-call(f32[8,40,128]{2,1,0:T(8,128)S(1)} %collective-permute-done.8.refs_0_, f32[5,8,40,128]{3,2,1,0:T(8,128)S(1)} %get-tuple-element.44.refs_1_, ...), custom_call_target="tpu_custom_call" | custom-call | flops 400000000 | bytes 400000 | tf_op jit(solution)/shard_map/pallas_call | solution.py:566
  25.9 0.0 collective-permute-done.7.refs_1_
  25.9 0.1 shard_map.70
  26.0 0.3 collective-permute-start.10
  26.3 1.9 %collective-permute-start.11 = (f32[6,2,32,128]{3,2,1,0:T(8,128)S(1)}, f32[6,2,32,128]{3,2,1,0:T(8,128)S(1)}, u32[]{:S(2)}, u32[]{:S(2)}) collective-permute-start(f32[6,2,32,128]{3,2,1,0:T(8,128)S(1)} %get-tuple-element.54), channel_id=1, source_target_pairs={{0,12},{4,8},{8,4},{12,0},{1,13},{5,9},{9,5},{13,1},{2,14},{6,10},... | collective-permute-start | bytes 589832 | tf_op jit(solution)/shard_map/ppermute | solution.py:582
  28.2 0.5 %collective-permute-start.9 = (f32[6,2,32,128]{3,2,1,0:T(8,128)S(1)}, f32[6,2,32,128]{3,2,1,0:T(8,128)S(1)}, u32[]{:S(2)}, u32[]{:S(2)}) collective-permute-start(f32[6,2,32,128]{3,2,1,0:T(8,128)S(1)} %get-tuple-element.52), channel_id=1, source_target_pairs={{0,4},{4,0},{8,12},{12,8},{1,5},{5,1},{9,13},{13,9},{2,6},{6,2},{1... | collective-permute-start | bytes 589832 | tf_op jit(solution)/shard_map/ppermute | solution.py:582
  28.8 5.7 %collective-permute-done.10.refs_2_ = f32[6,2,32,128]{3,2,1,0:T(8,128)S(1)} collective-permute-done((f32[6,2,32,128]{3,2,1,0:T(8,128)S(1)}, f32[6,2,32,128]{3,2,1,0:T(8,128)S(1)}, u32[]{:S(2)}, u32[]{:S(2)}) %collective-permute-start.10) | collective-permute-done | bytes 196640 | tf_op jit(solution)/shard_map/ppermute | solution.py:582
  34.5 0.0 collective-permute-done.11.refs_3_
  34.5 1.5 %collective-permute-done.9.refs_1_ = f32[6,2,32,128]{3,2,1,0:T(8,128)S(1)} collective-permute-done((f32[6,2,32,128]{3,2,1,0:T(8,128)S(1)}, f32[6,2,32,128]{3,2,1,0:T(8,128)S(1)}, u32[]{:S(2)}, u32[]{:S(2)}) %collective-permute-start.9) | collective-permute-done | bytes 196640 | tf_op jit(solution)/shard_map/ppermute | solution.py:582
  36.0 1.2 %shard_map.71 = f32[1472,128]{1,0:T(8,128)} custom-call(f32[6,2,32,128]{3,2,1,0:T(8,128)S(1)} %get-tuple-element.51.refs_0_, f32[6,2,32,128]{3,2,1,0:T(8,128)S(1)} %collective-permute-done.9.refs_1_, f32[6,2,32,128]{3,2,1,0:T(8,128)S(1)} %collective-permute-done.10.refs_2_, f32[6,2,32,128]{3,2,1,0:T(8,128)S(1)} %collective-permute-done.11.refs_3_), custom_call_target="tpu_custom_call" | custom-call | flops 100000000 | bytes 100000 | tf_op jit(solution)/shard_map/pallas_call | solution.py:566
  (2 shorter events, 0.0 us)
Async XLA Ops:
  1.5 6.0 %collective-permute-start = (f32[2,2,40,128]{3,2,1,0:T(8,128)S(1)}, f32[2,2,40,128]{3,2,1,0:T(8,128)S(1)}, u32[]{:S(2)}, u32[]{:S(2)}) collective-permute-start(f32[2,2,40,128]{3,2,1,0:T(8,128)S(1)} %get-tuple-element.31), channel_id=1, source_target_pairs={{0,4},{4,0},{8,12},{12,8},{1,5},{5,1},{9,13},{13,9},{2,6},{6,2},{1... | collective-permute-start | bytes 245768 | tf_op jit(solution)/shard_map/ppermute | solution.py:582
  3.6 8.7 %collective-permute-start.3 = (f32[4,2,40,128]{3,2,1,0:T(8,128)S(1)}, f32[4,2,40,128]{3,2,1,0:T(8,128)S(1)}, u32[]{:S(2)}, u32[]{:S(2)}) collective-permute-start(f32[4,2,40,128]{3,2,1,0:T(8,128)S(1)} %get-tuple-element.35), channel_id=1, source_target_pairs={{0,1},{1,0},{2,3},{3,2},{4,5},{5,4},{6,7},{7,6},{8,9},{9,8},{10,11... | collective-permute-start | bytes 491528 | tf_op jit(solution)/shard_map/ppermute | solution.py:593
  3.7 8.6 %collective-permute-start.4 = (f32[4,2,40,128]{3,2,1,0:T(8,128)S(1)}, f32[4,2,40,128]{3,2,1,0:T(8,128)S(1)}, u32[]{:S(2)}, u32[]{:S(2)}) collective-permute-start(f32[4,2,40,128]{3,2,1,0:T(8,128)S(1)} %get-tuple-element.36), channel_id=1, source_target_pairs={{0,1},{1,0},{2,3},{3,2},{4,5},{5,4},{6,7},{7,6},{8,9},{9,8},{10,11... | collective-permute-start | bytes 491528 | tf_op jit(solution)/shard_map/ppermute | solution.py:593
  5.1 7.2 %collective-permute-start.5 = (f32[4,2,40,128]{3,2,1,0:T(8,128)S(1)}, f32[4,2,40,128]{3,2,1,0:T(8,128)S(1)}, u32[]{:S(2)}, u32[]{:S(2)}) collective-permute-start(f32[4,2,40,128]{3,2,1,0:T(8,128)S(1)} %get-tuple-element.37), channel_id=1, source_target_pairs={{0,1},{1,0},{2,3},{3,2},{4,5},{5,4},{6,7},{7,6},{8,9},{9,8},{10,11... | collective-permute-start | bytes 491528 | tf_op jit(solution)/shard_map/ppermute | solution.py:593
  6.3 5.1 %collective-permute-start.1 = (f32[2,2,40,128]{3,2,1,0:T(8,128)S(1)}, f32[2,2,40,128]{3,2,1,0:T(8,128)S(1)}, u32[]{:S(2)}, u32[]{:S(2)}) collective-permute-start(f32[2,2,40,128]{3,2,1,0:T(8,128)S(1)} %get-tuple-element.32), channel_id=1, source_target_pairs={{0,8},{4,12},{8,0},{12,4},{1,9},{5,13},{9,1},{13,5},{2,10},{6,14},... | collective-permute-start | bytes 245768 | tf_op jit(solution)/shard_map/ppermute | solution.py:582
  7.5 4.8 %collective-permute-start.2 = (f32[2,2,40,128]{3,2,1,0:T(8,128)S(1)}, f32[2,2,40,128]{3,2,1,0:T(8,128)S(1)}, u32[]{:S(2)}, u32[]{:S(2)}) collective-permute-start(f32[2,2,40,128]{3,2,1,0:T(8,128)S(1)} %get-tuple-element.33), channel_id=1, source_target_pairs={{0,12},{4,8},{8,4},{12,0},{1,13},{5,9},{9,5},{13,1},{2,14},{6,10},... | collective-permute-start | bytes 245768 | tf_op jit(solution)/shard_map/ppermute | solution.py:582
  12.4 3.8 %collective-permute-start.6 = (f32[6,8,4,128]{3,2,1,0:T(4,128)S(1)}, f32[6,8,4,128]{3,2,1,0:T(4,128)S(1)}, u32[]{:S(2)}, u32[]{:S(2)}) collective-permute-start(f32[6,8,4,128]{3,2,1,0:T(4,128)S(1)} %shard_map.66), channel_id=1, source_target_pairs={{0,16},{1,2},{2,1},{3,19},{4,20},{5,21},{6,22},{7,23},{8,24},{9,25... | collective-permute-start | bytes 294920 | tf_op jit(solution)/shard_map/ppermute | solution.py:602
  20.2 5.8 %collective-permute-start.7 = (f32[5,8,32,128]{3,2,1,0:T(8,128)S(1)}, f32[5,8,32,128]{3,2,1,0:T(8,128)S(1)}, u32[]{:S(2)}, u32[]{:S(2)}) collective-permute-start(f32[5,8,32,128]{3,2,1,0:T(8,128)S(1)} %get-tuple-element.41), channel_id=1, source_target_pairs={{0,16},{16,0},{1,17},{17,1},{2,18},{18,2},{3,19},{19,3},{4,20},{20... | collective-permute-start | bytes 1966088 | tf_op jit(solution)/shard_map/ppermute | solution.py:605
  20.2 2.3 %collective-permute-start.8 = (f32[8,40,128]{2,1,0:T(8,128)S(1)}, f32[8,40,128]{2,1,0:T(8,128)S(1)}, u32[]{:S(2)}, u32[]{:S(2)}) collective-permute-start(f32[8,40,128]{2,1,0:T(8,128)S(1)} %get-tuple-element.39.refs_11_.refs_0_), channel_id=1, source_target_pairs={{0,16},{16,0},{1,17},{17,1},{2,18},{18,2},{3,19},{19,3},{4,20},{20... | collective-permute-start | bytes 491528 | tf_op jit(solution)/shard_map/ppermute | solution.py:605
  26.0 8.4 %collective-permute-start.10 = (f32[6,2,32,128]{3,2,1,0:T(8,128)S(1)}, f32[6,2,32,128]{3,2,1,0:T(8,128)S(1)}, u32[]{:S(2)}, u32[]{:S(2)}) collective-permute-start(f32[6,2,32,128]{3,2,1,0:T(8,128)S(1)} %get-tuple-element.53), channel_id=1, source_target_pairs={{0,8},{4,12},{8,0},{12,4},{1,9},{5,13},{9,1},{13,5},{2,10},{6,14},... | collective-permute-start | bytes 589832 | tf_op jit(solution)/shard_map/ppermute | solution.py:582
  26.3 8.2 %collective-permute-start.11 = (f32[6,2,32,128]{3,2,1,0:T(8,128)S(1)}, f32[6,2,32,128]{3,2,1,0:T(8,128)S(1)}, u32[]{:S(2)}, u32[]{:S(2)}) collective-permute-start(f32[6,2,32,128]{3,2,1,0:T(8,128)S(1)} %get-tuple-element.54), channel_id=1, source_target_pairs={{0,12},{4,8},{8,4},{12,0},{1,13},{5,9},{9,5},{13,1},{2,14},{6,10},... | collective-permute-start | bytes 589832 | tf_op jit(solution)/shard_map/ppermute | solution.py:582
  28.2 7.8 %collective-permute-start.9 = (f32[6,2,32,128]{3,2,1,0:T(8,128)S(1)}, f32[6,2,32,128]{3,2,1,0:T(8,128)S(1)}, u32[]{:S(2)}, u32[]{:S(2)}) collective-permute-start(f32[6,2,32,128]{3,2,1,0:T(8,128)S(1)} %get-tuple-element.52), channel_id=1, source_target_pairs={{0,4},{4,0},{8,12},{12,8},{1,5},{5,1},{9,13},{13,9},{2,6},{6,2},{1... | collective-permute-start | bytes 589832 | tf_op jit(solution)/shard_map/ppermute | solution.py:582

commit v4 on v3

--- a/solution.py
+++ b/solution.py
@@ -172,22 +172,25 @@
         copy(p.chunk)
 
 
-def assemble(p, src, z, g, dst):
+def assemble(p, src, z, groups):
     for mask in range(p.n):
         base = p.xor(mask) * p.rows
-        for r in range(p.rows):
-            dst[1 + base + r, PAD : PAD + p.width, :] = part(src, mask, g)[r]
+        for g, dst in groups:
+            for r in range(p.rows):
+                dst[1 + base + r, PAD : PAD + p.width, :] = part(src, mask, g)[r]
     chunk, tx = p.chunk_of(p.ty()), lax.axis_index("tx")
 
     @pl.when(chunk == 0)
     def _():
-        dst[1 : 1 + p.R, PAD : PAD + HALO, :] = jnp.where(tx > 0, z[g], 0.0)
+        for g, dst in groups:
+            dst[1 : 1 + p.R, PAD : PAD + HALO, :] = jnp.where(tx > 0, z[g], 0.0)
 
     @pl.when(chunk == p.n - 1)
     def _():
-        dst[1 : 1 + p.R, PAD + p.width - HALO : PAD + p.width, :] = jnp.where(
-            tx < p.m - 1, z[g], 0.0
-        )
+        for g, dst in groups:
+            dst[1 : 1 + p.R, PAD + p.width - HALO : PAD + p.width, :] = jnp.where(
+                tx < p.m - 1, z[g], 0.0
+            )
 
 
 def aux_fields(p, aux_ref, wet_ref, sw_ref):
@@ -280,9 +283,12 @@
     up = slice(PAD + 1, PAD + 1 + W)
     down = slice(PAD - 1, PAD - 1 + W)
     win = slice(PAD + lo, PAD + lo + count)
-    clear_pads(p, va)
+    none = jnp.zeros((W, LANES), F32)
     for g in range(p.tg):
-        clear_pads(p, *(x.at[g] for x in (c, ae, le, an, ln, rin, rout)))
+        for x in (c, ae, le):
+            x[g, 0, mid, :] = none
+        for x in (c, rin, rout):
+            x[g, R + 1, mid, :] = none
 
     flat = jnp.concatenate([d[1 + r, mid, :] for r in range(R)], axis=0)
     ua = spread(p, flat, 0)
@@ -409,28 +415,26 @@
     @pl.when(p.is_ocean())
     def _():
         clear_pads(p, d, aux, pp)
-        assemble(p, src, z, 0, d)
-        assemble(p, src, z, 1, aux)
+        assemble(p, src, z, [(0, d), (1, aux)])
         aux_fields(p, aux, wet, sw)
         ocean_step(p, d, lambda r: aux[1 + r, PAD : PAD + p.width, :], wet, dyn, pp)
 
 
 def tracer_first_kernel(p, *refs):
-    src, (z, absorb, mix, _, c1, core, wet, sw, d, spare), scratch = (
+    src, (z, absorb, mix, _, c1, core, wet, sw, d), scratch = (
         refs[: 2 * p.n],
-        refs[2 * p.n : 2 * p.n + 10],
-        refs[2 * p.n + 10 :],
+        refs[2 * p.n : 2 * p.n + 9],
+        refs[2 * p.n + 9 :],
     )
 
     @pl.when(jnp.logical_not(p.is_ocean()))
     def _():
         clear_pads(p, d)
-        assemble(p, src, z, p.groups - 1, spare)
-        aux_fields(p, spare, wet, sw)
-        assemble(p, src, z, 0, d)
+        assemble(p, src, z, [(0, d)] + [(g + 1, scratch[0].at[g]) for g in range(p.tg)])
+        aux_fields(p, scratch[0].at[p.tg - 1], wet, sw)
 
         def load(g, dst):
-            assemble(p, src, z, g + 1, dst)
+            pass
 
         def store(g, r0, r1, value):
             c1[g, r0:r1] = value
@@ -502,15 +506,23 @@
 
 
 def unpack_kernel(p, *refs):
-    src, out, t_ref = refs[: p.n], refs[p.n], refs[p.n + 1]
+    src, out, t_ref, flat, sems = refs[: p.n], refs[p.n], refs[p.n + 1], refs[p.n + 2], refs[p.n + 3]
     step = p.per * p.nz
+    copies = []
     for g in range(p.groups):
         count = min(step, (p.nf - g * p.per) * p.nz)
         for r in range(p.rows):
             for mask in range(p.n):
                 start = pl.multiple_of(p.chunk_of(p.xor(mask)) * p.chunk, 8)
-                t_ref[pl.ds(start, p.chunk), :] = src[mask][g, r]
-            out[pl.ds(g * step * p.rows + r, count, stride=p.rows), :] = t_ref[...].T[:count]
+                t_ref[g, r, pl.ds(start, p.chunk), :] = src[mask][g, r]
+        for r in range(p.rows):
+            flat[pl.ds(g * step * p.rows + r, count, stride=p.rows), :] = t_ref[g, r].T[:count]
+        at = pl.ds(g * step * p.rows, count * p.rows)
+        copy = pltpu.make_async_copy(flat.at[at], out.at[at], sems.at[g])
+        copy.start()
+        copies.append(copy)
+    for copy in copies:
+        copy.wait()
 
 
 def mix_kernel(p, reaction_hbm, absorb_hbm, mix, weights, small, reaction, absorb, sems):
@@ -562,12 +574,12 @@
         def sds(*shape, dtype=F32):
             return jax.ShapeDtypeStruct(shape, dtype)
 
-        def call(kernel, outs, ins, scratch=(), in_specs=None, aliases=None, cost=1):
+        def call(kernel, outs, ins, scratch=(), in_specs=None, aliases=None, cost=1, out_spec=VMEM):
             return pl.pallas_call(
                 functools.partial(kernel, p),
                 out_shape=outs,
                 in_specs=in_specs or [VMEM] * len(ins),
-                out_specs=jax.tree.map(lambda _: VMEM, outs),
+                out_specs=jax.tree.map(lambda _: out_spec, outs),
                 scratch_shapes=[pltpu.VMEM(s, F32) if isinstance(s, tuple) else s for s in scratch],
                 input_output_aliases=aliases or {},
                 cost_estimate=pl.CostEstimate(
@@ -654,7 +666,7 @@
             tracer_first_kernel,
             [sds(p.tg, *block), sds(p.tg, R, p.chunk, LANES), sds(*block), sds(*block)],
             got + [z, weights, mix, dyn1],
-            [padded, padded] + work(W),
+            [padded] + work(W),
             [VMEM] * (2 * n + 3) + [ANY],
             cost=4,
         )
@@ -675,7 +687,13 @@
             aliases={5 + k: k for k in range(n)},
         )
         home = [outs[0]] + [swap(outs[k], k) for k in range(1, n)]
-        out = call(unpack_kernel, [sds(p.nf * p.nz * p.rows, p.cols)], home, [(LANES, LANES)])[0]
+        out = call(
+            unpack_kernel,
+            [sds(p.nf * p.nz * p.rows, p.cols)],
+            home,
+            [(G, p.rows, LANES, LANES), flat.shape, pltpu.SemaphoreType.DMA((G,))],
+            out_spec=HBM,
+        )[0]
         return out.reshape((1,) + view.shape)
 
     in_specs = (

time: 37.4 us -> 36.9 us (0.987)
  Pallas kernels: 11.9 us -> 11.3 us
    pallas_call x8, Pallas kernels: 11.9 us -> 11.3 us  [call(): pl.pallas_call(functools.partial(kernel, p), out_shape=outs, in_specs=in_...]
where the time goes in v4:
time: 36.9 us; the launch traced here: 36.7 us
  waiting for transfers between devices  12.8 us (35%)
  starting transfers between devices  12.4 us (34%)
  Pallas kernels  11.3 us (31%)
    pallas_call x8, Pallas kernels, call(): pl.pallas_call(functools.partial(kernel, p), out_shape=outs, in_specs=in_...  11.3 us
    ppermute x6, waiting for transfers between devices, swap(): return lax.ppermute(value, 'ty', [(i, i ^ mask) for i in range(n)])  10.1 us
    ppermute x6, starting transfers between devices, swap(): return lax.ppermute(value, 'ty', [(i, i ^ mask) for i in range(n)])  6.4 us
    ppermute x1, starting transfers between devices, edges(): return lax.ppermute(value, ('grp', 'ty', 'tx'), list(to.items()))  2.83 us
    ppermute x3, starting transfers between devices, swap_tracers(): return lax.ppermute(value, ('grp', 'ty', 'tx'), pairs)  2.65 us
    ppermute x2, waiting for transfers between devices, across(): return lax.ppermute(value, 'grp', [(0, 1), (1, 0)])  1.82 us
    ppermute x1, waiting for transfers between devices, edges(): return lax.ppermute(value, ('grp', 'ty', 'tx'), list(to.items()))  0.94 us
  transfers between devices with their start and end apart: 12, of which 6 were waited for; matrix products, arithmetic and copies ran while one was open for 0% of the time, Pallas kernels for 14%

profile of v4, /device:TPU:1, one launch (start us, length us, event | category | flops | bytes accessed | tf_op | source)
XLA Modules:
  0.0 36.7 jit_solution(612560912831225190)
XLA Ops:
  0.0 1.5 %shard_map.64 = (f32[2,2,40,128]{3,2,1,0:T(8,128)S(1)}, f32[2,2,40,128]{3,2,1,0:T(8,128)S(1)}, f32[2,2,40,128]{3,2,1,0:T(8,128)S(1)}, f32[2,2,40,128]{3,2,1,0:T(...) custom-call(f32[1472,128]{1,0:T(8,128)} %bitcast.2, ...), custom_call_target="tpu_custom_call" | custom-call | flops 100000000 | bytes 100000 | tf_op jit(solution)/shard_map/pallas_call | solution.py:578
  1.5 2.1 %collective-permute-start = (f32[2,2,40,128]{3,2,1,0:T(8,128)S(1)}, f32[2,2,40,128]{3,2,1,0:T(8,128)S(1)}, u32[]{:S(2)}, u32[]{:S(2)}) collective-permute-start(f32[2,2,40,128]{3,2,1,0:T(8,128)S(1)} %get-tuple-element.31), channel_id=1, source_target_pairs={{0,4},{4,0},{8,12},{12,8},{1,5},{5,1},{9,13},{13,9},{2,6},{6,2},{1... | collective-permute-start | bytes 245768 | tf_op jit(solution)/shard_map/ppermute | solution.py:594
  3.6 0.1 collective-permute-start.3
  3.7 1.4 %collective-permute-start.4 = (f32[4,2,40,128]{3,2,1,0:T(8,128)S(1)}, f32[4,2,40,128]{3,2,1,0:T(8,128)S(1)}, u32[]{:S(2)}, u32[]{:S(2)}) collective-permute-start(f32[4,2,40,128]{3,2,1,0:T(8,128)S(1)} %get-tuple-element.36), channel_id=1, source_target_pairs={{0,1},{1,0},{2,3},{3,2},{4,5},{5,4},{6,7},{7,6},{8,9},{9,8},{10,11... | collective-permute-start | bytes 491528 | tf_op jit(solution)/shard_map/ppermute | solution.py:605
  5.1 1.1 %collective-permute-start.5 = (f32[4,2,40,128]{3,2,1,0:T(8,128)S(1)}, f32[4,2,40,128]{3,2,1,0:T(8,128)S(1)}, u32[]{:S(2)}, u32[]{:S(2)}) collective-permute-start(f32[4,2,40,128]{3,2,1,0:T(8,128)S(1)} %get-tuple-element.37), channel_id=1, source_target_pairs={{0,1},{1,0},{2,3},{3,2},{4,5},{5,4},{6,7},{7,6},{8,9},{9,8},{10,11... | collective-permute-start | bytes 491528 | tf_op jit(solution)/shard_map/ppermute | solution.py:605
  6.3 1.2 %collective-permute-start.1 = (f32[2,2,40,128]{3,2,1,0:T(8,128)S(1)}, f32[2,2,40,128]{3,2,1,0:T(8,128)S(1)}, u32[]{:S(2)}, u32[]{:S(2)}) collective-permute-start(f32[2,2,40,128]{3,2,1,0:T(8,128)S(1)} %get-tuple-element.32), channel_id=1, source_target_pairs={{0,8},{4,12},{8,0},{12,4},{1,9},{5,13},{9,1},{13,5},{2,10},{6,14},... | collective-permute-start | bytes 245768 | tf_op jit(solution)/shard_map/ppermute | solution.py:594
  7.5 0.0 collective-permute-done.refs_1_
  7.5 0.4 collective-permute-start.2
  7.9 1.7 %shard_map.65 = (bf16[1920,640]{1,0:T(8,128)(2,1)S(1)}, f32[5,128]{1,0:T(8,128)S(1)}) custom-call(f32[19,19]{1,0:T(8,128)} %reaction_hbm.1, f32[19]{0:T(128)} %absorb_hbm.1), custom_call_target="tpu_custom_call" | custom-call | flops 100000000 | bytes 100000 | tf_op jit(solution)/shard_map/pallas_call | solution.py:578
  9.6 1.8 %collective-permute-done.1.refs_2_ = f32[2,2,40,128]{3,2,1,0:T(8,128)S(1)} collective-permute-done((f32[2,2,40,128]{3,2,1,0:T(8,128)S(1)}, f32[2,2,40,128]{3,2,1,0:T(8,128)S(1)}, u32[]{:S(2)}, u32[]{:S(2)}) %collective-permute-start.1) | collective-permute-done | bytes 81952 | tf_op jit(solution)/shard_map/ppermute | solution.py:594
  11.4 0.9 %collective-permute-done.2.refs_3_ = f32[2,2,40,128]{3,2,1,0:T(8,128)S(1)} collective-permute-done((f32[2,2,40,128]{3,2,1,0:T(8,128)S(1)}, f32[2,2,40,128]{3,2,1,0:T(8,128)S(1)}, u32[]{:S(2)}, u32[]{:S(2)}) %collective-permute-start.2) | collective-permute-done | bytes 81952 | tf_op jit(solution)/shard_map/ppermute | solution.py:594
  12.3 0.0 collective-permute-done.3.refs_5_
  12.3 0.0 collective-permute-done.4.refs_6_
  12.3 0.0 collective-permute-done.5.refs_7_
  12.4 2.8 %collective-permute-start.6 = (f32[6,8,4,128]{3,2,1,0:T(4,128)S(1)}, f32[6,8,4,128]{3,2,1,0:T(4,128)S(1)}, u32[]{:S(2)}, u32[]{:S(2)}) collective-permute-start(f32[6,8,4,128]{3,2,1,0:T(4,128)S(1)} %shard_map.66), channel_id=1, source_target_pairs={{0,16},{1,2},{2,1},{3,19},{4,20},{5,21},{6,22},{7,23},{8,24},{9,25... | collective-permute-start | bytes 294920 | tf_op jit(solution)/shard_map/ppermute | solution.py:614
  15.2 0.9 %collective-permute-done.6.refs_8_ = f32[6,8,4,128]{3,2,1,0:T(4,128)S(1)} collective-permute-done((f32[6,8,4,128]{3,2,1,0:T(4,128)S(1)}, f32[6,8,4,128]{3,2,1,0:T(4,128)S(1)}, u32[]{:S(2)}, u32[]{:S(2)}) %collective-permute-start.6) | collective-permute-done | bytes 98336 | tf_op jit(solution)/shard_map/ppermute | solution.py:614
  16.1 3.6 %shard_map.68 = (f32[5,8,40,128]{3,2,1,0:T(8,128)S(1)}, f32[5,8,32,128]{3,2,1,0:T(8,128)S(1)}, f32[8,40,128]{2,1,0:T(8,128)S(1)}, f32[8,40,128]{2,1,0:T(8,128)S(1)}) custom-call(f32[2,2,40,128]{3,2,1,0:T(8,128)S(1)} %get-tuple-element.30.refs_0_, f32[2,2,40,128]{3,2,1,0:T(8,128)S(1)} %collective-permute-done.refs_1_, ...), custom_call_target="tpu_custom_call" | custom-call | flops 400000000 | bytes 400000 | tf_op jit(solution)/shard_map/pallas_call | solution.py:578
  19.8 0.1 collective-permute-start.7
  19.9 0.5 %collective-permute-start.8 = (f32[8,40,128]{2,1,0:T(8,128)S(1)}, f32[8,40,128]{2,1,0:T(8,128)S(1)}, u32[]{:S(2)}, u32[]{:S(2)}) collective-permute-start(f32[8,40,128]{2,1,0:T(8,128)S(1)} %get-tuple-element.39.refs_11_.refs_0_), channel_id=1, source_target_pairs={{0,16},{16,0},{1,17},{17,1},{2,18},{18,2},{3,19},{19,3},{4,20},{20... | collective-permute-start | bytes 491528 | tf_op jit(solution)/shard_map/ppermute | solution.py:617
  20.4 1.8 %collective-permute-done.8.refs_0_ = f32[8,40,128]{2,1,0:T(8,128)S(1)} collective-permute-done((f32[8,40,128]{2,1,0:T(8,128)S(1)}, f32[8,40,128]{2,1,0:T(8,128)S(1)}, u32[]{:S(2)}, u32[]{:S(2)}) %collective-permute-start.8) | collective-permute-done | bytes 163872 | tf_op jit(solution)/shard_map/ppermute | solution.py:617
  22.2 3.3 %shard_map.69 = (f32[6,2,32,128]{3,2,1,0:T(8,128)S(1)}, f32[6,2,32,128]{3,2,1,0:T(8,128)S(1)}, f32[6,2,32,128]{3,2,1,0:T(8,128)S(1)}, f32[6,2,32,128]{3,2,1,0:T(8,128)S(1)}) custom-call(f32[8,40,128]{2,1,0:T(8,128)S(1)} %collective-permute-done.8.refs_0_, f32[5,8,40,128]{3,2,1,0:T(8,128)S(1)} %get-tuple-element.44.refs_1_, ...), custom_call_target="tpu_custom_call" | custom-call | flops 400000000 | bytes 400000 | tf_op jit(solution)/shard_map/pallas_call | solution.py:578
  25.5 0.0 collective-permute-done.7.refs_1_
  25.5 0.1 shard_map.70
  25.6 0.3 collective-permute-start.10
  25.9 1.9 %collective-permute-start.11 = (f32[6,2,32,128]{3,2,1,0:T(8,128)S(1)}, f32[6,2,32,128]{3,2,1,0:T(8,128)S(1)}, u32[]{:S(2)}, u32[]{:S(2)}) collective-permute-start(f32[6,2,32,128]{3,2,1,0:T(8,128)S(1)} %get-tuple-element.54), channel_id=1, source_target_pairs={{0,12},{4,8},{8,4},{12,0},{1,13},{5,9},{9,5},{13,1},{2,14},{6,10},... | collective-permute-start | bytes 589832 | tf_op jit(solution)/shard_map/ppermute | solution.py:594
  27.8 0.5 %collective-permute-start.9 = (f32[6,2,32,128]{3,2,1,0:T(8,128)S(1)}, f32[6,2,32,128]{3,2,1,0:T(8,128)S(1)}, u32[]{:S(2)}, u32[]{:S(2)}) collective-permute-start(f32[6,2,32,128]{3,2,1,0:T(8,128)S(1)} %get-tuple-element.52), channel_id=1, source_target_pairs={{0,4},{4,0},{8,12},{12,8},{1,5},{5,1},{9,13},{13,9},{2,6},{6,2},{1... | collective-permute-start | bytes 589832 | tf_op jit(solution)/shard_map/ppermute | solution.py:594
  28.3 5.8 %collective-permute-done.10.refs_2_ = f32[6,2,32,128]{3,2,1,0:T(8,128)S(1)} collective-permute-done((f32[6,2,32,128]{3,2,1,0:T(8,128)S(1)}, f32[6,2,32,128]{3,2,1,0:T(8,128)S(1)}, u32[]{:S(2)}, u32[]{:S(2)}) %collective-permute-start.10) | collective-permute-done | bytes 196640 | tf_op jit(solution)/shard_map/ppermute | solution.py:594
  34.1 0.0 collective-permute-done.11.refs_3_
  34.1 1.5 %collective-permute-done.9.refs_1_ = f32[6,2,32,128]{3,2,1,0:T(8,128)S(1)} collective-permute-done((f32[6,2,32,128]{3,2,1,0:T(8,128)S(1)}, f32[6,2,32,128]{3,2,1,0:T(8,128)S(1)}, u32[]{:S(2)}, u32[]{:S(2)}) %collective-permute-start.9) | collective-permute-done | bytes 196640 | tf_op jit(solution)/shard_map/ppermute | solution.py:594
  35.6 1.0 %shard_map.71 = f32[1472,128]{1,0:T(8,128)} custom-call(f32[6,2,32,128]{3,2,1,0:T(8,128)S(1)} %get-tuple-element.51.refs_0_, f32[6,2,32,128]{3,2,1,0:T(8,128)S(1)} %collective-permute-done.9.refs_1_, f32[6,2,32,128]{3,2,1,0:T(8,128)S(1)} %collective-permute-done.10.refs_2_, f32[6,2,32,128]{3,2,1,0:T(8,128)S(1)} %collective-permute-done.11.refs_3_), custom_call_target="tpu_custom_call" | custom-call | flops 100000000 | bytes 100000 | tf_op jit(solution)/shard_map/pallas_call | solution.py:578
  (2 shorter events, 0.0 us)
Async XLA Ops:
  1.5 6.0 %collective-permute-start = (f32[2,2,40,128]{3,2,1,0:T(8,128)S(1)}, f32[2,2,40,128]{3,2,1,0:T(8,128)S(1)}, u32[]{:S(2)}, u32[]{:S(2)}) collective-permute-start(f32[2,2,40,128]{3,2,1,0:T(8,128)S(1)} %get-tuple-element.31), channel_id=1, source_target_pairs={{0,4},{4,0},{8,12},{12,8},{1,5},{5,1},{9,13},{13,9},{2,6},{6,2},{1... | collective-permute-start | bytes 245768 | tf_op jit(solution)/shard_map/ppermute | solution.py:594
  3.6 8.7 %collective-permute-start.3 = (f32[4,2,40,128]{3,2,1,0:T(8,128)S(1)}, f32[4,2,40,128]{3,2,1,0:T(8,128)S(1)}, u32[]{:S(2)}, u32[]{:S(2)}) collective-permute-start(f32[4,2,40,128]{3,2,1,0:T(8,128)S(1)} %get-tuple-element.35), channel_id=1, source_target_pairs={{0,1},{1,0},{2,3},{3,2},{4,5},{5,4},{6,7},{7,6},{8,9},{9,8},{10,11... | collective-permute-start | bytes 491528 | tf_op jit(solution)/shard_map/ppermute | solution.py:605
  3.7 8.6 %collective-permute-start.4 = (f32[4,2,40,128]{3,2,1,0:T(8,128)S(1)}, f32[4,2,40,128]{3,2,1,0:T(8,128)S(1)}, u32[]{:S(2)}, u32[]{:S(2)}) collective-permute-start(f32[4,2,40,128]{3,2,1,0:T(8,128)S(1)} %get-tuple-element.36), channel_id=1, source_target_pairs={{0,1},{1,0},{2,3},{3,2},{4,5},{5,4},{6,7},{7,6},{8,9},{9,8},{10,11... | collective-permute-start | bytes 491528 | tf_op jit(solution)/shard_map/ppermute | solution.py:605
  5.1 7.2 %collective-permute-start.5 = (f32[4,2,40,128]{3,2,1,0:T(8,128)S(1)}, f32[4,2,40,128]{3,2,1,0:T(8,128)S(1)}, u32[]{:S(2)}, u32[]{:S(2)}) collective-permute-start(f32[4,2,40,128]{3,2,1,0:T(8,128)S(1)} %get-tuple-element.37), channel_id=1, source_target_pairs={{0,1},{1,0},{2,3},{3,2},{4,5},{5,4},{6,7},{7,6},{8,9},{9,8},{10,11... | collective-permute-start | bytes 491528 | tf_op jit(solution)/shard_map/ppermute | solution.py:605
  6.3 5.1 %collective-permute-start.1 = (f32[2,2,40,128]{3,2,1,0:T(8,128)S(1)}, f32[2,2,40,128]{3,2,1,0:T(8,128)S(1)}, u32[]{:S(2)}, u32[]{:S(2)}) collective-permute-start(f32[2,2,40,128]{3,2,1,0:T(8,128)S(1)} %get-tuple-element.32), channel_id=1, source_target_pairs={{0,8},{4,12},{8,0},{12,4},{1,9},{5,13},{9,1},{13,5},{2,10},{6,14},... | collective-permute-start | bytes 245768 | tf_op jit(solution)/shard_map/ppermute | solution.py:594
  7.5 4.8 %collective-permute-start.2 = (f32[2,2,40,128]{3,2,1,0:T(8,128)S(1)}, f32[2,2,40,128]{3,2,1,0:T(8,128)S(1)}, u32[]{:S(2)}, u32[]{:S(2)}) collective-permute-start(f32[2,2,40,128]{3,2,1,0:T(8,128)S(1)} %get-tuple-element.33), channel_id=1, source_target_pairs={{0,12},{4,8},{8,4},{12,0},{1,13},{5,9},{9,5},{13,1},{2,14},{6,10},... | collective-permute-start | bytes 245768 | tf_op jit(solution)/shard_map/ppermute | solution.py:594
  12.4 3.8 %collective-permute-start.6 = (f32[6,8,4,128]{3,2,1,0:T(4,128)S(1)}, f32[6,8,4,128]{3,2,1,0:T(4,128)S(1)}, u32[]{:S(2)}, u32[]{:S(2)}) collective-permute-start(f32[6,8,4,128]{3,2,1,0:T(4,128)S(1)} %shard_map.66), channel_id=1, source_target_pairs={{0,16},{1,2},{2,1},{3,19},{4,20},{5,21},{6,22},{7,23},{8,24},{9,25... | collective-permute-start | bytes 294920 | tf_op jit(solution)/shard_map/ppermute | solution.py:614
  19.8 5.7 %collective-permute-start.7 = (f32[5,8,32,128]{3,2,1,0:T(8,128)S(1)}, f32[5,8,32,128]{3,2,1,0:T(8,128)S(1)}, u32[]{:S(2)}, u32[]{:S(2)}) collective-permute-start(f32[5,8,32,128]{3,2,1,0:T(8,128)S(1)} %get-tuple-element.41), channel_id=1, source_target_pairs={{0,16},{16,0},{1,17},{17,1},{2,18},{18,2},{3,19},{19,3},{4,20},{20... | collective-permute-start | bytes 1966088 | tf_op jit(solution)/shard_map/ppermute | solution.py:617
  19.9 2.3 %collective-permute-start.8 = (f32[8,40,128]{2,1,0:T(8,128)S(1)}, f32[8,40,128]{2,1,0:T(8,128)S(1)}, u32[]{:S(2)}, u32[]{:S(2)}) collective-permute-start(f32[8,40,128]{2,1,0:T(8,128)S(1)} %get-tuple-element.39.refs_11_.refs_0_), channel_id=1, source_target_pairs={{0,16},{16,0},{1,17},{17,1},{2,18},{18,2},{3,19},{19,3},{4,20},{20... | collective-permute-start | bytes 491528 | tf_op jit(solution)/shard_map/ppermute | solution.py:617
  25.6 8.5 %collective-permute-start.10 = (f32[6,2,32,128]{3,2,1,0:T(8,128)S(1)}, f32[6,2,32,128]{3,2,1,0:T(8,128)S(1)}, u32[]{:S(2)}, u32[]{:S(2)}) collective-permute-start(f32[6,2,32,128]{3,2,1,0:T(8,128)S(1)} %get-tuple-element.53), channel_id=1, source_target_pairs={{0,8},{4,12},{8,0},{12,4},{1,9},{5,13},{9,1},{13,5},{2,10},{6,14},... | collective-permute-start | bytes 589832 | tf_op jit(solution)/shard_map/ppermute | solution.py:594
  25.9 8.2 %collective-permute-start.11 = (f32[6,2,32,128]{3,2,1,0:T(8,128)S(1)}, f32[6,2,32,128]{3,2,1,0:T(8,128)S(1)}, u32[]{:S(2)}, u32[]{:S(2)}) collective-permute-start(f32[6,2,32,128]{3,2,1,0:T(8,128)S(1)} %get-tuple-element.54), channel_id=1, source_target_pairs={{0,12},{4,8},{8,4},{12,0},{1,13},{5,9},{9,5},{13,1},{2,14},{6,10},... | collective-permute-start | bytes 589832 | tf_op jit(solution)/shard_map/ppermute | solution.py:594
  27.8 7.8 %collective-permute-start.9 = (f32[6,2,32,128]{3,2,1,0:T(8,128)S(1)}, f32[6,2,32,128]{3,2,1,0:T(8,128)S(1)}, u32[]{:S(2)}, u32[]{:S(2)}) collective-permute-start(f32[6,2,32,128]{3,2,1,0:T(8,128)S(1)} %get-tuple-element.52), channel_id=1, source_target_pairs={{0,4},{4,0},{8,12},{12,8},{1,5},{5,1},{9,13},{13,9},{2,6},{6,2},{1... | collective-permute-start | bytes 589832 | tf_op jit(solution)/shard_map/ppermute | solution.py:594

commit v5 on v4

--- a/solution.py
+++ b/solution.py
@@ -421,11 +421,15 @@
 
 
 def tracer_first_kernel(p, *refs):
-    src, (z, absorb, mix, _, c1, core, wet, sw, d), scratch = (
+    src, (z, absorb, mix, dyn, c1, first, core, wet, sw, d), scratch = (
         refs[: 2 * p.n],
-        refs[2 * p.n : 2 * p.n + 9],
-        refs[2 * p.n + 9 :],
+        refs[2 * p.n : 2 * p.n + 10],
+        refs[2 * p.n + 10 :],
     )
+
+    @pl.when(p.is_ocean())
+    def _():
+        first[...] = dyn[...]
 
     @pl.when(jnp.logical_not(p.is_ocean()))
     def _():
@@ -438,7 +442,10 @@
 
         def store(g, r0, r1, value):
             c1[g, r0:r1] = value
-            core[g, r0:r1] = c1[g, r0:r1, HALO : HALO + p.chunk, :]
+            if g:
+                core[g - 1, r0:r1] = c1[g, r0:r1, HALO : HALO + p.chunk, :]
+            else:
+                first[r0:r1] = value
 
         tracer_step(p, d, load, wet, sw, absorb, mix, store, scratch, 0, p.width)
 
@@ -477,8 +484,8 @@
 
 
 def ocean_second_kernel(p, *refs):
-    dyn, c1, wet, sw, absorb = refs[:5]
-    same, outs, (d, pp, heat, dyn2) = refs[5 : 5 + p.n], refs[5 + p.n : 5 + 2 * p.n], refs[5 + 2 * p.n :]
+    dyn, first, c1, wet, sw, absorb = refs[:6]
+    same, outs, (d, pp, heat, dyn2) = refs[6 : 6 + p.n], refs[6 + p.n : 6 + 2 * p.n], refs[6 + 2 * p.n :]
     core = slice(HALO, HALO + p.chunk)
 
     @pl.when(jnp.logical_not(p.is_ocean()))
@@ -491,9 +498,9 @@
         load_dyn(p, dyn, d)
         clear_pads(p, pp)
         flat = (p.R * p.chunk, LANES)
-        att = c1[0].reshape(flat) * absorb[0:1, :]
+        att = first[:, core, :].reshape(flat) * absorb[0:1, :]
         for g in range(1, p.tg):
-            att = att + c1[g].reshape(flat) * absorb[g : g + 1, :]
+            att = att + c1[g - 1].reshape(flat) * absorb[g : g + 1, :]
         below = sw[:, core, :].reshape(flat) * jnp.exp(-optical_depth(p, att))
         kd = field_sum(p, att) + water_extinction
         above = below * jnp.exp(layer_depth * kd)
@@ -501,8 +508,9 @@
         heat[:, core, :] = ((above - below) / layer_depth).reshape(p.R, p.chunk, LANES)
         ocean_step(p, d, lambda r: heat[r], wet, dyn2, pp)
         put_back(p, outs, 0, lambda row: dyn2[pl.ds(row, p.rows), core, :])
-        for g in range(p.tg):
-            put_back(p, outs, g + 1, lambda row: c1[g, pl.ds(row, p.rows)])
+        put_back(p, outs, 1, lambda row: first[pl.ds(row, p.rows), core, :])
+        for g in range(1, p.tg):
+            put_back(p, outs, g + 1, lambda row: c1[g - 1, pl.ds(row, p.rows)])
 
 
 def unpack_kernel(p, *refs):
@@ -661,30 +669,36 @@
 
         dyn1, wet_o, sw_o = call(ocean_first_kernel, [sds(*block)] * 3, got + [z], [padded] * 3)
 
-        dyn1_t = across(dyn1)
-        c1, c1_core, wet_t, sw_t = call(
+        c1, first, c1_core, wet_t, sw_t = call(
             tracer_first_kernel,
-            [sds(p.tg, *block), sds(p.tg, R, p.chunk, LANES), sds(*block), sds(*block)],
+            [
+                sds(p.tg, *block),
+                sds(*block),
+                sds(p.tg - 1, R, p.chunk, LANES),
+                sds(*block),
+                sds(*block),
+            ],
             got + [z, weights, mix, dyn1],
             [padded] + work(W),
-            [VMEM] * (2 * n + 3) + [ANY],
+            [VMEM] * (2 * n + 4),
             cost=4,
         )
+        swapped = across(first)
         c1_o = across(c1_core)
         back = [sds(G, p.rows, p.chunk, LANES)] * n
         outs = call(
             tracer_second_kernel,
             back,
-            [dyn1_t, c1, wet_t, sw_t, weights, mix],
+            [swapped, c1, wet_t, sw_t, weights, mix],
             [padded, (p.tg, R, p.chunk, LANES)] + work(p.chunk),
             cost=4,
         )
         outs = call(
             ocean_second_kernel,
             back,
-            [dyn1, c1_o, wet_o, sw_o, weights] + list(outs),
+            [dyn1, swapped, c1_o, wet_o, sw_o, weights] + list(outs),
             [padded, padded, block, block],
-            aliases={5 + k: k for k in range(n)},
+            aliases={6 + k: k for k in range(n)},
         )
         home = [outs[0]] + [swap(outs[k], k) for k in range(1, n)]
         out = call(

time: 36.9 us -> 36.3 us (0.984)
  waiting for transfers between devices: 12.8 us -> 12.3 us
    ppermute x6, waiting for transfers between devices: 10.1 us -> 9.69 us  [swap(): return lax.ppermute(value, 'ty', [(i, i ^ mask) for i in range(n)])]
where the time goes in v5:
time: 36.3 us; the launch traced here: 36.1 us
  starting transfers between devices  12.4 us (34%)
  waiting for transfers between devices  12.3 us (34%)
  Pallas kernels  11.3 us (31%)
    pallas_call x8, Pallas kernels, call(): pl.pallas_call(functools.partial(kernel, p), out_shape=outs, in_specs=in_...  11.3 us
    ppermute x6, waiting for transfers between devices, swap(): return lax.ppermute(value, 'ty', [(i, i ^ mask) for i in range(n)])  9.69 us
    ppermute x6, starting transfers between devices, swap(): return lax.ppermute(value, 'ty', [(i, i ^ mask) for i in range(n)])  6.4 us
    ppermute x1, starting transfers between devices, edges(): return lax.ppermute(value, ('grp', 'ty', 'tx'), list(to.items()))  2.83 us
    ppermute x3, starting transfers between devices, swap_tracers(): return lax.ppermute(value, ('grp', 'ty', 'tx'), pairs)  2.65 us
    ppermute x2, waiting for transfers between devices, across(): return lax.ppermute(value, 'grp', [(0, 1), (1, 0)])  1.64 us
    ppermute x1, waiting for transfers between devices, edges(): return lax.ppermute(value, ('grp', 'ty', 'tx'), list(to.items()))  0.94 us
  transfers between devices with their start and end apart: 12, of which 6 were waited for; matrix products, arithmetic and copies ran while one was open for 0% of the time, Pallas kernels for 14%

profile of v5, /device:TPU:1, one launch (start us, length us, event | category | flops | bytes accessed | tf_op | source)
XLA Modules:
  0.0 36.1 jit_solution(5763525989808266705)
XLA Ops:
  0.0 1.5 %shard_map.64 = (f32[2,2,40,128]{3,2,1,0:T(8,128)S(1)}, f32[2,2,40,128]{3,2,1,0:T(8,128)S(1)}, f32[2,2,40,128]{3,2,1,0:T(8,128)S(1)}, f32[2,2,40,128]{3,2,1,0:T(...) custom-call(f32[1472,128]{1,0:T(8,128)} %bitcast.2, ...), custom_call_target="tpu_custom_call" | custom-call | flops 100000000 | bytes 100000 | tf_op jit(solution)/shard_map/pallas_call | solution.py:586
  1.5 2.1 %collective-permute-start = (f32[2,2,40,128]{3,2,1,0:T(8,128)S(1)}, f32[2,2,40,128]{3,2,1,0:T(8,128)S(1)}, u32[]{:S(2)}, u32[]{:S(2)}) collective-permute-start(f32[2,2,40,128]{3,2,1,0:T(8,128)S(1)} %get-tuple-element.32), channel_id=1, source_target_pairs={{0,4},{4,0},{8,12},{12,8},{1,5},{5,1},{9,13},{13,9},{2,6},{6,2},{1... | collective-permute-start | bytes 245768 | tf_op jit(solution)/shard_map/ppermute | solution.py:602
  3.6 0.1 collective-permute-start.3
  3.7 1.4 %collective-permute-start.4 = (f32[4,2,40,128]{3,2,1,0:T(8,128)S(1)}, f32[4,2,40,128]{3,2,1,0:T(8,128)S(1)}, u32[]{:S(2)}, u32[]{:S(2)}) collective-permute-start(f32[4,2,40,128]{3,2,1,0:T(8,128)S(1)} %get-tuple-element.37), channel_id=1, source_target_pairs={{0,1},{1,0},{2,3},{3,2},{4,5},{5,4},{6,7},{7,6},{8,9},{9,8},{10,11... | collective-permute-start | bytes 491528 | tf_op jit(solution)/shard_map/ppermute | solution.py:613
  5.1 1.1 %collective-permute-start.5 = (f32[4,2,40,128]{3,2,1,0:T(8,128)S(1)}, f32[4,2,40,128]{3,2,1,0:T(8,128)S(1)}, u32[]{:S(2)}, u32[]{:S(2)}) collective-permute-start(f32[4,2,40,128]{3,2,1,0:T(8,128)S(1)} %get-tuple-element.38), channel_id=1, source_target_pairs={{0,1},{1,0},{2,3},{3,2},{4,5},{5,4},{6,7},{7,6},{8,9},{9,8},{10,11... | collective-permute-start | bytes 491528 | tf_op jit(solution)/shard_map/ppermute | solution.py:613
  6.3 1.2 %collective-permute-start.1 = (f32[2,2,40,128]{3,2,1,0:T(8,128)S(1)}, f32[2,2,40,128]{3,2,1,0:T(8,128)S(1)}, u32[]{:S(2)}, u32[]{:S(2)}) collective-permute-start(f32[2,2,40,128]{3,2,1,0:T(8,128)S(1)} %get-tuple-element.33), channel_id=1, source_target_pairs={{0,8},{4,12},{8,0},{12,4},{1,9},{5,13},{9,1},{13,5},{2,10},{6,14},... | collective-permute-start | bytes 245768 | tf_op jit(solution)/shard_map/ppermute | solution.py:602
  7.5 0.0 collective-permute-done.refs_1_
  7.5 0.4 collective-permute-start.2
  7.9 1.7 %shard_map.65 = (bf16[1920,640]{1,0:T(8,128)(2,1)S(1)}, f32[5,128]{1,0:T(8,128)S(1)}) custom-call(f32[19,19]{1,0:T(8,128)} %reaction_hbm.1, f32[19]{0:T(128)} %absorb_hbm.1), custom_call_target="tpu_custom_call" | custom-call | flops 100000000 | bytes 100000 | tf_op jit(solution)/shard_map/pallas_call | solution.py:586
  9.6 1.8 %collective-permute-done.1.refs_2_ = f32[2,2,40,128]{3,2,1,0:T(8,128)S(1)} collective-permute-done((f32[2,2,40,128]{3,2,1,0:T(8,128)S(1)}, f32[2,2,40,128]{3,2,1,0:T(8,128)S(1)}, u32[]{:S(2)}, u32[]{:S(2)}) %collective-permute-start.1) | collective-permute-done | bytes 81952 | tf_op jit(solution)/shard_map/ppermute | solution.py:602
  11.4 0.9 %collective-permute-done.2.refs_3_ = f32[2,2,40,128]{3,2,1,0:T(8,128)S(1)} collective-permute-done((f32[2,2,40,128]{3,2,1,0:T(8,128)S(1)}, f32[2,2,40,128]{3,2,1,0:T(8,128)S(1)}, u32[]{:S(2)}, u32[]{:S(2)}) %collective-permute-start.2) | collective-permute-done | bytes 81952 | tf_op jit(solution)/shard_map/ppermute | solution.py:602
  12.3 0.0 collective-permute-done.3.refs_5_
  12.3 0.0 collective-permute-done.4.refs_6_
  12.3 0.0 collective-permute-done.5.refs_7_
  12.4 2.8 %collective-permute-start.6 = (f32[6,8,4,128]{3,2,1,0:T(4,128)S(1)}, f32[6,8,4,128]{3,2,1,0:T(4,128)S(1)}, u32[]{:S(2)}, u32[]{:S(2)}) collective-permute-start(f32[6,8,4,128]{3,2,1,0:T(4,128)S(1)} %shard_map.66), channel_id=1, source_target_pairs={{0,16},{1,2},{2,1},{3,19},{4,20},{5,21},{6,22},{7,23},{8,24},{9,25... | collective-permute-start | bytes 294920 | tf_op jit(solution)/shard_map/ppermute | solution.py:622
  15.2 0.9 %collective-permute-done.6.refs_8_ = f32[6,8,4,128]{3,2,1,0:T(4,128)S(1)} collective-permute-done((f32[6,8,4,128]{3,2,1,0:T(4,128)S(1)}, f32[6,8,4,128]{3,2,1,0:T(4,128)S(1)}, u32[]{:S(2)}, u32[]{:S(2)}) %collective-permute-start.6) | collective-permute-done | bytes 98336 | tf_op jit(solution)/shard_map/ppermute | solution.py:622
  16.1 3.6 %shard_map.68 = (f32[5,8,40,128]{3,2,1,0:T(8,128)S(1)}, f32[8,40,128]{2,1,0:T(8,128)S(1)}, f32[4,8,32,128]{3,2,1,0:T(8,128)S(1)}, f32[8,40,128]{2,1,0:T(8,128)S(1)}, f32[8,40,128]{2,1,0:T(8,128)S(1)}) custom-call(f32[2,2,40,128]{3,2,1,0:T(8,128)S(1)} %get-tuple-element.31.refs_0_, f32[2,2,40,128]{3,2,1,0:T(8,128)S(1)} %collective-permute-done.refs_1_, ...), custom_call_target="tpu_custom_call" | custom-call | flops 400000000 | bytes 400000 | tf_op jit(solution)/shard_map/pallas_call | solution.py:586
  19.8 0.1 collective-permute-start.8
  19.8 0.5 %collective-permute-start.7 = (f32[8,40,128]{2,1,0:T(8,128)S(1)}, f32[8,40,128]{2,1,0:T(8,128)S(1)}, u32[]{:S(2)}, u32[]{:S(2)}) collective-permute-start(f32[8,40,128]{2,1,0:T(8,128)S(1)} %get-tuple-element.42), channel_id=1, source_target_pairs={{0,16},{16,0},{1,17},{17,1},{2,18},{18,2},{3,19},{19,3},{4,20},{20... | collective-permute-start | bytes 491528 | tf_op jit(solution)/shard_map/ppermute | solution.py:625
  20.3 1.6 %collective-permute-done.7.refs_0_.refs_1_ = f32[8,40,128]{2,1,0:T(8,128)S(1)} collective-permute-done((f32[8,40,128]{2,1,0:T(8,128)S(1)}, f32[8,40,128]{2,1,0:T(8,128)S(1)}, u32[]{:S(2)}, u32[]{:S(2)}) %collective-permute-start.7) | collective-permute-done | bytes 163872 | tf_op jit(solution)/shard_map/ppermute | solution.py:625
  22.0 3.3 %shard_map.69 = (f32[6,2,32,128]{3,2,1,0:T(8,128)S(1)}, f32[6,2,32,128]{3,2,1,0:T(8,128)S(1)}, f32[6,2,32,128]{3,2,1,0:T(8,128)S(1)}, f32[6,2,32,128]{3,2,1,0:T(8,128)S(1)}) custom-call(f32[8,40,128]{2,1,0:T(8,128)S(1)} %collective-permute-done.7.refs_0_.refs_1_, f32[5,8,40,128]{3,2,1,0:T(8,128)S(1)} %get-tuple-element.46.refs_1_, ...), custom_call_target="tpu_custom_call" | custom-call | flops 400000000 | bytes 400000 | tf_op jit(solution)/shard_map/pallas_call | solution.py:586
  25.3 0.0 collective-permute-done.8.refs_2_
  25.3 0.1 shard_map.70
  25.4 0.6 %collective-permute-start.9 = (f32[6,2,32,128]{3,2,1,0:T(8,128)S(1)}, f32[6,2,32,128]{3,2,1,0:T(8,128)S(1)}, u32[]{:S(2)}, u32[]{:S(2)}) collective-permute-start(f32[6,2,32,128]{3,2,1,0:T(8,128)S(1)} %get-tuple-element.54), channel_id=1, source_target_pairs={{0,4},{4,0},{8,12},{12,8},{1,5},{5,1},{9,13},{13,9},{2,6},{6,2},{1... | collective-permute-start | bytes 589832 | tf_op jit(solution)/shard_map/ppermute | solution.py:602
  26.0 1.8 %collective-permute-start.10 = (f32[6,2,32,128]{3,2,1,0:T(8,128)S(1)}, f32[6,2,32,128]{3,2,1,0:T(8,128)S(1)}, u32[]{:S(2)}, u32[]{:S(2)}) collective-permute-start(f32[6,2,32,128]{3,2,1,0:T(8,128)S(1)} %get-tuple-element.55), channel_id=1, source_target_pairs={{0,8},{4,12},{8,0},{12,4},{1,9},{5,13},{9,1},{13,5},{2,10},{6,14},... | collective-permute-start | bytes 589832 | tf_op jit(solution)/shard_map/ppermute | solution.py:602
  27.8 0.3 collective-permute-start.11
  28.1 4.2 %collective-permute-done.9.refs_1_ = f32[6,2,32,128]{3,2,1,0:T(8,128)S(1)} collective-permute-done((f32[6,2,32,128]{3,2,1,0:T(8,128)S(1)}, f32[6,2,32,128]{3,2,1,0:T(8,128)S(1)}, u32[]{:S(2)}, u32[]{:S(2)}) %collective-permute-start.9) | collective-permute-done | bytes 196640 | tf_op jit(solution)/shard_map/ppermute | solution.py:602
  32.3 2.7 %collective-permute-done.10.refs_2_ = f32[6,2,32,128]{3,2,1,0:T(8,128)S(1)} collective-permute-done((f32[6,2,32,128]{3,2,1,0:T(8,128)S(1)}, f32[6,2,32,128]{3,2,1,0:T(8,128)S(1)}, u32[]{:S(2)}, u32[]{:S(2)}) %collective-permute-start.10) | collective-permute-done | bytes 196640 | tf_op jit(solution)/shard_map/ppermute | solution.py:602
  35.1 0.0 collective-permute-done.11.refs_3_
  35.1 1.0 %shard_map.71 = f32[1472,128]{1,0:T(8,128)} custom-call(f32[6,2,32,128]{3,2,1,0:T(8,128)S(1)} %get-tuple-element.53.refs_0_, f32[6,2,32,128]{3,2,1,0:T(8,128)S(1)} %collective-permute-done.9.refs_1_, f32[6,2,32,128]{3,2,1,0:T(8,128)S(1)} %collective-permute-done.10.refs_2_, f32[6,2,32,128]{3,2,1,0:T(8,128)S(1)} %collective-permute-done.11.refs_3_), custom_call_target="tpu_custom_call" | custom-call | flops 100000000 | bytes 100000 | tf_op jit(solution)/shard_map/pallas_call | solution.py:586
  (2 shorter events, 0.0 us)
Async XLA Ops:
  1.5 6.0 %collective-permute-start = (f32[2,2,40,128]{3,2,1,0:T(8,128)S(1)}, f32[2,2,40,128]{3,2,1,0:T(8,128)S(1)}, u32[]{:S(2)}, u32[]{:S(2)}) collective-permute-start(f32[2,2,40,128]{3,2,1,0:T(8,128)S(1)} %get-tuple-element.32), channel_id=1, source_target_pairs={{0,4},{4,0},{8,12},{12,8},{1,5},{5,1},{9,13},{13,9},{2,6},{6,2},{1... | collective-permute-start | bytes 245768 | tf_op jit(solution)/shard_map/ppermute | solution.py:602
  3.6 8.7 %collective-permute-start.3 = (f32[4,2,40,128]{3,2,1,0:T(8,128)S(1)}, f32[4,2,40,128]{3,2,1,0:T(8,128)S(1)}, u32[]{:S(2)}, u32[]{:S(2)}) collective-permute-start(f32[4,2,40,128]{3,2,1,0:T(8,128)S(1)} %get-tuple-element.36), channel_id=1, source_target_pairs={{0,1},{1,0},{2,3},{3,2},{4,5},{5,4},{6,7},{7,6},{8,9},{9,8},{10,11... | collective-permute-start | bytes 491528 | tf_op jit(solution)/shard_map/ppermute | solution.py:613
  3.7 8.6 %collective-permute-start.4 = (f32[4,2,40,128]{3,2,1,0:T(8,128)S(1)}, f32[4,2,40,128]{3,2,1,0:T(8,128)S(1)}, u32[]{:S(2)}, u32[]{:S(2)}) collective-permute-start(f32[4,2,40,128]{3,2,1,0:T(8,128)S(1)} %get-tuple-element.37), channel_id=1, source_target_pairs={{0,1},{1,0},{2,3},{3,2},{4,5},{5,4},{6,7},{7,6},{8,9},{9,8},{10,11... | collective-permute-start | bytes 491528 | tf_op jit(solution)/shard_map/ppermute | solution.py:613
  5.1 7.2 %collective-permute-start.5 = (f32[4,2,40,128]{3,2,1,0:T(8,128)S(1)}, f32[4,2,40,128]{3,2,1,0:T(8,128)S(1)}, u32[]{:S(2)}, u32[]{:S(2)}) collective-permute-start(f32[4,2,40,128]{3,2,1,0:T(8,128)S(1)} %get-tuple-element.38), channel_id=1, source_target_pairs={{0,1},{1,0},{2,3},{3,2},{4,5},{5,4},{6,7},{7,6},{8,9},{9,8},{10,11... | collective-permute-start | bytes 491528 | tf_op jit(solution)/shard_map/ppermute | solution.py:613
  6.3 5.1 %collective-permute-start.1 = (f32[2,2,40,128]{3,2,1,0:T(8,128)S(1)}, f32[2,2,40,128]{3,2,1,0:T(8,128)S(1)}, u32[]{:S(2)}, u32[]{:S(2)}) collective-permute-start(f32[2,2,40,128]{3,2,1,0:T(8,128)S(1)} %get-tuple-element.33), channel_id=1, source_target_pairs={{0,8},{4,12},{8,0},{12,4},{1,9},{5,13},{9,1},{13,5},{2,10},{6,14},... | collective-permute-start | bytes 245768 | tf_op jit(solution)/shard_map/ppermute | solution.py:602
  7.5 4.8 %collective-permute-start.2 = (f32[2,2,40,128]{3,2,1,0:T(8,128)S(1)}, f32[2,2,40,128]{3,2,1,0:T(8,128)S(1)}, u32[]{:S(2)}, u32[]{:S(2)}) collective-permute-start(f32[2,2,40,128]{3,2,1,0:T(8,128)S(1)} %get-tuple-element.34), channel_id=1, source_target_pairs={{0,12},{4,8},{8,4},{12,0},{1,13},{5,9},{9,5},{13,1},{2,14},{6,10},... | collective-permute-start | bytes 245768 | tf_op jit(solution)/shard_map/ppermute | solution.py:602
  12.4 3.8 %collective-permute-start.6 = (f32[6,8,4,128]{3,2,1,0:T(4,128)S(1)}, f32[6,8,4,128]{3,2,1,0:T(4,128)S(1)}, u32[]{:S(2)}, u32[]{:S(2)}) collective-permute-start(f32[6,8,4,128]{3,2,1,0:T(4,128)S(1)} %shard_map.66), channel_id=1, source_target_pairs={{0,16},{1,2},{2,1},{3,19},{4,20},{5,21},{6,22},{7,23},{8,24},{9,25... | collective-permute-start | bytes 294920 | tf_op jit(solution)/shard_map/ppermute | solution.py:622
  19.8 5.5 %collective-permute-start.8 = (f32[4,8,32,128]{3,2,1,0:T(8,128)S(1)}, f32[4,8,32,128]{3,2,1,0:T(8,128)S(1)}, u32[]{:S(2)}, u32[]{:S(2)}) collective-permute-start(f32[4,8,32,128]{3,2,1,0:T(8,128)S(1)} %get-tuple-element.43), channel_id=1, source_target_pairs={{0,16},{16,0},{1,17},{17,1},{2,18},{18,2},{3,19},{19,3},{4,20},{20... | collective-permute-start | bytes 1572872 | tf_op jit(solution)/shard_map/ppermute | solution.py:625
  19.8 2.1 %collective-permute-start.7 = (f32[8,40,128]{2,1,0:T(8,128)S(1)}, f32[8,40,128]{2,1,0:T(8,128)S(1)}, u32[]{:S(2)}, u32[]{:S(2)}) collective-permute-start(f32[8,40,128]{2,1,0:T(8,128)S(1)} %get-tuple-element.42), channel_id=1, source_target_pairs={{0,16},{16,0},{1,17},{17,1},{2,18},{18,2},{3,19},{19,3},{4,20},{20... | collective-permute-start | bytes 491528 | tf_op jit(solution)/shard_map/ppermute | solution.py:625
  25.4 6.9 %collective-permute-start.9 = (f32[6,2,32,128]{3,2,1,0:T(8,128)S(1)}, f32[6,2,32,128]{3,2,1,0:T(8,128)S(1)}, u32[]{:S(2)}, u32[]{:S(2)}) collective-permute-start(f32[6,2,32,128]{3,2,1,0:T(8,128)S(1)} %get-tuple-element.54), channel_id=1, source_target_pairs={{0,4},{4,0},{8,12},{12,8},{1,5},{5,1},{9,13},{13,9},{2,6},{6,2},{1... | collective-permute-start | bytes 589832 | tf_op jit(solution)/shard_map/ppermute | solution.py:602
  26.0 9.1 %collective-permute-start.10 = (f32[6,2,32,128]{3,2,1,0:T(8,128)S(1)}, f32[6,2,32,128]{3,2,1,0:T(8,128)S(1)}, u32[]{:S(2)}, u32[]{:S(2)}) collective-permute-start(f32[6,2,32,128]{3,2,1,0:T(8,128)S(1)} %get-tuple-element.55), channel_id=1, source_target_pairs={{0,8},{4,12},{8,0},{12,4},{1,9},{5,13},{9,1},{13,5},{2,10},{6,14},... | collective-permute-start | bytes 589832 | tf_op jit(solution)/shard_map/ppermute | solution.py:602
  27.8 7.3 %collective-permute-start.11 = (f32[6,2,32,128]{3,2,1,0:T(8,128)S(1)}, f32[6,2,32,128]{3,2,1,0:T(8,128)S(1)}, u32[]{:S(2)}, u32[]{:S(2)}) collective-permute-start(f32[6,2,32,128]{3,2,1,0:T(8,128)S(1)} %get-tuple-element.56), channel_id=1, source_target_pairs={{0,12},{4,8},{8,4},{12,0},{1,13},{5,9},{9,5},{13,1},{2,14},{6,10},... | collective-permute-start | bytes 589832 | tf_op jit(solution)/shard_map/ppermute | solution.py:602

commit v6 on v5

--- a/solution.py
+++ b/solution.py
@@ -389,7 +389,7 @@
             new = wets * (whole[g] + growth * mixed[:, g * LANES : (g + 1) * LANES])
             store(g, r0, r1, new.reshape(r1 - r0, count, LANES))
 
-    h = (5 * R) // 8
+    h = R // 2
     for g in range(p.tg):
         load_group(g, c.at[g])
         for r in range(h + 1):
@@ -410,7 +410,7 @@
 
 
 def ocean_first_kernel(p, *refs):
-    src, z, dyn, wet, sw, d, aux, pp = (refs[: 2 * p.n],) + refs[2 * p.n :]
+    src, z, dyn, ahead, wet, sw, d, aux, pp = (refs[: 2 * p.n],) + refs[2 * p.n :]
 
     @pl.when(p.is_ocean())
     def _():
@@ -418,6 +418,8 @@
         assemble(p, src, z, [(0, d), (1, aux)])
         aux_fields(p, aux, wet, sw)
         ocean_step(p, d, lambda r: aux[1 + r, PAD : PAD + p.width, :], wet, dyn, pp)
+        load_dyn(p, dyn, d)
+        ocean_step(p, d, lambda r: jnp.zeros((p.width, LANES), F32), wet, ahead, pp)
 
 
 def tracer_first_kernel(p, *refs):
@@ -484,8 +486,8 @@
 
 
 def ocean_second_kernel(p, *refs):
-    dyn, first, c1, wet, sw, absorb = refs[:6]
-    same, outs, (d, pp, heat, dyn2) = refs[6 : 6 + p.n], refs[6 + p.n : 6 + 2 * p.n], refs[6 + 2 * p.n :]
+    ahead, first, c1, wet, sw, absorb = refs[:6]
+    same, outs, (dyn2,) = refs[6 : 6 + p.n], refs[6 + p.n : 6 + 2 * p.n], refs[6 + 2 * p.n :]
     core = slice(HALO, HALO + p.chunk)
 
     @pl.when(jnp.logical_not(p.is_ocean()))
@@ -495,8 +497,6 @@
 
     @pl.when(p.is_ocean())
     def _():
-        load_dyn(p, dyn, d)
-        clear_pads(p, pp)
         flat = (p.R * p.chunk, LANES)
         att = first[:, core, :].reshape(flat) * absorb[0:1, :]
         for g in range(1, p.tg):
@@ -504,10 +504,11 @@
         below = sw[:, core, :].reshape(flat) * jnp.exp(-optical_depth(p, att))
         kd = field_sum(p, att) + water_extinction
         above = below * jnp.exp(layer_depth * kd)
-        heat[...] = jnp.zeros(heat.shape, F32)
-        heat[:, core, :] = ((above - below) / layer_depth).reshape(p.R, p.chunk, LANES)
-        ocean_step(p, d, lambda r: heat[r], wet, dyn2, pp)
-        put_back(p, outs, 0, lambda row: dyn2[pl.ds(row, p.rows), core, :])
+        f, _ = lanes_of(p, flat, 1)
+        warming = jnp.where(f == 2, (integration_interval / layer_depth) * (above - below), 0.0)
+        wets = wet[:, core, :].reshape(flat)
+        dyn2[...] = (ahead[:, core, :].reshape(flat) + wets * warming).reshape(dyn2.shape)
+        put_back(p, outs, 0, lambda row: dyn2[pl.ds(row, p.rows)])
         put_back(p, outs, 1, lambda row: first[pl.ds(row, p.rows), core, :])
         for g in range(1, p.tg):
             put_back(p, outs, g + 1, lambda row: c1[g - 1, pl.ds(row, p.rows)])
@@ -667,7 +668,9 @@
             scratch = [every, block, block, padded] + [every] * 4
             return scratch + [(p.tg,) + block] + [every] * 2 + [cut] * 2
 
-        dyn1, wet_o, sw_o = call(ocean_first_kernel, [sds(*block)] * 3, got + [z], [padded] * 3)
+        dyn1, ahead, wet_o, sw_o = call(
+            ocean_first_kernel, [sds(*block)] * 4, got + [z], [padded] * 3
+        )
 
         c1, first, c1_core, wet_t, sw_t = call(
             tracer_first_kernel,
@@ -696,8 +699,8 @@
         outs = call(
             ocean_second_kernel,
             back,
-            [dyn1, swapped, c1_o, wet_o, sw_o, weights] + list(outs),
-            [padded, padded, block, block],
+            [ahead, swapped, c1_o, wet_o, sw_o, weights] + list(outs),
+            [(R, p.chunk, LANES)],
             aliases={6 + k: k for k in range(n)},
         )
         home = [outs[0]] + [swap(outs[k], k) for k in range(1, n)]

time: 36.3 us -> 36.4 us (level)
  no operation moved by 1% of the time
where the time goes in v6:
time: 36.4 us; the launch traced here: 36.2 us
  starting transfers between devices  12.4 us (34%)
  waiting for transfers between devices  12.3 us (34%)
  Pallas kernels  11.4 us (31%)
    pallas_call x8, Pallas kernels, call(): pl.pallas_call(functools.partial(kernel, p), out_shape=outs, in_specs=in_...  11.4 us
    ppermute x6, waiting for transfers between devices, swap(): return lax.ppermute(value, 'ty', [(i, i ^ mask) for i in range(n)])  9.69 us
    ppermute x6, starting transfers between devices, swap(): return lax.ppermute(value, 'ty', [(i, i ^ mask) for i in range(n)])  6.4 us
    ppermute x1, starting transfers between devices, edges(): return lax.ppermute(value, ('grp', 'ty', 'tx'), list(to.items()))  2.83 us
    ppermute x3, starting transfers between devices, swap_tracers(): return lax.ppermute(value, ('grp', 'ty', 'tx'), pairs)  2.65 us
    ppermute x2, waiting for transfers between devices, across(): return lax.ppermute(value, 'grp', [(0, 1), (1, 0)])  1.64 us
    ppermute x1, waiting for transfers between devices, edges(): return lax.ppermute(value, ('grp', 'ty', 'tx'), list(to.items()))  0.94 us
  transfers between devices with their start and end apart: 12, of which 6 were waited for; matrix products, arithmetic and copies ran while one was open for 0% of the time, Pallas kernels for 14%

profile of v6, /device:TPU:1, one launch (start us, length us, event | category | flops | bytes accessed | tf_op | source)
XLA Modules:
  0.0 36.2 jit_solution(5472697129184451189)
XLA Ops:
  0.0 1.5 %shard_map.64 = (f32[2,2,40,128]{3,2,1,0:T(8,128)S(1)}, f32[2,2,40,128]{3,2,1,0:T(8,128)S(1)}, f32[2,2,40,128]{3,2,1,0:T(8,128)S(1)}, f32[2,2,40,128]{3,2,1,0:T(...) custom-call(f32[1472,128]{1,0:T(8,128)} %bitcast.2, ...), custom_call_target="tpu_custom_call" | custom-call | flops 100000000 | bytes 100000 | tf_op jit(solution)/shard_map/pallas_call | solution.py:587
  1.5 2.1 %collective-permute-start = (f32[2,2,40,128]{3,2,1,0:T(8,128)S(1)}, f32[2,2,40,128]{3,2,1,0:T(8,128)S(1)}, u32[]{:S(2)}, u32[]{:S(2)}) collective-permute-start(f32[2,2,40,128]{3,2,1,0:T(8,128)S(1)} %get-tuple-element.33), channel_id=1, source_target_pairs={{0,4},{4,0},{8,12},{12,8},{1,5},{5,1},{9,13},{13,9},{2,6},{6,2},{1... | collective-permute-start | bytes 245768 | tf_op jit(solution)/shard_map/ppermute | solution.py:603
  3.6 0.1 collective-permute-start.3
  3.7 1.4 %collective-permute-start.4 = (f32[4,2,40,128]{3,2,1,0:T(8,128)S(1)}, f32[4,2,40,128]{3,2,1,0:T(8,128)S(1)}, u32[]{:S(2)}, u32[]{:S(2)}) collective-permute-start(f32[4,2,40,128]{3,2,1,0:T(8,128)S(1)} %get-tuple-element.38), channel_id=1, source_target_pairs={{0,1},{1,0},{2,3},{3,2},{4,5},{5,4},{6,7},{7,6},{8,9},{9,8},{10,11... | collective-permute-start | bytes 491528 | tf_op jit(solution)/shard_map/ppermute | solution.py:614
  5.1 1.1 %collective-permute-start.5 = (f32[4,2,40,128]{3,2,1,0:T(8,128)S(1)}, f32[4,2,40,128]{3,2,1,0:T(8,128)S(1)}, u32[]{:S(2)}, u32[]{:S(2)}) collective-permute-start(f32[4,2,40,128]{3,2,1,0:T(8,128)S(1)} %get-tuple-element.39), channel_id=1, source_target_pairs={{0,1},{1,0},{2,3},{3,2},{4,5},{5,4},{6,7},{7,6},{8,9},{9,8},{10,11... | collective-permute-start | bytes 491528 | tf_op jit(solution)/shard_map/ppermute | solution.py:614
  6.3 1.2 %collective-permute-start.1 = (f32[2,2,40,128]{3,2,1,0:T(8,128)S(1)}, f32[2,2,40,128]{3,2,1,0:T(8,128)S(1)}, u32[]{:S(2)}, u32[]{:S(2)}) collective-permute-start(f32[2,2,40,128]{3,2,1,0:T(8,128)S(1)} %get-tuple-element.34), channel_id=1, source_target_pairs={{0,8},{4,12},{8,0},{12,4},{1,9},{5,13},{9,1},{13,5},{2,10},{6,14},... | collective-permute-start | bytes 245768 | tf_op jit(solution)/shard_map/ppermute | solution.py:603
  7.5 0.0 collective-permute-done.refs_1_
  7.5 0.4 collective-permute-start.2
  7.9 1.7 %shard_map.65 = (bf16[1920,640]{1,0:T(8,128)(2,1)S(1)}, f32[5,128]{1,0:T(8,128)S(1)}) custom-call(f32[19,19]{1,0:T(8,128)} %reaction_hbm.1, f32[19]{0:T(128)} %absorb_hbm.1), custom_call_target="tpu_custom_call" | custom-call | flops 100000000 | bytes 100000 | tf_op jit(solution)/shard_map/pallas_call | solution.py:587
  9.6 1.8 %collective-permute-done.1.refs_2_ = f32[2,2,40,128]{3,2,1,0:T(8,128)S(1)} collective-permute-done((f32[2,2,40,128]{3,2,1,0:T(8,128)S(1)}, f32[2,2,40,128]{3,2,1,0:T(8,128)S(1)}, u32[]{:S(2)}, u32[]{:S(2)}) %collective-permute-start.1) | collective-permute-done | bytes 81952 | tf_op jit(solution)/shard_map/ppermute | solution.py:603
  11.4 0.9 %collective-permute-done.2.refs_3_ = f32[2,2,40,128]{3,2,1,0:T(8,128)S(1)} collective-permute-done((f32[2,2,40,128]{3,2,1,0:T(8,128)S(1)}, f32[2,2,40,128]{3,2,1,0:T(8,128)S(1)}, u32[]{:S(2)}, u32[]{:S(2)}) %collective-permute-start.2) | collective-permute-done | bytes 81952 | tf_op jit(solution)/shard_map/ppermute | solution.py:603
  12.3 0.0 collective-permute-done.3.refs_5_
  12.3 0.0 collective-permute-done.4.refs_6_
  12.3 0.0 collective-permute-done.5.refs_7_
  12.4 2.8 %collective-permute-start.6 = (f32[6,8,4,128]{3,2,1,0:T(4,128)S(1)}, f32[6,8,4,128]{3,2,1,0:T(4,128)S(1)}, u32[]{:S(2)}, u32[]{:S(2)}) collective-permute-start(f32[6,8,4,128]{3,2,1,0:T(4,128)S(1)} %shard_map.66), channel_id=1, source_target_pairs={{0,16},{1,2},{2,1},{3,19},{4,20},{5,21},{6,22},{7,23},{8,24},{9,25... | collective-permute-start | bytes 294920 | tf_op jit(solution)/shard_map/ppermute | solution.py:623
  15.2 0.9 %collective-permute-done.6.refs_8_ = f32[6,8,4,128]{3,2,1,0:T(4,128)S(1)} collective-permute-done((f32[6,8,4,128]{3,2,1,0:T(4,128)S(1)}, f32[6,8,4,128]{3,2,1,0:T(4,128)S(1)}, u32[]{:S(2)}, u32[]{:S(2)}) %collective-permute-start.6) | collective-permute-done | bytes 98336 | tf_op jit(solution)/shard_map/ppermute | solution.py:623
  16.1 3.6 %shard_map.68 = (f32[5,8,40,128]{3,2,1,0:T(8,128)S(1)}, f32[8,40,128]{2,1,0:T(8,128)S(1)}, f32[4,8,32,128]{3,2,1,0:T(8,128)S(1)}, f32[8,40,128]{2,1,0:T(8,128)S(1)}, f32[8,40,128]{2,1,0:T(8,128)S(1)}) custom-call(f32[2,2,40,128]{3,2,1,0:T(8,128)S(1)} %get-tuple-element.32.refs_0_, f32[2,2,40,128]{3,2,1,0:T(8,128)S(1)} %collective-permute-done.refs_1_, ...), custom_call_target="tpu_custom_call" | custom-call | flops 400000000 | bytes 400000 | tf_op jit(solution)/shard_map/pallas_call | solution.py:587
  19.8 0.1 collective-permute-start.8
  19.9 0.5 %collective-permute-start.7 = (f32[8,40,128]{2,1,0:T(8,128)S(1)}, f32[8,40,128]{2,1,0:T(8,128)S(1)}, u32[]{:S(2)}, u32[]{:S(2)}) collective-permute-start(f32[8,40,128]{2,1,0:T(8,128)S(1)} %get-tuple-element.44), channel_id=1, source_target_pairs={{0,16},{16,0},{1,17},{17,1},{2,18},{18,2},{3,19},{19,3},{4,20},{20... | collective-permute-start | bytes 491528 | tf_op jit(solution)/shard_map/ppermute | solution.py:626
  20.3 1.6 %collective-permute-done.7.refs_0_.refs_1_ = f32[8,40,128]{2,1,0:T(8,128)S(1)} collective-permute-done((f32[8,40,128]{2,1,0:T(8,128)S(1)}, f32[8,40,128]{2,1,0:T(8,128)S(1)}, u32[]{:S(2)}, u32[]{:S(2)}) %collective-permute-start.7) | collective-permute-done | bytes 163872 | tf_op jit(solution)/shard_map/ppermute | solution.py:626
  22.0 3.4 %shard_map.69 = (f32[6,2,32,128]{3,2,1,0:T(8,128)S(1)}, f32[6,2,32,128]{3,2,1,0:T(8,128)S(1)}, f32[6,2,32,128]{3,2,1,0:T(8,128)S(1)}, f32[6,2,32,128]{3,2,1,0:T(8,128)S(1)}) custom-call(f32[8,40,128]{2,1,0:T(8,128)S(1)} %collective-permute-done.7.refs_0_.refs_1_, f32[5,8,40,128]{3,2,1,0:T(8,128)S(1)} %get-tuple-element.48.refs_1_, ...), custom_call_target="tpu_custom_call" | custom-call | flops 400000000 | bytes 400000 | tf_op jit(solution)/shard_map/pallas_call | solution.py:587
  25.4 0.0 collective-permute-done.8.refs_2_
  25.4 0.1 shard_map.70
  25.5 0.6 %collective-permute-start.9 = (f32[6,2,32,128]{3,2,1,0:T(8,128)S(1)}, f32[6,2,32,128]{3,2,1,0:T(8,128)S(1)}, u32[]{:S(2)}, u32[]{:S(2)}) collective-permute-start(f32[6,2,32,128]{3,2,1,0:T(8,128)S(1)} %get-tuple-element.56), channel_id=1, source_target_pairs={{0,4},{4,0},{8,12},{12,8},{1,5},{5,1},{9,13},{13,9},{2,6},{6,2},{1... | collective-permute-start | bytes 589832 | tf_op jit(solution)/shard_map/ppermute | solution.py:603
  26.1 1.8 %collective-permute-start.10 = (f32[6,2,32,128]{3,2,1,0:T(8,128)S(1)}, f32[6,2,32,128]{3,2,1,0:T(8,128)S(1)}, u32[]{:S(2)}, u32[]{:S(2)}) collective-permute-start(f32[6,2,32,128]{3,2,1,0:T(8,128)S(1)} %get-tuple-element.57), channel_id=1, source_target_pairs={{0,8},{4,12},{8,0},{12,4},{1,9},{5,13},{9,1},{13,5},{2,10},{6,14},... | collective-permute-start | bytes 589832 | tf_op jit(solution)/shard_map/ppermute | solution.py:603
  27.9 0.3 collective-permute-start.11
  28.2 4.0 %collective-permute-done.9.refs_1_ = f32[6,2,32,128]{3,2,1,0:T(8,128)S(1)} collective-permute-done((f32[6,2,32,128]{3,2,1,0:T(8,128)S(1)}, f32[6,2,32,128]{3,2,1,0:T(8,128)S(1)}, u32[]{:S(2)}, u32[]{:S(2)}) %collective-permute-start.9) | collective-permute-done | bytes 196640 | tf_op jit(solution)/shard_map/ppermute | solution.py:603
  32.2 3.0 %collective-permute-done.10.refs_2_ = f32[6,2,32,128]{3,2,1,0:T(8,128)S(1)} collective-permute-done((f32[6,2,32,128]{3,2,1,0:T(8,128)S(1)}, f32[6,2,32,128]{3,2,1,0:T(8,128)S(1)}, u32[]{:S(2)}, u32[]{:S(2)}) %collective-permute-start.10) | collective-permute-done | bytes 196640 | tf_op jit(solution)/shard_map/ppermute | solution.py:603
  35.2 0.0 collective-permute-done.11.refs_3_
  35.2 1.0 %shard_map.71 = f32[1472,128]{1,0:T(8,128)} custom-call(f32[6,2,32,128]{3,2,1,0:T(8,128)S(1)} %get-tuple-element.55.refs_0_, f32[6,2,32,128]{3,2,1,0:T(8,128)S(1)} %collective-permute-done.9.refs_1_, f32[6,2,32,128]{3,2,1,0:T(8,128)S(1)} %collective-permute-done.10.refs_2_, f32[6,2,32,128]{3,2,1,0:T(8,128)S(1)} %collective-permute-done.11.refs_3_), custom_call_target="tpu_custom_call" | custom-call | flops 100000000 | bytes 100000 | tf_op jit(solution)/shard_map/pallas_call | solution.py:587
  (2 shorter events, 0.0 us)
Async XLA Ops:
  1.5 6.0 %collective-permute-start = (f32[2,2,40,128]{3,2,1,0:T(8,128)S(1)}, f32[2,2,40,128]{3,2,1,0:T(8,128)S(1)}, u32[]{:S(2)}, u32[]{:S(2)}) collective-permute-start(f32[2,2,40,128]{3,2,1,0:T(8,128)S(1)} %get-tuple-element.33), channel_id=1, source_target_pairs={{0,4},{4,0},{8,12},{12,8},{1,5},{5,1},{9,13},{13,9},{2,6},{6,2},{1... | collective-permute-start | bytes 245768 | tf_op jit(solution)/shard_map/ppermute | solution.py:603
  3.6 8.7 %collective-permute-start.3 = (f32[4,2,40,128]{3,2,1,0:T(8,128)S(1)}, f32[4,2,40,128]{3,2,1,0:T(8,128)S(1)}, u32[]{:S(2)}, u32[]{:S(2)}) collective-permute-start(f32[4,2,40,128]{3,2,1,0:T(8,128)S(1)} %get-tuple-element.37), channel_id=1, source_target_pairs={{0,1},{1,0},{2,3},{3,2},{4,5},{5,4},{6,7},{7,6},{8,9},{9,8},{10,11... | collective-permute-start | bytes 491528 | tf_op jit(solution)/shard_map/ppermute | solution.py:614
  3.7 8.6 %collective-permute-start.4 = (f32[4,2,40,128]{3,2,1,0:T(8,128)S(1)}, f32[4,2,40,128]{3,2,1,0:T(8,128)S(1)}, u32[]{:S(2)}, u32[]{:S(2)}) collective-permute-start(f32[4,2,40,128]{3,2,1,0:T(8,128)S(1)} %get-tuple-element.38), channel_id=1, source_target_pairs={{0,1},{1,0},{2,3},{3,2},{4,5},{5,4},{6,7},{7,6},{8,9},{9,8},{10,11... | collective-permute-start | bytes 491528 | tf_op jit(solution)/shard_map/ppermute | solution.py:614
  5.1 7.2 %collective-permute-start.5 = (f32[4,2,40,128]{3,2,1,0:T(8,128)S(1)}, f32[4,2,40,128]{3,2,1,0:T(8,128)S(1)}, u32[]{:S(2)}, u32[]{:S(2)}) collective-permute-start(f32[4,2,40,128]{3,2,1,0:T(8,128)S(1)} %get-tuple-element.39), channel_id=1, source_target_pairs={{0,1},{1,0},{2,3},{3,2},{4,5},{5,4},{6,7},{7,6},{8,9},{9,8},{10,11... | collective-permute-start | bytes 491528 | tf_op jit(solution)/shard_map/ppermute | solution.py:614
  6.3 5.1 %collective-permute-start.1 = (f32[2,2,40,128]{3,2,1,0:T(8,128)S(1)}, f32[2,2,40,128]{3,2,1,0:T(8,128)S(1)}, u32[]{:S(2)}, u32[]{:S(2)}) collective-permute-start(f32[2,2,40,128]{3,2,1,0:T(8,128)S(1)} %get-tuple-element.34), channel_id=1, source_target_pairs={{0,8},{4,12},{8,0},{12,4},{1,9},{5,13},{9,1},{13,5},{2,10},{6,14},... | collective-permute-start | bytes 245768 | tf_op jit(solution)/shard_map/ppermute | solution.py:603
  7.5 4.8 %collective-permute-start.2 = (f32[2,2,40,128]{3,2,1,0:T(8,128)S(1)}, f32[2,2,40,128]{3,2,1,0:T(8,128)S(1)}, u32[]{:S(2)}, u32[]{:S(2)}) collective-permute-start(f32[2,2,40,128]{3,2,1,0:T(8,128)S(1)} %get-tuple-element.35), channel_id=1, source_target_pairs={{0,12},{4,8},{8,4},{12,0},{1,13},{5,9},{9,5},{13,1},{2,14},{6,10},... | collective-permute-start | bytes 245768 | tf_op jit(solution)/shard_map/ppermute | solution.py:603
  12.4 3.8 %collective-permute-start.6 = (f32[6,8,4,128]{3,2,1,0:T(4,128)S(1)}, f32[6,8,4,128]{3,2,1,0:T(4,128)S(1)}, u32[]{:S(2)}, u32[]{:S(2)}) collective-permute-start(f32[6,8,4,128]{3,2,1,0:T(4,128)S(1)} %shard_map.66), channel_id=1, source_target_pairs={{0,16},{1,2},{2,1},{3,19},{4,20},{5,21},{6,22},{7,23},{8,24},{9,25... | collective-permute-start | bytes 294920 | tf_op jit(solution)/shard_map/ppermute | solution.py:623
  19.8 5.6 %collective-permute-start.8 = (f32[4,8,32,128]{3,2,1,0:T(8,128)S(1)}, f32[4,8,32,128]{3,2,1,0:T(8,128)S(1)}, u32[]{:S(2)}, u32[]{:S(2)}) collective-permute-start(f32[4,8,32,128]{3,2,1,0:T(8,128)S(1)} %get-tuple-element.45), channel_id=1, source_target_pairs={{0,16},{16,0},{1,17},{17,1},{2,18},{18,2},{3,19},{19,3},{4,20},{20... | collective-permute-start | bytes 1572872 | tf_op jit(solution)/shard_map/ppermute | solution.py:626
  19.9 2.1 %collective-permute-start.7 = (f32[8,40,128]{2,1,0:T(8,128)S(1)}, f32[8,40,128]{2,1,0:T(8,128)S(1)}, u32[]{:S(2)}, u32[]{:S(2)}) collective-permute-start(f32[8,40,128]{2,1,0:T(8,128)S(1)} %get-tuple-element.44), channel_id=1, source_target_pairs={{0,16},{16,0},{1,17},{17,1},{2,18},{18,2},{3,19},{19,3},{4,20},{20... | collective-permute-start | bytes 491528 | tf_op jit(solution)/shard_map/ppermute | solution.py:626
  25.5 6.7 %collective-permute-start.9 = (f32[6,2,32,128]{3,2,1,0:T(8,128)S(1)}, f32[6,2,32,128]{3,2,1,0:T(8,128)S(1)}, u32[]{:S(2)}, u32[]{:S(2)}) collective-permute-start(f32[6,2,32,128]{3,2,1,0:T(8,128)S(1)} %get-tuple-element.56), channel_id=1, source_target_pairs={{0,4},{4,0},{8,12},{12,8},{1,5},{5,1},{9,13},{13,9},{2,6},{6,2},{1... | collective-permute-start | bytes 589832 | tf_op jit(solution)/shard_map/ppermute | solution.py:603
  26.1 9.1 %collective-permute-start.10 = (f32[6,2,32,128]{3,2,1,0:T(8,128)S(1)}, f32[6,2,32,128]{3,2,1,0:T(8,128)S(1)}, u32[]{:S(2)}, u32[]{:S(2)}) collective-permute-start(f32[6,2,32,128]{3,2,1,0:T(8,128)S(1)} %get-tuple-element.57), channel_id=1, source_target_pairs={{0,8},{4,12},{8,0},{12,4},{1,9},{5,13},{9,1},{13,5},{2,10},{6,14},... | collective-permute-start | bytes 589832 | tf_op jit(solution)/shard_map/ppermute | solution.py:603
  27.9 7.3 %collective-permute-start.11 = (f32[6,2,32,128]{3,2,1,0:T(8,128)S(1)}, f32[6,2,32,128]{3,2,1,0:T(8,128)S(1)}, u32[]{:S(2)}, u32[]{:S(2)}) collective-permute-start(f32[6,2,32,128]{3,2,1,0:T(8,128)S(1)} %get-tuple-element.58), channel_id=1, source_target_pairs={{0,12},{4,8},{8,4},{12,0},{1,13},{5,9},{9,5},{13,1},{2,14},{6,10},... | collective-permute-start | bytes 589832 | tf_op jit(solution)/shard_map/ppermute | solution.py:603
